TPU v7x, 512 devices: a whole 4x4x16 slice. The times are simulated.
512 devices in a mesh: section: 32 (over z, core), tensor: 16 (over x, y).
Axes of the slice: x: 4, y: 4, z: 16, core: 2. Of those that a mesh axis runs over, the one named last changes fastest.
Arguments:
- activations: bfloat16 [32, 512, 4096], P('section', None, 'tensor'), may hold values from -48 to 48
- gain: bfloat16 [32, 4096], P('section', 'tensor'), may hold values from 0.5 to 1.5
- w_query: bfloat16 [32, 4096, 4096], P('section', None, 'tensor'), may hold values from -0.0625 to 0.0625
- w_kv: bfloat16 [32, 1024, 4096], P('section', 'tensor'), may hold values from -1.8782524 to 1.8782524
- segments: int32 [32, 512], replicated, may hold values from 0 to 31, never falling along the last dimension, each value on 1 to 128 neighbouring positions
- pool: bfloat16 [64, 128, 4096], P('section', None, 'tensor'), may hold values from -48 to 48
- row_ids: int32 [32], replicated, may hold values from 0 to 63, as said below
- row_lengths: int32 [32], replicated, may hold values from 1 to 128, 512 in all
Outputs:
- after_first: bfloat16 [32, 512, 4096], P('section', None, 'tensor')
- after_second: bfloat16 [32, 512, 4096], P('section', None, 'tensor')
Inputs may be any that keep to these rules, and one draw needn't show every extreme that they name: `row_ids`: every block of 2 consecutive ids, the rows of one buffer host, is named at least once; ids may repeat.
All inputs are finite; a program needn't handle non-finite values.
Results may differ from a plain program's by a relative error of at most 0.01.
Values may be sent and summed in bfloat16 or wider, within the bound.
No kernel may reach another device: no remote copies, remote signals or barrier semaphores. Data moves between devices by JAX's collectives and lax.ppermute only.
A program may use at most 64 MiB of HBM per device.

v0:
```python
import jax
import jax.numpy as jnp
from jax import lax
from jax.sharding import PartitionSpec as P

D = 4096
HEADS = 32
KV_HEADS = 4
HEAD_DIM = 128


norm_eps = 1e-05
masked_score = -1e30


def partner_2(block, axis, distance):
    count = lax.axis_size(axis)
    route = []
    for low in range(count):
        high = low | 1 << distance
        if high != low and high < count:
            route += [(low, high), (high, low)]
    return lax.ppermute(block, axis, route)


def from_behind(block, axis, distance):
    devices = range(lax.axis_size(axis))
    route = [(i - distance, i) for i in devices if i - distance in devices]
    return lax.ppermute(block, axis, route)


def attend(inputs, gain_cols, query_weight, keyval_weight, seg_ids, tensor_index):
    row_count, col_count = inputs.shape
    wide_inputs = inputs.astype(jnp.float32)
    square_total = lax.psum(jnp.sum(wide_inputs * wide_inputs, axis=1), "tensor")
    row_scale = lax.rsqrt(square_total / D + norm_eps)
    normed = (wide_inputs * row_scale[:, None] * gain_cols.astype(jnp.float32)[None, :]).astype(
        jnp.bfloat16
    )
    part_cols = lax.all_gather(normed, "tensor", axis=1, tiled=True)
    query_part = jnp.dot(part_cols, query_weight, preferred_element_type=jnp.float32)
    keyval_part = lax.dot_general(
        keyval_weight, part_cols, (((1,), (1,)), ((), ())), preferred_element_type=jnp.float32
    )
    query = query_part.astype(jnp.bfloat16)
    keyval = keyval_part.astype(jnp.bfloat16)
    heads_here = query_weight.shape[1] // HEAD_DIM
    group_size = HEADS // KV_HEADS
    group_devices = group_size // heads_here
    head_block = keyval
    for bit_number in range(group_devices.bit_length() - 1):
        partner = partner_2(head_block, "tensor", bit_number)
        is_lower = tensor_index // (1 << bit_number) % 2 == 0
        head_block = jnp.where(
            is_lower,
            jnp.concatenate([head_block, partner], axis=0),
            jnp.concatenate([partner, head_block], axis=0),
        )
    keys_cols = head_block[:HEAD_DIM]
    values_cols = head_block[HEAD_DIM:]
    query_heads = query.reshape(row_count, heads_here, HEAD_DIM)
    scores = jnp.einsum(
        "rhd,ds->hrs", query_heads, keys_cols, preferred_element_type=jnp.float32
    ) * HEAD_DIM ** (-0.5)
    positions = jnp.arange(row_count, dtype=jnp.int32)
    allowed = (seg_ids[:, None] == seg_ids[None, :]) & (positions[None, :] <= positions[:, None])
    scores = jnp.where(allowed[None, :, :], scores, masked_score)
    weights = jax.nn.softmax(scores, axis=-1).astype(jnp.bfloat16)
    context = jnp.einsum("hrs,ds->rhd", weights, values_cols, preferred_element_type=jnp.float32)
    context = context.astype(jnp.bfloat16).reshape(row_count, col_count)
    return (wide_inputs + context.astype(jnp.float32)).astype(jnp.bfloat16)


def pick_rows(running, host_rows, source):
    flat_rows = host_rows.reshape(-1, host_rows.shape[2])
    inside = (source >= 0) & (source < flat_rows.shape[0])
    taken = jnp.take(flat_rows, jnp.clip(source, 0, flat_rows.shape[0] - 1), axis=0)
    return jnp.where(inside[:, None], taken, running)


def per_device(activations, gain, w_query, w_kv, segments, pool, row_ids, row_lengths):
    section_index = lax.axis_index("section")
    tensor_index = lax.axis_index("tensor")
    token_count = activations.shape[1]
    col_count = activations.shape[2]
    own_segments = lax.dynamic_index_in_dim(segments, section_index, 0, keepdims=False)
    after_first = attend(activations[0], gain[0], w_query[0], w_kv[0], own_segments, tensor_index)[
        None
    ]
    ends = jnp.cumsum(row_lengths)
    positions = jnp.arange(token_count, dtype=jnp.int32)
    slot = jnp.sum((positions[:, None] >= ends[None, :]).astype(jnp.int32), axis=1)
    slot_match = slot[:, None] == jnp.arange(row_ids.shape[0], dtype=jnp.int32)[None, :]
    slot_start = jnp.sum(jnp.where(slot_match, (ends - row_lengths)[None, :], 0), axis=1)
    slot_row = jnp.sum(jnp.where(slot_match, row_ids[None, :], 0), axis=1)
    source = slot_row * pool.shape[1] + positions - slot_start
    empty_rows = jnp.zeros((token_count, col_count), jnp.bfloat16)
    fresh = pick_rows(empty_rows, lax.all_gather(pool, "section", axis=0, tiled=True), source)
    handed = from_behind(after_first, "section", 1)
    second_inputs = jnp.where(section_index == 0, fresh[None], handed)
    prior_segments = lax.dynamic_index_in_dim(
        segments, jnp.maximum(section_index - 1, 0), 0, keepdims=False
    )
    second_segments = jnp.where(section_index == 0, slot, prior_segments)
    after_second = attend(
        second_inputs[0], gain[0], w_query[0], w_kv[0], second_segments, tensor_index
    )[None]
    return (after_first, after_second)


def solution(mesh):
    return jax.shard_map(
        per_device,
        mesh=mesh,
        in_specs=(
            P("section", None, "tensor"),
            P("section", "tensor"),
            P("section", None, "tensor"),
            P("section", "tensor", None),
            P(),
            P("section", None, "tensor"),
            P(),
            P(),
        ),
        out_specs=(P("section", None, "tensor"), P("section", None, "tensor")),
        check_vma=False,
    )
```

profile of v0, /device:TPU:6, one launch (start us, length us, event | category | flops | bytes accessed | tf_op | source)
XLA Modules:
  0.0 339.0 jit_solution(10043609363938623515)
XLA Ops:
  8.0 1.1 fusion.30
  9.1 34.5 %psum.14 = f32[512]{0:T(512)S(1)} all-reduce(f32[512]{0:T(512)S(1)} %fusion.30), channel_id=1, replica_groups=mesh['section'=32,'tensor'=16] {'tensor'}, use_global_device_ids=true, to_apply=%region_1.2 | all-reduce | flops 512 | bytes 4096 | tf_op jit(solution)/shard_map/psum | solution.py:35
  43.6 1.8 fusion.32
  49.7 74.0 %all-gather.4.cloned.1.call-done = bf16[512,4096]{1,0:T(8,128)(2,1)} async-done(((bf16[512,256]{1,0:T(8,128)(2,1)}), bf16[512,4096]{1,0:T(8,128)(2,1)}) %all-gather.4.cloned.1.call-update) | async-done | bytes 4194320 | tf_op jit(solution)/shard_map/all_gather | solution.py:40
  123.7 3.7 %fusion.16 = bf16[64,512]{1,0:T(8,128)(2,1)S(1)} fusion(bf16[512,4096]{1,0:T(8,128)(2,1)} %all-gather.4.cloned.1.call-done, bf16[1,64,4096]{2,1,0:T(8,128)(2,1)} %param.11), kind=kOutput, calls=%fused_computation.23 | convolution fusion | flops 268468224 | bytes 4784128 | tf_op jit(solution)/shard_map/dot_general | solution.py:42
  127.4 2.2 collective-permute-start
  129.6 3.9 %collective-permute-done = bf16[64,512]{1,0:T(8,128)(2,1)S(1)} collective-permute-done((bf16[64,512]{1,0:T(8,128)(2,1)S(1)}, bf16[64,512]{1,0:T(8,128)(2,1)S(1)}, u32[]{:S(2)}, u32[]{:S(2)}) %collective-permute-start) | collective-permute-done | bytes 65568 | tf_op jit(solution)/shard_map/ppermute | solution.py:23
  133.5 3.4 %collective-permute-start.1 = (bf16[128,512]{1,0:T(8,128)(2,1)S(1)}, bf16[128,512]{1,0:T(8,128)(2,1)S(1)}, u32[]{:S(2)}, u32[]{:S(2)}) collective-permute-start(bf16[128,512]{1,0:T(8,128)(2,1)S(1)} %maximum_select_fusion.2), channel_id=1, source_target_pairs={{0,2},{2,0},{1,3},{3,1},{4,6},{6,4},{5,7},{7,5},{8,10},{10,8},{9,1... | collective-permute-start | bytes 393224 | tf_op jit(solution)/shard_map/ppermute | solution.py:23
  137.0 3.5 %fusion.8 = bf16[512,256]{0,1:T(8,128)(2,1)S(1)} fusion(bf16[512,4096]{1,0:T(8,128)(2,1)} %all-gather.4.cloned.1.call-done, bf16[1,4096,256]{2,1,0:T(8,128)(2,1)S(1)} %copy-done), kind=kOutput, calls=%fused_computation.15 | convolution fusion | flops 1073872896 | bytes 6553600 | tf_op jit(solution)/shard_map/dot_general | solution.py:41
  140.5 1.4 collective-permute-done.1
  142.0 0.9 fusion.63
  142.9 2.2 fusion.14
  146.1 1.4 collective-permute-start.2
  147.6 52.2 %all-gather.6.cloned.1.call-done = bf16[64,128,256]{2,1,0:T(8,128)(2,1)} async-done(((bf16[2,128,256]{2,1,0:T(8,128)(2,1)}), bf16[64,128,256]{2,1,0:T(8,128)(2,1)}) %all-gather.6.cloned.1.call-update) | async-done | bytes 4194320 | tf_op jit(solution)/shard_map/all_gather | solution.py:98
  199.8 4.3 %gather_fusion = bf16[512,256]{1,0:T(8,128)(2,1)S(1)} fusion(bf16[8192,256]{1,0:T(8,128)(2,1)} %bitcast.129, s32[1024]{0:T(1024)S(1)} %pad_clamp_fusion), kind=kCustom, calls=%fused_computation | custom fusion | bytes 526336 | tf_op jit(solution)/shard_map/jit(_take)/gather | solution.py:77
  204.4 33.5 %psum.15 = f32[512]{0:T(512)S(1)} all-reduce(f32[512]{0:T(512)S(1)} %get-tuple-element.4), channel_id=1, replica_groups=mesh['section'=32,'tensor'=16] {'tensor'}, use_global_device_ids=true, to_apply=%region_9.10 | all-reduce | flops 512 | bytes 4096 | tf_op jit(solution)/shard_map/psum | solution.py:35
  238.8 71.3 %all-gather.8.cloned.1.call-done = bf16[512,4096]{1,0:T(8,128)(2,1)} async-done(((bf16[512,256]{1,0:T(8,128)(2,1)}), bf16[512,4096]{1,0:T(8,128)(2,1)}) %all-gather.8.cloned.1.call-update) | async-done | bytes 4194320 | tf_op jit(solution)/shard_map/all_gather | solution.py:40
  310.1 3.7 %fusion.17 = bf16[64,512]{1,0:T(8,128)(2,1)S(1)} fusion(bf16[512,4096]{1,0:T(8,128)(2,1)} %all-gather.8.cloned.1.call-done, bf16[1,64,4096]{2,1,0:T(8,128)(2,1)S(1)} %copy-done.3), kind=kOutput, calls=%fused_computation.24 | convolution fusion | flops 268468224 | bytes 4784128 | tf_op jit(solution)/shard_map/dot_general | solution.py:42
  313.8 2.2 collective-permute-start.3
  316.2 3.8 %collective-permute-done.3 = bf16[64,512]{1,0:T(8,128)(2,1)S(1)} collective-permute-done((bf16[64,512]{1,0:T(8,128)(2,1)S(1)}, bf16[64,512]{1,0:T(8,128)(2,1)S(1)}, u32[]{:S(2)}, u32[]{:S(2)}) %collective-permute-start.3) | collective-permute-done | bytes 65568 | tf_op jit(solution)/shard_map/ppermute | solution.py:23
  320.0 3.6 %collective-permute-start.4 = (bf16[128,512]{1,0:T(8,128)(2,1)S(1)}, bf16[128,512]{1,0:T(8,128)(2,1)S(1)}, u32[]{:S(2)}, u32[]{:S(2)}) collective-permute-start(bf16[128,512]{1,0:T(8,128)(2,1)S(1)} %maximum_select_fusion.3), channel_id=1, source_target_pairs={{0,2},{2,0},{1,3},{3,1},{4,6},{6,4},{5,7},{7,5},{8,10},{10,8},{9,1... | collective-permute-start | bytes 393224 | tf_op jit(solution)/shard_map/ppermute | solution.py:23
  323.6 1.3 fusion.11
  324.9 3.4 %collective-permute-done.4 = bf16[128,512]{1,0:T(8,128)(2,1)S(1)} collective-permute-done((bf16[128,512]{1,0:T(8,128)(2,1)S(1)}, bf16[128,512]{1,0:T(8,128)(2,1)S(1)}, u32[]{:S(2)}, u32[]{:S(2)}) %collective-permute-start.4) | collective-permute-done | bytes 131104 | tf_op jit(solution)/shard_map/ppermute | solution.py:23
  329.3 2.1 fusion.15
  (47 shorter events, 9.5 us)
Async XLA Ops:
  7.2 129.8 %copy-start = (bf16[1,4096,256]{2,1,0:T(8,128)(2,1)S(1)}, bf16[1,4096,256]{2,1,0:T(8,128)(2,1)}, u32[]{:S(2)}) copy-start(bf16[1,4096,256]{2,1,0:T(8,128)(2,1)} %param.10) | copy-start | bytes 6291460
  7.2 116.5 %all-gather.4.cloned.1.call-start = ((), (), s32[]{:S(2)}) async-start(), calls=%async_computation | async-start | bytes 4456448 | tf_op jit(solution)/shard_map/all_gather | solution.py:40
  45.4 154.4 %all-gather.6.cloned.1.call-start = ((), (), s32[]{:S(2)}) async-start(), calls=%async_computation.1 | async-start | bytes 4325376 | tf_op jit(solution)/shard_map/all_gather | solution.py:98
  46.2 263.9 %all-gather.8.cloned.1.call-start = ((), (), s32[]{:S(2)}) async-start(), calls=%async_computation.2 | async-start | bytes 4456448 | tf_op jit(solution)/shard_map/all_gather | solution.py:40
  127.4 6.2 %collective-permute-start = (bf16[64,512]{1,0:T(8,128)(2,1)S(1)}, bf16[64,512]{1,0:T(8,128)(2,1)S(1)}, u32[]{:S(2)}, u32[]{:S(2)}) collective-permute-start(bf16[64,512]{1,0:T(8,128)(2,1)S(1)} %fusion.16), channel_id=1, source_target_pairs={{0,1},{1,0},{2,3},{3,2},{4,5},{5,4},{6,7},{7,6},{8,9},{9,8},{10,11... | collective-permute-start | bytes 196616 | tf_op jit(solution)/shard_map/ppermute | solution.py:23
  133.5 8.4 %collective-permute-start.1 = (bf16[128,512]{1,0:T(8,128)(2,1)S(1)}, bf16[128,512]{1,0:T(8,128)(2,1)S(1)}, u32[]{:S(2)}, u32[]{:S(2)}) collective-permute-start(bf16[128,512]{1,0:T(8,128)(2,1)S(1)} %maximum_select_fusion.2), channel_id=1, source_target_pairs={{0,2},{2,0},{1,3},{3,1},{4,6},{6,4},{5,7},{7,5},{8,10},{10,8},{9,1... | collective-permute-start | bytes 393224 | tf_op jit(solution)/shard_map/ppermute | solution.py:23
  140.5 1.5 copy-start.5
  142.9 2.4 copy-start.2
  146.1 163.9 %copy-start.3 = (bf16[1,64,4096]{2,1,0:T(8,128)(2,1)S(1)}, bf16[1,64,4096]{2,1,0:T(8,128)(2,1)}, u32[]{:S(2)}) copy-start(bf16[1,64,4096]{2,1,0:T(8,128)(2,1)} %param.11) | copy-start | bytes 1572868
  146.1 58.0 %collective-permute-start.2 = (bf16[1,512,256]{2,1,0:T(8,128)(2,1)}, bf16[1,512,256]{2,1,0:T(8,128)(2,1)S(1)}, u32[]{:S(2)}, u32[]{:S(2)}) collective-permute-start(bf16[1,512,256]{2,1,0:T(8,128)(2,1)} %fusion.33), channel_id=1, source_target_pairs={{0,16},{16,32},{32,48},{48,64},{64,80},{80,96},{96,112},{112,128},... | collective-permute-start | bytes 786440 | tf_op jit(solution)/shard_map/ppermute | solution.py:29
  310.0 13.5 %copy-start.1 = (bf16[512,4096]{1,0:T(8,128)(2,1)S(1)}, bf16[512,4096]{1,0:T(8,128)(2,1)}, u32[]{:S(2)}) copy-start(bf16[512,4096]{1,0:T(8,128)(2,1)} %all-gather.8.cloned.1.call-done) | copy-start | bytes 12582916
  313.8 6.2 %collective-permute-start.3 = (bf16[64,512]{1,0:T(8,128)(2,1)S(1)}, bf16[64,512]{1,0:T(8,128)(2,1)S(1)}, u32[]{:S(2)}, u32[]{:S(2)}) collective-permute-start(bf16[64,512]{1,0:T(8,128)(2,1)S(1)} %fusion.17), channel_id=1, source_target_pairs={{0,1},{1,0},{2,3},{3,2},{4,5},{5,4},{6,7},{7,6},{8,9},{9,8},{10,11... | collective-permute-start | bytes 196616 | tf_op jit(solution)/shard_map/ppermute | solution.py:23
  320.0 8.4 %collective-permute-start.4 = (bf16[128,512]{1,0:T(8,128)(2,1)S(1)}, bf16[128,512]{1,0:T(8,128)(2,1)S(1)}, u32[]{:S(2)}, u32[]{:S(2)}) collective-permute-start(bf16[128,512]{1,0:T(8,128)(2,1)S(1)} %maximum_select_fusion.3), channel_id=1, source_target_pairs={{0,2},{2,0},{1,3},{3,1},{4,6},{6,4},{5,7},{7,5},{8,10},{10,8},{9,1... | collective-permute-start | bytes 393224 | tf_op jit(solution)/shard_map/ppermute | solution.py:23
  324.9 3.5 %copy-start.4 = (bf16[512,256]{0,1:T(8,128)(2,1)}, bf16[512,256]{0,1:T(8,128)(2,1)S(1)}, u32[]{:S(2)}) copy-start(bf16[512,256]{0,1:T(8,128)(2,1)S(1)} %fusion.11) | copy-start | bytes 786436
Sparse Core Ops, SparseCore 0:
  45.5 78.0 all-gather.3
  125.8 73.9 all-gather.5
  238.9 71.0 all-gather.7
where the time goes:
time: 340 us; the launch traced here: 339 us
  waiting for transfers between devices  211 us (62%)
  blocking collectives  67.9 us (20%)
  matrix products  18.4 us (5%)
  between operations  14 us (4%)
  starting transfers between devices  12.9 us (4%)
  other arithmetic  9.48 us (3%)
  local copies, waits for them, and re-layouts  5.46 us (2%)
    all_gather x2, waiting for transfers between devices, attend(): part_cols = lax.all_gather(normed, 'tensor', axis=1, tiled=True)  145 us
    psum x2, blocking collectives, attend(): lax.psum(jnp.sum(wide_inputs * wide_inputs, axis=1), 'tensor')  67.9 us
    all_gather x1, waiting for transfers between devices, per_device(): lax.all_gather(pool, 'section', axis=0, tiled=True)  52.2 us
    ppermute x4, waiting for transfers between devices, partner_2(): return lax.ppermute(block, axis, route)  12.6 us
    ppermute x4, starting transfers between devices, partner_2(): return lax.ppermute(block, axis, route)  11.3 us
    dot_general x2, matrix products, attend(): lax.dot_general(keyval_weight, part_cols, (((1,), (1,)), ((), ())), prefe...  7.42 us
  transfers between devices with their start and end apart: 8, of which 7 were waited for; matrix products, arithmetic and copies ran while one was open for 6% of the time, Pallas kernels for 0%

commit v1 on v0

v1 whole, which is shorter than its diff:
```python
import functools

import jax
import jax.numpy as jnp
from jax import lax
from jax.experimental import pallas as pl
from jax.experimental.pallas import tpu as pltpu
from jax.sharding import PartitionSpec as P

D = 4096
HEAD_DIM = 128
SIDE = 4
BLOCK = 256
KV_ROWS = 64
TOKENS = 512
HALF = 256
ROW_MAX = 128
HOST_ROWS = 2
SLOTS = 32
SENT_ROWS = TOKENS + 2 * KV_ROWS + 16
AXES = ("section", "tensor")
norm_eps = 1e-05
masked_score = -1e30
f32, bf16 = jnp.float32, jnp.bfloat16
VMEM = pl.BlockSpec(memory_space=pltpu.VMEM)
SMEM = pl.BlockSpec(memory_space=pltpu.SMEM)
NT = (((1,), (1,)), ((), ()))


def place(section, first, second):
    return SIDE * first + second if section % 2 == 0 else SIDE * second + first


def rings(sections, along_a):
    groups = []
    for s in range(sections):
        for i in range(SIDE):
            ring = [(place(s, j, i) if along_a else place(s, i, j)) for j in range(SIDE)]
            groups.append([s * SIDE * SIDE + t for t in ring])
    return groups


def head_rings(sections):
    return [[(s * SIDE + g) * SIDE + i for i in range(SIDE)] for s in range(sections) for g in range(SIDE)]


def call(body, out_shape, operands, specs, flops, moved, **more):
    return pl.pallas_call(
        body,
        out_shape=out_shape,
        in_specs=specs,
        out_specs=jax.tree.map(lambda _: VMEM, out_shape),
        compiler_params=pltpu.CompilerParams(vmem_limit_bytes=48 << 20),
        cost_estimate=pl.CostEstimate(flops=flops, bytes_accessed=moved, transcendentals=0),
        **more,
    )(*operands)


def pack_body(odd_ref, query_ref, keyval_ref, out_ref):
    out_ref[0, 0, :BLOCK] = query_ref[...]
    out_ref[0, 0, BLOCK:] = keyval_ref[...]


def pack_weights(odd, w_query, w_kv):
    def source(i, j, odd_ref):
        return jnp.where(odd_ref[0] == 1, SIDE * i + j, SIDE * j + i)

    return pl.pallas_call(
        pack_body,
        out_shape=jax.ShapeDtypeStruct((SIDE, SIDE, BLOCK + KV_ROWS, BLOCK), bf16),
        grid_spec=pltpu.PrefetchScalarGridSpec(
            num_scalar_prefetch=1,
            grid=(SIDE, SIDE),
            in_specs=[
                pl.BlockSpec((BLOCK, BLOCK), lambda i, j, o: (source(i, j, o), 0)),
                pl.BlockSpec((KV_ROWS, BLOCK), lambda i, j, o: (0, source(i, j, o))),
            ],
            out_specs=pl.BlockSpec((1, 1, BLOCK + KV_ROWS, BLOCK), lambda i, j, o: (i, j, 0, 0)),
        ),
        cost_estimate=pl.CostEstimate(flops=0, bytes_accessed=5 << 20, transcendentals=0),
    )(odd, w_query, w_kv)


def project_body(x_ref, gain_ref, w_ref, out_ref, wide_ref, kv_ref):
    ones = jnp.ones((8, BLOCK), bf16)
    squares = jnp.zeros((8, TOKENS), f32)
    for a in range(SIDE):
        part = x_ref[a, :TOKENS].astype(f32)
        gain = gain_ref[a, TOKENS : TOKENS + 1].astype(f32)
        wide_ref[:, a * BLOCK : (a + 1) * BLOCK] = (part * gain).astype(bf16)
        square = part * part
        upper = square.astype(bf16)
        lower = (square - upper.astype(f32)).astype(bf16)
        squares += lax.dot_general(ones, upper, NT, preferred_element_type=f32)
        squares += lax.dot_general(ones, lower, NT, preferred_element_type=f32)
        for b in range(SIDE):
            kv_ref[b * KV_ROWS : (b + 1) * KV_ROWS, a * BLOCK : (a + 1) * BLOCK] = w_ref[b, a, BLOCK:]
    keyval = lax.dot_general(kv_ref[...], wide_ref[...], NT, preferred_element_type=f32).astype(bf16)
    first = squares.astype(bf16)
    second = (squares - first.astype(f32)).astype(bf16)
    stats = [first[:1, :HALF], first[:1, HALF:], second[:1, :HALF], second[:1, HALF:]]
    stats = jnp.concatenate([s.astype(f32) for s in stats] + [jnp.zeros((12, HALF), f32)], axis=0).astype(bf16)
    for b in range(SIDE):
        total = jnp.zeros((TOKENS, BLOCK), f32)
        for a in range(SIDE):
            total += jnp.dot(
                wide_ref[:, a * BLOCK : (a + 1) * BLOCK], w_ref[b, a, :BLOCK], preferred_element_type=f32
            )
        out_ref[b, :TOKENS] = total.astype(bf16)
        rows = slice(b * KV_ROWS, (b + 1) * KV_ROWS)
        out_ref[b, TOKENS : TOKENS + KV_ROWS] = keyval[rows, :HALF]
        out_ref[b, TOKENS + KV_ROWS : TOKENS + 2 * KV_ROWS] = keyval[rows, HALF:]
        out_ref[b, TOKENS + 2 * KV_ROWS :] = stats


def project(x, gain_rows, weights):
    return call(
        project_body,
        jax.ShapeDtypeStruct((SIDE, SENT_ROWS, BLOCK), bf16),
        (x, gain_rows, weights),
        [VMEM] * 3,
        2 * TOKENS * 1024 * 1280,
        6 << 20,
        scratch_shapes=[pltpu.VMEM((TOKENS, SIDE * BLOCK), bf16), pltpu.VMEM((SIDE * KV_ROWS, SIDE * BLOCK), bf16)],
    )


def down(row):
    return jnp.transpose(jnp.broadcast_to(row, (HEAD_DIM, HEAD_DIM)))


def combine_body(parts_ref, query_ref, keyval_ref):
    tail = parts_ref[0, TOKENS:].astype(f32)
    for b in range(1, SIDE):
        tail += parts_ref[b, TOKENS:].astype(f32)
    stats = tail[2 * KV_ROWS :]
    for h in range(2):
        mean = (stats[h : h + 1] + stats[2 + h : 3 + h]) / D
        scale = lax.rsqrt(mean + norm_eps)
        keyval_ref[:, h * HALF : (h + 1) * HALF] = (tail[h * KV_ROWS : (h + 1) * KV_ROWS] * scale).astype(bf16)
        for q in range(2):
            start = h * HALF + q * HEAD_DIM
            rows = slice(start, start + HEAD_DIM)
            total = parts_ref[0, rows].astype(f32)
            for b in range(1, SIDE):
                total += parts_ref[b, rows].astype(f32)
            factor = down(scale[:, q * HEAD_DIM : (q + 1) * HEAD_DIM])
            query_ref[rows] = (total * jnp.concatenate([factor, factor], axis=1)).astype(bf16)


def combine(parts):
    return call(
        combine_body,
        (jax.ShapeDtypeStruct((TOKENS, BLOCK), bf16), jax.ShapeDtypeStruct((KV_ROWS, TOKENS), bf16)),
        (parts,),
        [VMEM],
        TOKENS * BLOCK * 8,
        2 << 20,
    )


def attend_body(is_second, number_ref, lengths_ref, x_ref, query_ref, keyval_ref, segments_ref, out_ref):
    section = number_ref[0]
    if is_second:
        ids = segments_ref[pl.ds(jnp.maximum(section - 1, 0), 1), :]
        spot = lax.broadcasted_iota(jnp.int32, (1, TOKENS), 1)

        def count(k, carried):
            end, slot = carried
            end = end + lengths_ref[k]
            return end, slot + (spot >= end).astype(jnp.int32)

        _, slot = lax.fori_loop(0, SLOTS, count, (jnp.int32(0), jnp.zeros((1, TOKENS), jnp.int32)))
        ids = jnp.where(section == 0, slot, ids)
    else:
        ids = segments_ref[pl.ds(section, 1), :]
    ids = ids.astype(f32)
    for i in range(TOKENS // HEAD_DIM):
        rows = slice(i * HEAD_DIM, (i + 1) * HEAD_DIM)
        low = max(i - 1, 0) * HEAD_DIM
        width = (i + 1) * HEAD_DIM - low
        cols = slice(low, low + width)
        own = down(ids[:, rows])
        if width > HEAD_DIM:
            own = jnp.concatenate([own, own], axis=1)
        place_r = lax.broadcasted_iota(jnp.int32, (HEAD_DIM, width), 0) + i * HEAD_DIM
        place_c = lax.broadcasted_iota(jnp.int32, (HEAD_DIM, width), 1) + low
        allowed = (own == ids[:, cols]) & (place_c <= place_r)
        keys = keyval_ref[:HEAD_DIM, cols]
        values = keyval_ref[HEAD_DIM:, cols]
        for h in range(2):
            lanes = slice(h * HEAD_DIM, (h + 1) * HEAD_DIM)
            scores = jnp.dot(query_ref[rows, lanes], keys, preferred_element_type=f32) * HEAD_DIM ** (-0.5)
            scores = jnp.where(allowed, scores, masked_score)
            grown = jnp.exp(scores - jnp.max(scores, axis=1, keepdims=True))
            weights = (grown / jnp.sum(grown, axis=1, keepdims=True)).astype(bf16)
            context = lax.dot_general(weights, values, NT, preferred_element_type=f32).astype(bf16)
            out_ref[rows, lanes] = (x_ref[rows, lanes].astype(f32) + context.astype(f32)).astype(bf16)


def attend(is_second, number, lengths, x, query, keyval, segments):
    return call(
        functools.partial(attend_body, is_second),
        jax.ShapeDtypeStruct((TOKENS, BLOCK), bf16),
        (number, lengths, x, query, keyval, segments),
        [SMEM, SMEM] + [VMEM] * 4,
        2 * TOKENS * 256 * 128 * 4,
        1 << 20,
    )


def frame_body(number_ref, ids_ref, lengths_ref, pool_ref, out_ref, total_ref):
    total_ref[...] = jnp.zeros_like(total_ref)
    section = number_ref[0]
    row = lax.broadcasted_iota(jnp.int32, (TOKENS, ROW_MAX), 0)
    col = lax.broadcasted_iota(jnp.int32, (TOKENS, ROW_MAX), 1)

    def take(k, start):
        length = lengths_ref[k]
        which = ids_ref[k] - HOST_ROWS * section

        @pl.when((which >= 0) & (which < HOST_ROWS))
        def _():
            hit = ((row - start == col) & (col < length)).astype(f32).astype(bf16)
            total_ref[...] += jnp.dot(hit, pool_ref[which], preferred_element_type=f32)

        return start + length

    lax.fori_loop(0, SLOTS, take, jnp.int32(0))
    out_ref[...] = total_ref[...].astype(bf16)


def make_frame(number, row_ids, row_lengths, pool):
    return call(
        frame_body,
        jax.ShapeDtypeStruct((TOKENS, BLOCK), bf16),
        (number, row_ids, row_lengths, pool),
        [SMEM, SMEM, SMEM, VMEM],
        2 * TOKENS * 128 * 256,
        1 << 20,
        scratch_shapes=[pltpu.VMEM((TOKENS, BLOCK), f32)],
    )


def tree_step(frame, sections, level):
    step = 1 << level
    last = sections - 1
    route = [(i, i + step) for i in range(sections) if (last - i) % (2 * step) == step]
    return frame + lax.ppermute(frame, "section", route)


def per_device(activations, gain, w_query, w_kv, segments, pool, row_ids, row_lengths):
    sections = lax.axis_size("section")
    section = lax.axis_index("section").astype(jnp.int32)
    number = section[None]
    ring_a, ring_b, ring_y = rings(sections, True), rings(sections, False), head_rings(sections)

    def exchange(array, groups):
        return lax.all_to_all(array, AXES, 0, 0, axis_index_groups=groups)

    x = activations[0]
    packed = pack_weights(number % 2, w_query[0], w_kv[0])
    weights = exchange(packed, ring_b)
    own = jnp.concatenate([x, jnp.broadcast_to(gain, (16, BLOCK))], axis=0)
    gathered = exchange(jnp.broadcast_to(own[None], (SIDE,) + own.shape), ring_a)

    frame = make_frame(number, row_ids, row_lengths, pool)
    levels = sections.bit_length() - 1
    for level in range(levels):
        frame = tree_step(frame, sections, level)

    def layer(inputs, blocks, is_second):
        parts = exchange(project(blocks, gathered, weights), ring_b)
        query, keyval = combine(parts)
        keyval = lax.all_gather(keyval, AXES, axis=0, axis_index_groups=ring_y, tiled=True)
        return attend(is_second, number, row_lengths, inputs, query, keyval, segments)

    first = layer(x, gathered, False)
    sent = jnp.where(section == sections - 1, frame, first)
    route = [(i, (i + 1) % sections) for i in range(sections)]
    handed = lax.ppermute(sent, "section", route)
    blocks = exchange(jnp.broadcast_to(handed[None], (SIDE,) + handed.shape), ring_a)
    second = layer(handed, blocks, True)
    return first[None], second[None]


def solution(mesh):
    return jax.shard_map(
        per_device,
        mesh=mesh,
        in_specs=(
            P("section", None, "tensor"),
            P("section", "tensor"),
            P("section", None, "tensor"),
            P("section", "tensor", None),
            P(),
            P("section", None, "tensor"),
            P(),
            P(),
        ),
        out_specs=(P("section", None, "tensor"), P("section", None, "tensor")),
        check_vma=False,
    )
```

time: 340 us -> 155 us (0.46)
  waiting for transfers between devices: 211 us -> 46.7 us
  Pallas kernels: 0 us -> 22.4 us
  matrix products: 18.4 us -> 0 us
  blocking collectives: 67.9 us -> 54.4 us
  between operations: 14 us -> 0.88 us
  starting transfers between devices: 12.9 us -> 21.5 us
  other arithmetic: 9.48 us -> 2.94 us
    all_gather x3 -> x0, waiting for transfers between devices: 197 us -> none  [the longest x2 145 us: attend(): part_cols = lax.all_gather(normed, 'tensor', axis=1, tiled=True)]
    psum x2 -> x0, blocking collectives: 67.9 us -> none  [attend(): lax.psum(jnp.sum(wide_inputs * wide_inputs, axis=1), 'tensor')]
    all_to_all x0 -> x2, blocking collectives: none -> 29.8 us  [exchange(): return lax.all_to_all(array, AXES, 0, 0, axis_index_groups=groups)]
    all_to_all x0 -> x3, waiting for transfers between devices: none -> 26.3 us  [exchange(): return lax.all_to_all(array, AXES, 0, 0, axis_index_groups=groups)]
    all_gather x0 -> x2, blocking collectives: none -> 24.5 us  [layer(): lax.all_gather(keyval, AXES, axis=0, axis_index_groups=ring_y, tiled=True)]
    pallas_call x0 -> x8, Pallas kernels: none -> 22.4 us  [the longest x7 12.8 us: call(): pl.pallas_call(body, out_shape=out_shape, in_specs=specs, out_specs=jax.t...]
    all_to_all x0 -> x3, starting transfers between devices: none -> 17.3 us  [exchange(): return lax.all_to_all(array, AXES, 0, 0, axis_index_groups=groups)]
    dot_general x6 -> x0, matrix products: 16.6 us -> none  [the longest x2 7.42 us: attend(): lax.dot_general(keyval_weight, part_cols, (((1,), (1,)), ((), ())), prefe...]
  transfers between devices with their start and end apart: 8 -> 9, of which waited for: 7 -> 3; matrix products, arithmetic and copies ran while one was open for 6% -> 0% of each run, Pallas kernels for 0% -> 11%
where the time goes in v1:
time: 155 us; the launch traced here: 153 us
  blocking collectives  54.4 us (35%)
  waiting for transfers between devices  46.7 us (30%)
  Pallas kernels  22.4 us (14%)
  starting transfers between devices  21.5 us (14%)
  local copies, waits for them, and re-layouts  4.43 us (3%)
  other arithmetic  2.94 us (2%)
    all_to_all x2, blocking collectives, exchange(): return lax.all_to_all(array, AXES, 0, 0, axis_index_groups=groups)  29.8 us
    all_to_all x3, waiting for transfers between devices, exchange(): return lax.all_to_all(array, AXES, 0, 0, axis_index_groups=groups)  26.3 us
    all_gather x2, blocking collectives, layer(): lax.all_gather(keyval, AXES, axis=0, axis_index_groups=ring_y, tiled=True)  24.5 us
    ppermute x1, waiting for transfers between devices, per_device(): handed = lax.ppermute(sent, 'section', route)  20.4 us
    all_to_all x3, starting transfers between devices, exchange(): return lax.all_to_all(array, AXES, 0, 0, axis_index_groups=groups)  17.3 us
    pallas_call x7, Pallas kernels, call(): pl.pallas_call(body, out_shape=out_shape, in_specs=specs, out_specs=jax.t...  12.8 us
    pallas_call x1, Pallas kernels, pack_weights(): pl.pallas_call(pack_body, out_shape=jax.ShapeDtypeStruct((SIDE, SIDE, BLO...  9.57 us
    ppermute x5, starting transfers between devices, tree_step(): return frame + lax.ppermute(frame, 'section', route)  4.15 us
  transfers between devices with their start and end apart: 9, of which 3 were waited for; matrix products, arithmetic and copies ran while one was open for 0% of the time, Pallas kernels for 11%

profile of v1, /device:TPU:6, one launch (start us, length us, event | category | flops | bytes accessed | tf_op | source)
XLA Modules:
  0.0 153.1 jit_solution(2618532539920237741)
XLA Ops:
  1.3 1.0 pad_maximum_fusion
  2.3 1.0 broadcast_in_dim.31
  3.4 9.3 %all-to-all-start = ((bf16[4,528,256]{2,1,0:T(8,128)(2,1)}), bf16[4,528,256]{2,1,0:T(8,128)(2,1)S(1)}, u32[]{:S(2)}, u32[]{:S(2)}) async-start(bf16[4,528,256]{2,1,0:T(8,128)(2,1)} %broadcast_in_dim.31), calls=%async_computation | async-start | bytes 2162688 | tf_op jit(solution)/shard_map/all_to_all | solution.py:259
  12.7 9.6 %shard_map.95 = bf16[4,4,320,256]{3,2,1,0:T(8,128)(2,1)} custom-call(s32[1]{0:T(128)S(6)} %select_n.15.odd_ref, bf16[4096,256]{1,0:T(8,128)(2,1)} %bitcast.8, bf16[64,4096]{1,0:T(8,128)(2,1)} %bitcast.10), custom_call_target="tpu_custom_call" | custom-call | bytes 5242880 | tf_op jit(solution)/shard_map/pallas_call | solution.py:68
  22.3 1.0 copy-done
  23.3 3.7 %all-to-all-start.1 = ((bf16[4,4,320,256]{3,2,1,0:T(8,128)(2,1)}), bf16[4,4,320,256]{3,2,1,0:T(8,128)(2,1)S(1)}, u32[]{:S(2)}, u32[]{:S(2)}) async-start(bf16[4,4,320,256]{3,2,1,0:T(8,128)(2,1)} %shard_map.95), calls=%async_computation.1 | async-start | bytes 5242880 | tf_op jit(solution)/shard_map/all_to_all | solution.py:259
  27.0 1.3 shard_map.99
  28.3 1.3 collective-permute-start
  29.6 16.6 %all-to-all-done.1.w_ref = bf16[4,4,320,256]{3,2,1,0:T(8,128)(2,1)S(1)} async-done(((bf16[4,4,320,256]{3,2,1,0:T(8,128)(2,1)}), bf16[4,4,320,256]{3,2,1,0:T(8,128)(2,1)S(1)}, u32[]{:S(2)}, u32[]{:S(2)}) %all-to-all-start.1) | async-done | bytes 2621472 | tf_op jit(solution)/shard_map/all_to_all | solution.py:259
  46.2 1.2 copy-done.1
  47.5 2.1 %shard_map.96 = bf16[4,656,256]{2,1,0:T(8,128)(2,1)S(1)} custom-call(bf16[4,528,256]{2,1,0:T(8,128)(2,1)S(1)} %copy-done.1, bf16[4,528,256]{2,1,0:T(8,128)(2,1)S(1)} %copy-done.1, bf16[4,4,320,256]{3,2,1,0:T(8,128)(2,1)S(1)} %all-to-all-done.1.w_ref), custom_call_target="tpu_custom_call" | custom-call | flops 1342177280 | bytes 6291456 | tf_op jit(solution)/shard_map/pallas_call | solution.py:48
  49.6 1.1 copy-done.3
  50.7 4.3 %all-to-all-start.2 = ((bf16[4,656,256]{2,1,0:T(8,128)(2,1)}), bf16[4,656,256]{2,1,0:T(8,128)(2,1)}, u32[]{:S(2)}, u32[]{:S(2)}) async-start(bf16[4,656,256]{2,1,0:T(8,128)(2,1)} %copy-done.3), calls=%async_computation.2 | async-start | bytes 2686976 | tf_op jit(solution)/shard_map/all_to_all | solution.py:259
  58.2 9.6 %all-to-all-done.2.parts_ref = bf16[4,656,256]{2,1,0:T(8,128)(2,1)} async-done(((bf16[4,656,256]{2,1,0:T(8,128)(2,1)}), bf16[4,656,256]{2,1,0:T(8,128)(2,1)}, u32[]{:S(2)}, u32[]{:S(2)}) %all-to-all-start.2) | async-done | bytes 1343520 | tf_op jit(solution)/shard_map/all_to_all | solution.py:259
  67.9 1.5 shard_map.97
  69.4 12.3 %all_gather.6.keyval_ref = bf16[256,512]{1,0:T(8,128)(2,1)S(1)} all-gather(bf16[64,512]{1,0:T(8,128)(2,1)S(1)} %get-tuple-element.7), channel_id=1, replica_groups={{0,1,2,3},{4,5,6,7},{8,9,10,11},{12,13,14,15},{16,17,18,19},{20,21,22,2..., dimensions={0}, use_global_device_ids=true | all-gather | bytes 327680 | tf_op jit(solution)/shard_map/all_gather | solution.py:275
  81.7 2.6 %shard_map.98 = bf16[512,256]{1,0:T(8,128)(2,1)} custom-call(s32[1]{0:T(128)} %bitcast.number_ref, s32[32]{0:T(128)S(1)} %copy-done.7, bf16[512,256]{1,0:T(8,128)(2,1)S(1)} %bitcast.7, bf16[512,256]{1,0:T(8,128)(2,1)S(1)} %get-tuple-element.6.query_ref, bf16[256,512]{1,0:T(8,128)(2,1)S(1)} %all_gather.6.keyval_ref, s32[32,512]{1,0:T(8,128)S(1)} %copy-done.5), custom_call_target="tpu_custom_call" | custom-call | flops 134217728 | bytes 1048576 | tf_op jit(solution)/shard_map/pallas_call | solution.py:48
  84.3 1.0 add_select_fusion
  85.3 20.4 %collective-permute-done.5.x_ref = bf16[512,256]{1,0:T(8,128)(2,1)S(1)} collective-permute-done((bf16[512,256]{1,0:T(8,128)(2,1)S(1)}, bf16[512,256]{1,0:T(8,128)(2,1)S(1)}, u32[]{:S(2)}, u32[]{:S(2)}) %collective-permute-start.5) | collective-permute-done | bytes 262176 | tf_op jit(solution)/shard_map/ppermute | solution.py:281
  105.8 15.0 %all_to_all.25.x_ref = bf16[4,512,256]{2,1,0:T(8,128)(2,1)S(1)} all-to-all(bf16[4,512,256]{2,1,0:T(8,128)(2,1)S(1)} %broadcast_in_dim.33), channel_id=1, replica_groups={{0,4,8,12},{1,5,9,13},{2,6,10,14},{3,7,11,15},{16,17,18,19},{20,21,22,2..., dimensions={0} | all-to-all | bytes 2097152 | tf_op jit(solution)/shard_map/all_to_all | solution.py:259
  120.8 2.1 %shard_map.100 = bf16[4,656,256]{2,1,0:T(8,128)(2,1)S(1)} custom-call(bf16[4,512,256]{2,1,0:T(8,128)(2,1)S(1)} %all_to_all.25.x_ref, bf16[4,528,256]{2,1,0:T(8,128)(2,1)S(1)} %copy-done.2, bf16[4,4,320,256]{3,2,1,0:T(8,128)(2,1)S(1)} %all-to-all-done.1.w_ref), custom_call_target="tpu_custom_call" | custom-call | flops 1342177280 | bytes 6291456 | tf_op jit(solution)/shard_map/pallas_call | solution.py:48
  122.9 14.9 %all_to_all.26.parts_ref = bf16[4,656,256]{2,1,0:T(8,128)(2,1)S(1)} all-to-all(bf16[4,656,256]{2,1,0:T(8,128)(2,1)S(1)} %shard_map.100), channel_id=1, replica_groups={{0,1,2,3},{4,5,6,7},{8,9,10,11},{12,13,14,15},{16,20,24,28},{17,21,25,2..., dimensions={0} | all-to-all | bytes 2686976 | tf_op jit(solution)/shard_map/all_to_all | solution.py:259
  138.0 12.3 %all_gather.7.keyval_ref = bf16[256,512]{1,0:T(8,128)(2,1)S(1)} all-gather(bf16[64,512]{1,0:T(8,128)(2,1)S(1)} %get-tuple-element.9), channel_id=1, replica_groups={{0,1,2,3},{4,5,6,7},{8,9,10,11},{12,13,14,15},{16,17,18,19},{20,21,22,2..., dimensions={0}, use_global_device_ids=true | all-gather | bytes 327680 | tf_op jit(solution)/shard_map/all_gather | solution.py:275
  150.3 2.9 %shard_map.102 = bf16[512,256]{1,0:T(8,128)(2,1)} custom-call(s32[1]{0:T(128)} %bitcast.number_ref, s32[32]{0:T(128)S(1)} %copy-done.7, bf16[512,256]{1,0:T(8,128)(2,1)S(1)} %collective-permute-done.5.x_ref, bf16[512,256]{1,0:T(8,128)(2,1)S(1)} %get-tuple-element.8.query_ref, bf16[256,512]{1,0:T(8,128)(2,1)S(1)} %all_gather.7.keyval_ref, s32[32,512]{1,0:T(8,128)S(1)} %copy-done.5), custom_call_target="tpu_custom_call" | custom-call | flops 134217728 | bytes 1048576 | tf_op jit(solution)/shard_map/pallas_call | solution.py:48
  (34 shorter events, 4.1 us)
Async XLA Ops:
  3.4 18.9 %all-to-all-start = ((bf16[4,528,256]{2,1,0:T(8,128)(2,1)}), bf16[4,528,256]{2,1,0:T(8,128)(2,1)S(1)}, u32[]{:S(2)}, u32[]{:S(2)}) async-start(bf16[4,528,256]{2,1,0:T(8,128)(2,1)} %broadcast_in_dim.31), calls=%async_computation | async-start | bytes 2162688 | tf_op jit(solution)/shard_map/all_to_all | solution.py:259
  22.3 4.7 %copy-start.6 = (bf16[2,128,256]{2,1,0:T(8,128)(2,1)S(1)}, bf16[2,128,256]{2,1,0:T(8,128)(2,1)}, u32[]{:S(2)}) copy-start(bf16[2,128,256]{2,1,0:T(8,128)(2,1)} %pool_ref.1) | copy-start | bytes 393220
  22.3 4.7 %copy-start.7 = (s32[32]{0:T(128)S(1)}, s32[32]{0:T(128)}, u32[]{:S(2)}) copy-start(s32[32]{0:T(128)} %lengths_ref.5) | copy-start | bytes 388
  22.3 4.7 %copy-start.8 = (s32[32]{0:T(128)S(1)}, s32[32]{0:T(128)}, u32[]{:S(2)}) copy-start(s32[32]{0:T(128)} %ids_ref.1) | copy-start | bytes 388
  22.3 1.0 copy-start
  23.3 22.9 %all-to-all-start.1 = ((bf16[4,4,320,256]{3,2,1,0:T(8,128)(2,1)}), bf16[4,4,320,256]{3,2,1,0:T(8,128)(2,1)S(1)}, u32[]{:S(2)}, u32[]{:S(2)}) async-start(bf16[4,4,320,256]{3,2,1,0:T(8,128)(2,1)} %shard_map.95), calls=%async_computation.1 | async-start | bytes 5242880 | tf_op jit(solution)/shard_map/all_to_all | solution.py:259
  28.3 26.7 %collective-permute-start = (bf16[512,256]{1,0:T(8,128)(2,1)S(1)}, bf16[512,256]{1,0:T(8,128)(2,1)S(1)}, u32[]{:S(2)}, u32[]{:S(2)}) collective-permute-start(bf16[512,256]{1,0:T(8,128)(2,1)S(1)} %shard_map.99), channel_id=1, source_target_pairs={{0,16},{32,48},{64,80},{96,112},{128,144},{160,176},{192,208},{224... | collective-permute-start | bytes 786440 | tf_op jit(solution)/shard_map/ppermute | solution.py:249
  46.2 1.2 copy-start.1
  49.6 1.1 copy-start.3
  50.7 17.2 %all-to-all-start.2 = ((bf16[4,656,256]{2,1,0:T(8,128)(2,1)}), bf16[4,656,256]{2,1,0:T(8,128)(2,1)}, u32[]{:S(2)}, u32[]{:S(2)}) async-start(bf16[4,656,256]{2,1,0:T(8,128)(2,1)} %copy-done.3), calls=%async_computation.2 | async-start | bytes 2686976 | tf_op jit(solution)/shard_map/all_to_all | solution.py:259
  55.1 0.7 collective-permute-start.1
  55.9 0.7 collective-permute-start.2
  56.6 25.0 %copy-start.4 = (bf16[1,512,256]{2,1,0:T(8,128)(2,1)S(1)}, bf16[1,512,256]{2,1,0:T(8,128)(2,1)}, u32[]{:S(2)}) copy-start(bf16[1,512,256]{2,1,0:T(8,128)(2,1)} %param.8) | copy-start | bytes 786436
  56.6 25.0 %copy-start.5 = (s32[32,512]{1,0:T(8,128)S(1)}, s32[32,512]{1,0:T(8,128)}, u32[]{:S(2)}) copy-start(s32[32,512]{1,0:T(8,128)} %segments_ref.3) | copy-start | bytes 196612
  56.6 0.8 collective-permute-start.3
  57.5 26.8 %collective-permute-start.4 = (bf16[512,256]{1,0:T(8,128)(2,1)S(1)}, bf16[512,256]{1,0:T(8,128)(2,1)S(1)}, u32[]{:S(2)}, u32[]{:S(2)}) collective-permute-start(bf16[512,256]{1,0:T(8,128)(2,1)S(1)} %add.25), channel_id=1, source_target_pairs={{240,496},{241,497},{242,498},{243,499},{244,500},{245,501},{246,5... | collective-permute-start | bytes 786440 | tf_op jit(solution)/shard_map/ppermute | solution.py:249
  85.3 20.4 %collective-permute-start.5 = (bf16[512,256]{1,0:T(8,128)(2,1)S(1)}, bf16[512,256]{1,0:T(8,128)(2,1)S(1)}, u32[]{:S(2)}, u32[]{:S(2)}) collective-permute-start(bf16[512,256]{1,0:T(8,128)(2,1)S(1)} %add_select_fusion), channel_id=1, source_target_pairs={{0,16},{16,32},{32,48},{48,64},{64,80},{80,96},{96,112},{112,128},... | collective-permute-start | bytes 786440 | tf_op jit(solution)/shard_map/ppermute | solution.py:281
  105.8 15.0 %copy-start.2 = (bf16[4,528,256]{2,1,0:T(8,128)(2,1)S(1)}, bf16[4,528,256]{2,1,0:T(8,128)(2,1)}, u32[]{:S(2)}) copy-start(bf16[4,528,256]{2,1,0:T(8,128)(2,1)} %copy-done) | copy-start | bytes 3244036

commit v2 on v1

v2 whole, which is shorter than its diff:
```python
import functools

import jax
import jax.numpy as jnp
from jax import lax
from jax.experimental import pallas as pl
from jax.experimental.pallas import tpu as pltpu
from jax.sharding import PartitionSpec as P

D = 4096
HEAD_DIM = 128
SIDE = 4
BLOCK = 256
KV_ROWS = 64
TOKENS = 512
HALF = 256
ROW_MAX = 128
HOST_ROWS = 2
SLOTS = 32
SENT_ROWS = 2 * KV_ROWS + 16
PROJECT_VMEM = 62_500_000
AXES = ("section", "tensor")
norm_eps = 1e-05
masked_score = -1e30
f32, bf16 = jnp.float32, jnp.bfloat16
VMEM = pl.BlockSpec(memory_space=pltpu.VMEM)
ANY = pl.BlockSpec(memory_space=pl.ANY)
SMEM = pl.BlockSpec(memory_space=pltpu.SMEM)
NT = (((1,), (1,)), ((), ()))


def place(section, first, second):
    return SIDE * first + second if section % 2 == 0 else SIDE * second + first


def rings(sections, along_a):
    groups = []
    for s in range(sections):
        for i in range(SIDE):
            ring = [(place(s, j, i) if along_a else place(s, i, j)) for j in range(SIDE)]
            groups.append([s * SIDE * SIDE + t for t in ring])
    return groups


def head_rings(sections):
    return [[(s * SIDE + g) * SIDE + i for i in range(SIDE)] for s in range(sections) for g in range(SIDE)]


def call(body, out_shape, operands, specs, flops, moved, out_specs=None, vmem=12 << 20, **more):
    return pl.pallas_call(
        body,
        out_shape=out_shape,
        in_specs=specs,
        out_specs=out_specs or jax.tree.map(lambda _: VMEM, out_shape),
        compiler_params=pltpu.CompilerParams(vmem_limit_bytes=vmem),
        cost_estimate=pl.CostEstimate(flops=flops, bytes_accessed=moved, transcendentals=0),
        **more,
    )(*operands)


def prepare_body(x_ref, gain_ref, query_ref, keyval_ref, packed_ref, own_ref, gain_rows, sems):
    odd = lax.axis_index("section") % 2
    gain_rows[...] = jnp.broadcast_to(gain_ref[...].astype(f32), (16, BLOCK)).astype(bf16)
    copies = [
        (x_ref, own_ref.at[pl.ds(0, TOKENS)]),
        (gain_rows, own_ref.at[pl.ds(TOKENS, 16)]),
    ]
    for i in range(SIDE):
        for j in range(SIDE):
            start = pl.multiple_of(jnp.where(odd == 1, SIDE * i + j, SIDE * j + i) * BLOCK, BLOCK)
            copies.append((query_ref.at[pl.ds(start, BLOCK)], packed_ref.at[i, j, pl.ds(0, BLOCK)]))
            copies.append((keyval_ref.at[:, pl.ds(start, BLOCK)], packed_ref.at[i, j, pl.ds(BLOCK, KV_ROWS)]))
    copies = [pltpu.make_async_copy(src, dst, sems.at[n]) for n, (src, dst) in enumerate(copies)]
    for copy in copies:
        copy.start()
    for copy in copies:
        copy.wait()


def prepare(x, gain, w_query, w_kv):
    return pl.pallas_call(
        prepare_body,
        out_shape=(
            jax.ShapeDtypeStruct((SIDE, SIDE, BLOCK + KV_ROWS, BLOCK), bf16),
            jax.ShapeDtypeStruct((TOKENS + 16, BLOCK), bf16),
        ),
        in_specs=[ANY, VMEM, ANY, ANY],
        out_specs=(ANY, ANY),
        scratch_shapes=[pltpu.VMEM((16, BLOCK), bf16), pltpu.SemaphoreType.DMA((2 + 2 * SIDE * SIDE,))],
        cost_estimate=pl.CostEstimate(flops=0, bytes_accessed=6 << 20, transcendentals=0),
    )(x, gain, w_query, w_kv)


def ring_place():
    section, tensor = lax.axis_index("section"), lax.axis_index("tensor")
    return jnp.where(section % 2 == 1, tensor % SIDE, tensor // SIDE)


def project_body(is_second, *refs):
    x_refs, gain_refs = refs[:SIDE], refs[SIDE : SIDE + is_second]
    w_hbm, query_ref, keyval_ref, *more, x_ref, w_ref, wide_ref, kv_ref, made_ref, sems = refs[SIDE + len(gain_refs) :]
    x_copies = [pltpu.make_async_copy(x_refs[d], x_ref.at[d], sems.at[d]) for d in range(SIDE)]
    w_copies = [pltpu.make_async_copy(w_hbm.at[b], w_ref.at[b], sems.at[SIDE + b]) for b in range(SIDE)]
    for copy in x_copies + w_copies:
        copy.start()
    here = ring_place()
    origins = [(here + SIDE - d) % SIDE for d in range(SIDE)]
    ones = jnp.ones((8, BLOCK), bf16)
    squares = jnp.zeros((8, TOKENS), f32)
    for d in range(SIDE):
        x_copies[d].wait()
        cols = slice(d * BLOCK, (d + 1) * BLOCK)
        if is_second:
            gain = gain_refs[0][16 * d : 16 * d + 1]
        else:
            gain = x_ref[d, TOKENS : TOKENS + 1]
            more[0][16 * d : 16 * (d + 1)] = x_ref[d, TOKENS:]
        part = x_ref[d, :TOKENS].astype(f32)
        wide_ref[:, cols] = (part * gain.astype(f32)).astype(bf16)
        square = part * part
        upper = square.astype(bf16)
        lower = (square - upper.astype(f32)).astype(bf16)
        squares += lax.dot_general(ones, upper, NT, preferred_element_type=f32)
        squares += lax.dot_general(ones, lower, NT, preferred_element_type=f32)
    copies = []
    for b in range(SIDE):
        w_copies[b].wait()
        for d in range(SIDE):
            kv_ref[b * KV_ROWS : (b + 1) * KV_ROWS, d * BLOCK : (d + 1) * BLOCK] = w_ref[b, origins[d], BLOCK:]
        total = jnp.zeros((TOKENS, BLOCK), f32)
        for d in range(SIDE):
            total += jnp.dot(
                wide_ref[:, d * BLOCK : (d + 1) * BLOCK], w_ref[b, origins[d], :BLOCK], preferred_element_type=f32
            )
        made_ref[b] = total.astype(bf16)
        copy = pltpu.make_async_copy(made_ref.at[b], query_ref.at[b], sems.at[2 * SIDE + b])
        copy.start()
        copies.append(copy)
    keyval = lax.dot_general(kv_ref[...], wide_ref[...], NT, preferred_element_type=f32).astype(bf16)
    first = squares.astype(bf16)
    second = (squares - first.astype(f32)).astype(bf16)
    stats = [first[:1, :HALF], first[:1, HALF:], second[:1, :HALF], second[:1, HALF:]]
    stats = jnp.concatenate([s.astype(f32) for s in stats] + [jnp.zeros((12, HALF), f32)], axis=0).astype(bf16)
    for b in range(SIDE):
        rows = slice(b * KV_ROWS, (b + 1) * KV_ROWS)
        keyval_ref[b, :KV_ROWS] = keyval[rows, :HALF]
        keyval_ref[b, KV_ROWS : 2 * KV_ROWS] = keyval[rows, HALF:]
        keyval_ref[b, 2 * KV_ROWS :] = stats
    for copy in copies:
        copy.wait()


def project(is_second, blocks, gains, weights):
    made = (SIDE, TOKENS, BLOCK)
    out_shape = [jax.ShapeDtypeStruct(made, bf16), jax.ShapeDtypeStruct((SIDE, SENT_ROWS, HALF), bf16)]
    if not is_second:
        out_shape.append(jax.ShapeDtypeStruct((16 * SIDE, BLOCK), bf16))
    return call(
        functools.partial(project_body, is_second),
        tuple(out_shape),
        (*blocks, *gains, weights),
        [ANY] * SIDE + [VMEM] * len(gains) + [ANY],
        2 * TOKENS * 1024 * 1280,
        5 << 20,
        out_specs=(ANY,) + (VMEM,) * (len(out_shape) - 1),
        vmem=PROJECT_VMEM,
        scratch_shapes=[
            pltpu.VMEM((SIDE, *blocks[0].shape), bf16),
            pltpu.VMEM(weights.shape, bf16),
            pltpu.VMEM((TOKENS, SIDE * BLOCK), bf16),
            pltpu.VMEM((SIDE * KV_ROWS, SIDE * BLOCK), bf16),
            pltpu.VMEM(made, bf16),
            pltpu.SemaphoreType.DMA((3 * SIDE,)),
        ],
    )


def down(row):
    return jnp.transpose(jnp.broadcast_to(row, (HEAD_DIM, HEAD_DIM)))


def combine_body(parts_ref, keyval_ref, scale_ref):
    tail = parts_ref[0].astype(f32)
    for b in range(1, SIDE):
        tail += parts_ref[b].astype(f32)
    stats = tail[2 * KV_ROWS :]
    for h in range(2):
        cols = slice(h * HALF, (h + 1) * HALF)
        scale = lax.rsqrt((stats[h : h + 1] + stats[2 + h : 3 + h]) / D + norm_eps)
        keyval_ref[:, cols] = (tail[h * KV_ROWS : (h + 1) * KV_ROWS] * scale).astype(bf16)
        scale_ref[:, cols] = jnp.broadcast_to(scale, (8, HALF))


def combine(parts):
    return call(
        combine_body,
        (jax.ShapeDtypeStruct((KV_ROWS, TOKENS), bf16), jax.ShapeDtypeStruct((8, TOKENS), f32)),
        (parts,),
        [VMEM],
        TOKENS * KV_ROWS * 8,
        1 << 19,
    )


def attend_body(is_second, lengths_ref, x_ref, parts_ref, scale_ref, keyval_ref, segments_ref, *refs):
    section = lax.axis_index("section")
    if is_second:
        (out_ref,) = refs
    else:
        *frame_refs, out_ref, sent_ref, held, sems = refs
    if is_second:
        ids = segments_ref[pl.ds(jnp.maximum(section - 1, 0), 1), :]
        spot = lax.broadcasted_iota(jnp.int32, (1, TOKENS), 1)

        def count(k, carried):
            end, slot = carried
            end = end + lengths_ref[k]
            return end, slot + (spot >= end).astype(jnp.int32)

        _, slot = lax.fori_loop(0, SLOTS, count, (jnp.int32(0), jnp.zeros((1, TOKENS), jnp.int32)))
        ids = jnp.where(section == 0, slot, ids)
    else:
        ids = segments_ref[pl.ds(section, 1), :]
    ids = ids.astype(f32)
    for i in range(TOKENS // HEAD_DIM):
        rows = slice(i * HEAD_DIM, (i + 1) * HEAD_DIM)
        low = max(i - 1, 0) * HEAD_DIM
        width = (i + 1) * HEAD_DIM - low
        cols = slice(low, low + width)
        own = down(ids[:, rows])
        if width > HEAD_DIM:
            own = jnp.concatenate([own, own], axis=1)
        place_r = lax.broadcasted_iota(jnp.int32, (HEAD_DIM, width), 0) + i * HEAD_DIM
        place_c = lax.broadcasted_iota(jnp.int32, (HEAD_DIM, width), 1) + low
        allowed = (own == ids[:, cols]) & (place_c <= place_r)
        total = parts_ref[0, rows].astype(f32)
        for b in range(1, SIDE):
            total += parts_ref[b, rows].astype(f32)
        factor = down(scale_ref[:1, rows])
        query = (total * jnp.concatenate([factor, factor], axis=1)).astype(bf16)
        keys = keyval_ref[:HEAD_DIM, cols]
        values = keyval_ref[HEAD_DIM:, cols]
        for h in range(2):
            lanes = slice(h * HEAD_DIM, (h + 1) * HEAD_DIM)
            scores = jnp.dot(query[:, lanes], keys, preferred_element_type=f32) * HEAD_DIM ** (-0.5)
            scores = jnp.where(allowed, scores, masked_score)
            grown = jnp.exp(scores - jnp.max(scores, axis=1, keepdims=True))
            weights = (grown / jnp.sum(grown, axis=1, keepdims=True)).astype(bf16)
            context = lax.dot_general(weights, values, NT, preferred_element_type=f32).astype(bf16)
            done = (x_ref[rows, lanes].astype(f32) + context.astype(f32)).astype(bf16)
            out_ref[rows, lanes] = done
            if not is_second:
                sent_ref[rows, lanes] = done
    if not is_second:

        @pl.when(section == lax.axis_size("section") - 1)
        def _():
            copies = [pltpu.make_async_copy(ref, held.at[n], sems.at[n]) for n, ref in enumerate(frame_refs)]
            for copy in copies:
                copy.start()
            for copy in copies:
                copy.wait()
            sent_ref[...] = functools.reduce(jnp.add, [held[n].astype(f32) for n in range(SIDE)]).astype(bf16)


def attend(is_second, lengths, x, parts, scale, keyval, segments, frames):
    made = jax.ShapeDtypeStruct((TOKENS, BLOCK), bf16)
    held = pltpu.VMEM((SIDE, TOKENS, BLOCK), bf16)
    scratch = [] if is_second else [held, pltpu.SemaphoreType.DMA((SIDE,))]
    return call(
        functools.partial(attend_body, is_second),
        made if is_second else (made, made),
        (lengths, x, parts, scale, keyval, segments, *frames),
        [SMEM] + [VMEM] * 5 + [ANY] * len(frames),
        2 * TOKENS * 256 * 128 * 4,
        1 << 20,
        scratch_shapes=scratch,
    )


def frame_body(ids_ref, lengths_ref, pool_ref, out_ref, total_ref):
    total_ref[...] = jnp.zeros_like(total_ref)
    section = lax.axis_index("section")
    row = lax.broadcasted_iota(jnp.int32, (TOKENS, ROW_MAX), 0)
    col = lax.broadcasted_iota(jnp.int32, (TOKENS, ROW_MAX), 1)

    def take(k, start):
        length = lengths_ref[k]
        which = ids_ref[k] - HOST_ROWS * section

        @pl.when((which >= 0) & (which < HOST_ROWS))
        def _():
            hit = ((row - start == col) & (col < length)).astype(f32).astype(bf16)
            total_ref[...] += jnp.dot(hit, pool_ref[which], preferred_element_type=f32)

        return start + length

    lax.fori_loop(0, SLOTS, take, jnp.int32(0))
    out_ref[...] = total_ref[...].astype(bf16)


def make_frame(row_ids, row_lengths, pool):
    return call(
        frame_body,
        jax.ShapeDtypeStruct((TOKENS, BLOCK), bf16),
        (row_ids, row_lengths, pool),
        [SMEM, SMEM, VMEM],
        2 * TOKENS * 128 * 256,
        1 << 20,
        scratch_shapes=[pltpu.VMEM((TOKENS, BLOCK), f32)],
    )


def bring(array, sections, step, count=1):
    last, span = sections - 1, (count + 1) * step
    got = []
    for n in range(1, count + 1):
        route = [(i - n * step, i) for i in range(sections) if (last - i) % span == 0]
        got.append(lax.ppermute(array, "section", route))
    return got


def per_device(activations, gain, w_query, w_kv, segments, pool, row_ids, row_lengths):
    sections = lax.axis_size("section")
    ring_b, ring_y = rings(sections, False), head_rings(sections)
    grid = [(s, a, b) for s in range(sections) for a in range(SIDE) for b in range(SIDE)]
    barrier = lax.optimization_barrier

    def number(s, a, b, like):
        return s * SIDE * SIDE + place(like, a % SIDE, b)

    def exchange(array):
        return lax.all_to_all(array, AXES, 0, 0, axis_index_groups=ring_b)

    x = activations[0]
    packed, own = prepare(x, gain, w_query[0], w_kv[0])
    weights = exchange(packed)
    blocks = [own]
    for d in range(1, SIDE):
        route = [(number(s, a - d, b, s), number(s, a, b, s)) for s, a, b in grid]
        blocks.append(lax.ppermute(own, AXES, route))

    blocks, pool = barrier((blocks, pool))
    frame = make_frame(row_ids, row_lengths, pool)
    frame = frame + bring(frame, sections, 1)[0]
    weights, frame = barrier((weights, frame))
    piece = bring(frame, sections, 2)[0]

    query_parts, keyval_parts, gains = project(False, blocks, [], weights)
    query_parts = exchange(query_parts)
    keyval_parts, frame = barrier((keyval_parts, frame + piece))
    piece = bring(frame, sections, 4)[0]
    keyval, scale = combine(exchange(keyval_parts))
    keyval, frame = barrier((keyval, frame + piece))
    frames = [frame, *bring(frame, sections, 8, 3)]
    keyval = lax.all_gather(keyval, AXES, axis=0, axis_index_groups=ring_y, tiled=True)
    first, sent = attend(False, row_lengths, x, query_parts, scale, keyval, segments, frames)

    blocks = []
    for d in range(SIDE):
        route = [(number((s - 1) % sections, a - d, b, s), number(s, a, b, s)) for s, a, b in grid]
        blocks.append(lax.ppermute(sent, AXES, route))
    query_parts, keyval_parts = project(True, blocks, [gains], weights)
    query_parts = exchange(query_parts)
    keyval, scale = combine(exchange(keyval_parts))
    keyval = lax.all_gather(keyval, AXES, axis=0, axis_index_groups=ring_y, tiled=True)
    second = attend(True, row_lengths, blocks[0], query_parts, scale, keyval, segments, [])
    return first[None], second[None]


def solution(mesh):
    return jax.shard_map(
        per_device,
        mesh=mesh,
        in_specs=(
            P("section", None, "tensor"),
            P("section", "tensor"),
            P("section", None, "tensor"),
            P("section", "tensor", None),
            P(),
            P("section", None, "tensor"),
            P(),
            P(),
        ),
        out_specs=(P("section", None, "tensor"), P("section", None, "tensor")),
        check_vma=False,
    )
```

time: 155 us -> 238 us (1.54)
  Pallas kernels: 22.4 us -> 109 us
  starting transfers between devices: 21.5 us -> 42.6 us
  waiting for transfers between devices: 46.7 us -> 27.9 us
  local copies, waits for them, and re-layouts: 4.43 us -> 0.76 us
  other arithmetic: 2.94 us -> 0.21 us
    pallas_call x8, Pallas kernels: 22.4 us -> 109 us  [the longest x1 89.4 us: prepare(): pl.pallas_call(prepare_body, out_shape=(jax.ShapeDtypeStruct((SIDE, SIDE,...]
    ppermute x6 -> x13, starting transfers between devices: 4.17 us -> 30.9 us  [the longest x3 13.1 us: per_device(): blocks.append(lax.ppermute(own, AXES, route))]
    all_to_all x3, waiting for transfers between devices: 26.3 us -> 0.01 us  [exchange(): return lax.all_to_all(array, AXES, 0, 0, axis_index_groups=ring_b)]
    ppermute x6 -> x13, waiting for transfers between devices: 20.4 us -> 27.9 us  [the longest x4 17.7 us: per_device(): blocks.append(lax.ppermute(sent, AXES, route))]
    all_gather x2, blocking collectives: 24.5 us -> 31.3 us  [per_device(): lax.all_gather(keyval, AXES, axis=0, axis_index_groups=ring_y, tiled=True)]
    all_to_all x2, blocking collectives: 29.8 us -> 24.1 us  [exchange(): return lax.all_to_all(array, AXES, 0, 0, axis_index_groups=ring_b)]
    all_to_all x3, starting transfers between devices: 17.3 us -> 11.7 us  [exchange(): return lax.all_to_all(array, AXES, 0, 0, axis_index_groups=ring_b)]
    unnamed x18 -> x28, local copies, waits for them, and re-layouts: 3.31 us -> 0.76 us
  transfers between devices with their start and end apart: 9 -> 16, of which waited for: 3 -> 7; matrix products, arithmetic and copies ran while one was open for 0% -> 0% of each run, Pallas kernels for 11% -> 3%
where the time goes in v2:
time: 238 us; the launch traced here: 237 us
  Pallas kernels  109 us (46%)
  blocking collectives  55.4 us (23%)
  starting transfers between devices  42.6 us (18%)
  waiting for transfers between devices  27.9 us (12%)
    pallas_call x1, Pallas kernels, prepare(): pl.pallas_call(prepare_body, out_shape=(jax.ShapeDtypeStruct((SIDE, SIDE,...  89.4 us
    all_gather x2, blocking collectives, per_device(): lax.all_gather(keyval, AXES, axis=0, axis_index_groups=ring_y, tiled=True)  31.3 us
    all_to_all x2, blocking collectives, exchange(): return lax.all_to_all(array, AXES, 0, 0, axis_index_groups=ring_b)  24.1 us
    pallas_call x7, Pallas kernels, call(): pl.pallas_call(body, out_shape=out_shape, in_specs=specs, out_specs=out_s...  19.8 us
    ppermute x4, waiting for transfers between devices, per_device(): blocks.append(lax.ppermute(sent, AXES, route))  17.7 us
    ppermute x3, starting transfers between devices, per_device(): blocks.append(lax.ppermute(own, AXES, route))  13.1 us
    ppermute x4, starting transfers between devices, per_device(): blocks.append(lax.ppermute(sent, AXES, route))  12.8 us
    all_to_all x3, starting transfers between devices, exchange(): return lax.all_to_all(array, AXES, 0, 0, axis_index_groups=ring_b)  11.7 us
  transfers between devices with their start and end apart: 16, of which 7 were waited for; matrix products, arithmetic and copies ran while one was open for 0% of the time, Pallas kernels for 3%

profile of v2, /device:TPU:6, one launch (start us, length us, event | category | flops | bytes accessed | tf_op | source)
XLA Modules:
  0.0 237.1 jit_solution(3008030363891161089)
XLA Ops:
  0.6 89.4 %shard_map.95 = (bf16[4,4,320,256]{3,2,1,0:T(8,128)(2,1)}, bf16[528,256]{1,0:T(8,128)(2,1)}) custom-call(bf16[512,256]{1,0:T(8,128)(2,1)} %bitcast.5, bf16[1,256]{1,0:T(2,128)(2,1)} %gain_ref.1, bf16[4096,256]{1,0:T(8,128)(2,1)} %bitcast.7, bf16[64,4096]{1,0:T(8,128)(2,1)} %bitcast.8), custom_call_target="tpu_custom_call" | custom-call | bytes 6291456 | tf_op jit(solution)/shard_map/pallas_call | solution.py:81
  90.1 4.7 %all-to-all-start = ((bf16[4,4,320,256]{3,2,1,0:T(8,128)(2,1)}), bf16[4,4,320,256]{3,2,1,0:T(8,128)(2,1)}, u32[]{:S(2)}, u32[]{:S(2)}) async-start(bf16[4,4,320,256]{3,2,1,0:T(8,128)(2,1)} %get-tuple-element.31), calls=%async_computation | async-start | bytes 5242880 | tf_op jit(solution)/shard_map/all_to_all | solution.py:333
  94.8 2.7 %collective-permute-start.2 = (bf16[528,256]{1,0:T(8,128)(2,1)S(1)}, bf16[528,256]{1,0:T(8,128)(2,1)S(1)}, u32[]{:S(2)}, u32[]{:S(2)}) collective-permute-start(bf16[528,256]{1,0:T(8,128)(2,1)S(1)} %copy-done.7), channel_id=1, source_target_pairs={{4,0},{5,1},{6,2},{7,3},{8,4},{9,5},{10,6},{11,7},{12,8},{13,9},{1... | collective-permute-start | bytes 811016 | tf_op jit(solution)/shard_map/ppermute | solution.py:341
  97.6 8.4 %collective-permute-start.1 = (bf16[528,256]{1,0:T(8,128)(2,1)S(1)}, bf16[528,256]{1,0:T(8,128)(2,1)S(1)}, u32[]{:S(2)}, u32[]{:S(2)}) collective-permute-start(bf16[528,256]{1,0:T(8,128)(2,1)S(1)} %copy-done.7), channel_id=1, source_target_pairs={{8,0},{9,1},{10,2},{11,3},{12,4},{13,5},{14,6},{15,7},{0,8},{1,9},... | collective-permute-start | bytes 811016 | tf_op jit(solution)/shard_map/ppermute | solution.py:341
  106.0 1.9 collective-permute-start
  107.9 3.5 %collective-permute-done.2.refs_3_ = bf16[528,256]{1,0:T(8,128)(2,1)S(1)} collective-permute-done((bf16[528,256]{1,0:T(8,128)(2,1)S(1)}, bf16[528,256]{1,0:T(8,128)(2,1)S(1)}, u32[]{:S(2)}, u32[]{:S(2)}) %collective-permute-start.2) | collective-permute-done | bytes 270368 | tf_op jit(solution)/shard_map/ppermute | solution.py:341
  111.5 5.5 %collective-permute-done.1.refs_2_ = bf16[528,256]{1,0:T(8,128)(2,1)S(1)} collective-permute-done((bf16[528,256]{1,0:T(8,128)(2,1)S(1)}, bf16[528,256]{1,0:T(8,128)(2,1)S(1)}, u32[]{:S(2)}, u32[]{:S(2)}) %collective-permute-start.1) | collective-permute-done | bytes 270368 | tf_op jit(solution)/shard_map/ppermute | solution.py:341
  121.9 6.0 %shard_map.97 = (bf16[4,512,256]{2,1,0:T(8,128)(2,1)}, bf16[4,144,256]{2,1,0:T(8,128)(2,1)}, bf16[64,256]{1,0:T(8,128)(2,1)}) custom-call(bf16[528,256]{1,0:T(8,128)(2,1)} %get-tuple-element.27.refs_0_, bf16[528,256]{1,0:T(8,128)(2,1)} %copy-done.10, bf16[528,256]{1,0:T(8,128)(2,1)} %copy-done.9, bf16[528,256]{1,0:T(8,128)(2,1)} %copy-done.8, ...), custom_call_target="tpu_custom_call" | custom-call | flops 1342177280 | bytes 5242880 | tf_op jit(solution)/shard_map/pallas_call | solution.py:50
  128.0 11.9 %all_to_all.25.parts_ref = bf16[4,144,256]{2,1,0:T(8,128)(2,1)S(1)} all-to-all(bf16[4,144,256]{2,1,0:T(8,128)(2,1)} %get-tuple-element.37), channel_id=1, replica_groups={{0,1,2,3},{4,5,6,7},{8,9,10,11},{12,13,14,15},{16,20,24,28},{17,21,25,2..., dimensions={0} | all-to-all | bytes 589824 | tf_op jit(solution)/shard_map/all_to_all | solution.py:333
  140.0 3.5 %all-to-all-start.1 = ((bf16[4,512,256]{2,1,0:T(8,128)(2,1)}), bf16[4,512,256]{2,1,0:T(8,128)(2,1)S(1)}, u32[]{:S(2)}, u32[]{:S(2)}) async-start(bf16[4,512,256]{2,1,0:T(8,128)(2,1)} %get-tuple-element.34), calls=%async_computation.1 | async-start | bytes 2097152 | tf_op jit(solution)/shard_map/all_to_all | solution.py:333
  146.4 15.1 %all_gather.6.keyval_ref = bf16[256,512]{1,0:T(8,128)(2,1)S(1)} all-gather(bf16[64,512]{1,0:T(8,128)(2,1)S(1)} %get-tuple-element.41), channel_id=1, replica_groups={{0,1,2,3},{4,5,6,7},{8,9,10,11},{12,13,14,15},{16,17,18,19},{20,21,22,2..., dimensions={0}, use_global_device_ids=true | all-gather | bytes 327680 | tf_op jit(solution)/shard_map/all_gather | solution.py:356
  161.5 2.7 %shard_map.99 = (bf16[512,256]{1,0:T(8,128)(2,1)}, bf16[512,256]{1,0:T(8,128)(2,1)S(1)}) custom-call(s32[32]{0:T(128)S(1)} %copy-done.5, bf16[512,256]{1,0:T(8,128)(2,1)S(1)} %bitcast.6, bf16[4,512,256]{2,1,0:T(8,128)(2,1)S(1)} %all-to-all-done.1.parts_ref, f32[8,512]{1,0:T(8,128)S(1)} %get-tuple-element.38.scale_ref, ...), custom_call_target="tpu_custom_call" | custom-call | flops 134217728 | bytes 1048576 | tf_op jit(solution)/shard_map/pallas_call | solution.py:50
  164.3 1.9 collective-permute-start.12
  166.2 4.7 %collective-permute-start.11 = (bf16[512,256]{1,0:T(8,128)(2,1)S(1)}, bf16[512,256]{1,0:T(8,128)(2,1)S(1)}, u32[]{:S(2)}, u32[]{:S(2)}) collective-permute-start(bf16[512,256]{1,0:T(8,128)(2,1)S(1)} %get-tuple-element.44), channel_id=1, source_target_pairs={{504,0},{505,1},{506,2},{507,3},{508,4},{509,5},{510,6},{511,7},{4... | collective-permute-start | bytes 786440 | tf_op jit(solution)/shard_map/ppermute | solution.py:362
  170.9 5.0 %collective-permute-start.10 = (bf16[512,256]{1,0:T(8,128)(2,1)S(1)}, bf16[512,256]{1,0:T(8,128)(2,1)S(1)}, u32[]{:S(2)}, u32[]{:S(2)}) collective-permute-start(bf16[512,256]{1,0:T(8,128)(2,1)S(1)} %get-tuple-element.44), channel_id=1, source_target_pairs={{508,0},{509,1},{510,2},{511,3},{496,4},{497,5},{498,6},{499,7},{5... | collective-permute-start | bytes 786440 | tf_op jit(solution)/shard_map/ppermute | solution.py:362
  177.0 8.9 %collective-permute-done.12.refs_3_ = bf16[512,256]{1,0:T(8,128)(2,1)S(1)} collective-permute-done((bf16[512,256]{1,0:T(8,128)(2,1)S(1)}, bf16[512,256]{1,0:T(8,128)(2,1)S(1)}, u32[]{:S(2)}, u32[]{:S(2)}) %collective-permute-start.12) | collective-permute-done | bytes 262176 | tf_op jit(solution)/shard_map/ppermute | solution.py:362
  185.9 3.9 %collective-permute-done.11.refs_2_ = bf16[512,256]{1,0:T(8,128)(2,1)S(1)} collective-permute-done((bf16[512,256]{1,0:T(8,128)(2,1)S(1)}, bf16[512,256]{1,0:T(8,128)(2,1)S(1)}, u32[]{:S(2)}, u32[]{:S(2)}) %collective-permute-start.11) | collective-permute-done | bytes 262176 | tf_op jit(solution)/shard_map/ppermute | solution.py:362
  189.8 2.2 collective-permute-done.10.refs_1_
  192.0 2.7 %collective-permute-done.9.refs_0_.x_ref = bf16[512,256]{1,0:T(8,128)(2,1)S(1)} collective-permute-done((bf16[512,256]{1,0:T(8,128)(2,1)S(1)}, bf16[512,256]{1,0:T(8,128)(2,1)S(1)}, u32[]{:S(2)}, u32[]{:S(2)}) %collective-permute-start.9) | collective-permute-done | bytes 262176 | tf_op jit(solution)/shard_map/ppermute | solution.py:362
  195.5 6.8 %shard_map.100 = (bf16[4,512,256]{2,1,0:T(8,128)(2,1)}, bf16[4,144,256]{2,1,0:T(8,128)(2,1)}) custom-call(bf16[512,256]{1,0:T(8,128)(2,1)} %copy-done.2, bf16[512,256]{1,0:T(8,128)(2,1)} %copy-done.13, bf16[512,256]{1,0:T(8,128)(2,1)} %copy-done.12, bf16[512,256]{1,0:T(8,128)(2,1)} %copy-done.11, bf16[64,256]{1,0:T(8,128)(2,1)} %get-tuple-element.45.refs_4_, ...), custom_call_target="tpu_custom_call" | custom-call | flops 1342177280 | bytes 5242880 | tf_op jit(solution)/shard_map/pallas_call | solution.py:50
  202.3 12.2 %all_to_all.26.parts_ref = bf16[4,144,256]{2,1,0:T(8,128)(2,1)S(1)} all-to-all(bf16[4,144,256]{2,1,0:T(8,128)(2,1)} %get-tuple-element.47), channel_id=1, replica_groups={{0,1,2,3},{4,5,6,7},{8,9,10,11},{12,13,14,15},{16,20,24,28},{17,21,25,2..., dimensions={0} | all-to-all | bytes 589824 | tf_op jit(solution)/shard_map/all_to_all | solution.py:333
  214.5 3.5 %all-to-all-start.3 = ((bf16[4,512,256]{2,1,0:T(8,128)(2,1)}), bf16[4,512,256]{2,1,0:T(8,128)(2,1)S(1)}, u32[]{:S(2)}, u32[]{:S(2)}) async-start(bf16[4,512,256]{2,1,0:T(8,128)(2,1)} %get-tuple-element.46), calls=%async_computation.3 | async-start | bytes 2097152 | tf_op jit(solution)/shard_map/all_to_all | solution.py:333
  218.1 16.1 %all_gather.7.keyval_ref = bf16[256,512]{1,0:T(8,128)(2,1)S(1)} all-gather(bf16[64,512]{1,0:T(8,128)(2,1)S(1)} %get-tuple-element.49), channel_id=1, replica_groups={{0,1,2,3},{4,5,6,7},{8,9,10,11},{12,13,14,15},{16,17,18,19},{20,21,22,2..., dimensions={0}, use_global_device_ids=true | all-gather | bytes 327680 | tf_op jit(solution)/shard_map/all_gather | solution.py:366
  234.2 2.9 %shard_map.102 = bf16[512,256]{1,0:T(8,128)(2,1)} custom-call(s32[32]{0:T(128)S(1)} %copy-done.5, bf16[512,256]{1,0:T(8,128)(2,1)S(1)} %copy-done.3, bf16[4,512,256]{2,1,0:T(8,128)(2,1)S(1)} %all-to-all-done.3.parts_ref, f32[8,512]{1,0:T(8,128)S(1)} %get-tuple-element.48.scale_ref, bf16[256,512]{1,0:T(8,128)(2,1)S(1)} %all_gather.7.keyval_ref, ...), custom_call_target="tpu_custom_call" | custom-call | flops 134217728 | bytes 1048576 | tf_op jit(solution)/shard_map/pallas_call | solution.py:50
  (51 shorter events, 9.7 us)
Async XLA Ops:
  90.1 26.9 %copy-start.4 = (bf16[2,128,256]{2,1,0:T(8,128)(2,1)S(1)}, bf16[2,128,256]{2,1,0:T(8,128)(2,1)}, u32[]{:S(2)}) copy-start(bf16[2,128,256]{2,1,0:T(8,128)(2,1)} %pool_ref) | copy-start | bytes 393220
  90.1 26.9 %copy-start.5 = (s32[32]{0:T(128)S(1)}, s32[32]{0:T(128)}, u32[]{:S(2)}) copy-start(s32[32]{0:T(128)} %lengths_ref.5) | copy-start | bytes 388
  90.1 26.9 %copy-start.6 = (s32[32]{0:T(128)S(1)}, s32[32]{0:T(128)}, u32[]{:S(2)}) copy-start(s32[32]{0:T(128)} %ids_ref.1) | copy-start | bytes 388
  90.1 31.0 %all-to-all-start = ((bf16[4,4,320,256]{3,2,1,0:T(8,128)(2,1)}), bf16[4,4,320,256]{3,2,1,0:T(8,128)(2,1)}, u32[]{:S(2)}, u32[]{:S(2)}) async-start(bf16[4,4,320,256]{3,2,1,0:T(8,128)(2,1)} %get-tuple-element.31), calls=%async_computation | async-start | bytes 5242880 | tf_op jit(solution)/shard_map/all_to_all | solution.py:333
  94.8 16.6 %collective-permute-start.2 = (bf16[528,256]{1,0:T(8,128)(2,1)S(1)}, bf16[528,256]{1,0:T(8,128)(2,1)S(1)}, u32[]{:S(2)}, u32[]{:S(2)}) collective-permute-start(bf16[528,256]{1,0:T(8,128)(2,1)S(1)} %copy-done.7), channel_id=1, source_target_pairs={{4,0},{5,1},{6,2},{7,3},{8,4},{9,5},{10,6},{11,7},{12,8},{13,9},{1... | collective-permute-start | bytes 811016 | tf_op jit(solution)/shard_map/ppermute | solution.py:341
  97.6 19.3 %collective-permute-start.1 = (bf16[528,256]{1,0:T(8,128)(2,1)S(1)}, bf16[528,256]{1,0:T(8,128)(2,1)S(1)}, u32[]{:S(2)}, u32[]{:S(2)}) collective-permute-start(bf16[528,256]{1,0:T(8,128)(2,1)S(1)} %copy-done.7), channel_id=1, source_target_pairs={{8,0},{9,1},{10,2},{11,3},{12,4},{13,5},{14,6},{15,7},{0,8},{1,9},... | collective-permute-start | bytes 811016 | tf_op jit(solution)/shard_map/ppermute | solution.py:341
  106.0 11.0 %collective-permute-start = (bf16[528,256]{1,0:T(8,128)(2,1)S(1)}, bf16[528,256]{1,0:T(8,128)(2,1)S(1)}, u32[]{:S(2)}, u32[]{:S(2)}) collective-permute-start(bf16[528,256]{1,0:T(8,128)(2,1)S(1)} %copy-done.7), channel_id=1, source_target_pairs={{12,0},{13,1},{14,2},{15,3},{0,4},{1,5},{2,6},{3,7},{4,8},{5,9},{6... | collective-permute-start | bytes 811016 | tf_op jit(solution)/shard_map/ppermute | solution.py:341
  111.4 10.4 %copy-start.8 = (bf16[528,256]{1,0:T(8,128)(2,1)}, bf16[528,256]{1,0:T(8,128)(2,1)S(1)}, u32[]{:S(2)}) copy-start(bf16[528,256]{1,0:T(8,128)(2,1)S(1)} %collective-permute-done.2.refs_3_) | copy-start | bytes 811012
  118.3 2.8 %collective-permute-start.3 = (bf16[512,256]{1,0:T(8,128)(2,1)S(1)}, bf16[512,256]{1,0:T(8,128)(2,1)S(1)}, u32[]{:S(2)}, u32[]{:S(2)}) collective-permute-start(bf16[512,256]{1,0:T(8,128)(2,1)S(1)} %shard_map.96), channel_id=1, source_target_pairs={{0,16},{32,48},{64,80},{96,112},{128,144},{160,176},{192,208},{224... | collective-permute-start | bytes 786440 | tf_op jit(solution)/shard_map/ppermute | solution.py:319
  121.2 6.8 %collective-permute-start.4 = (bf16[512,256]{1,0:T(8,128)(2,1)S(1)}, bf16[512,256]{1,0:T(8,128)(2,1)S(1)}, u32[]{:S(2)}, u32[]{:S(2)}) collective-permute-start(bf16[512,256]{1,0:T(8,128)(2,1)S(1)} %add.9), channel_id=1, source_target_pairs={{16,48},{80,112},{144,176},{208,240},{272,304},{336,368},{400,432}... | collective-permute-start | bytes 786440 | tf_op jit(solution)/shard_map/ppermute | solution.py:319
  127.9 33.6 %copy-start = (bf16[1,512,256]{2,1,0:T(8,128)(2,1)S(1)}, bf16[1,512,256]{2,1,0:T(8,128)(2,1)}, u32[]{:S(2)}) copy-start(bf16[1,512,256]{2,1,0:T(8,128)(2,1)} %param.8) | copy-start | bytes 786436
  127.9 33.6 %copy-start.1 = (s32[32,512]{1,0:T(8,128)S(1)}, s32[32,512]{1,0:T(8,128)}, u32[]{:S(2)}) copy-start(s32[32,512]{1,0:T(8,128)} %segments_ref.3) | copy-start | bytes 196612
  140.0 21.5 %all-to-all-start.1 = ((bf16[4,512,256]{2,1,0:T(8,128)(2,1)}), bf16[4,512,256]{2,1,0:T(8,128)(2,1)S(1)}, u32[]{:S(2)}, u32[]{:S(2)}) async-start(bf16[4,512,256]{2,1,0:T(8,128)(2,1)} %get-tuple-element.34), calls=%async_computation.1 | async-start | bytes 2097152 | tf_op jit(solution)/shard_map/all_to_all | solution.py:333
  143.5 0.7 collective-permute-start.5
  144.3 17.2 %collective-permute-start.8 = (bf16[512,256]{1,0:T(8,128)(2,1)S(1)}, bf16[512,256]{1,0:T(8,128)(2,1)S(1)}, u32[]{:S(2)}, u32[]{:S(2)}) collective-permute-start(bf16[512,256]{1,0:T(8,128)(2,1)S(1)} %add.11.refs_0_), channel_id=1, source_target_pairs={{112,496},{113,497},{114,498},{115,499},{116,500},{117,501},{118,5... | collective-permute-start | bytes 786440 | tf_op jit(solution)/shard_map/ppermute | solution.py:319
  145.0 16.5 %collective-permute-start.7 = (bf16[512,256]{1,0:T(8,128)(2,1)S(1)}, bf16[512,256]{1,0:T(8,128)(2,1)S(1)}, u32[]{:S(2)}, u32[]{:S(2)}) collective-permute-start(bf16[512,256]{1,0:T(8,128)(2,1)S(1)} %add.11.refs_0_), channel_id=1, source_target_pairs={{240,496},{241,497},{242,498},{243,499},{244,500},{245,501},{246,5... | collective-permute-start | bytes 786440 | tf_op jit(solution)/shard_map/ppermute | solution.py:319
  145.7 15.8 %collective-permute-start.6 = (bf16[512,256]{1,0:T(8,128)(2,1)S(1)}, bf16[512,256]{1,0:T(8,128)(2,1)S(1)}, u32[]{:S(2)}, u32[]{:S(2)}) collective-permute-start(bf16[512,256]{1,0:T(8,128)(2,1)S(1)} %add.11.refs_0_), channel_id=1, source_target_pairs={{368,496},{369,497},{370,498},{371,499},{372,500},{373,501},{374,5... | collective-permute-start | bytes 786440 | tf_op jit(solution)/shard_map/ppermute | solution.py:319
  164.3 21.6 %collective-permute-start.12 = (bf16[512,256]{1,0:T(8,128)(2,1)S(1)}, bf16[512,256]{1,0:T(8,128)(2,1)S(1)}, u32[]{:S(2)}, u32[]{:S(2)}) collective-permute-start(bf16[512,256]{1,0:T(8,128)(2,1)S(1)} %get-tuple-element.44), channel_id=1, source_target_pairs={{500,0},{501,1},{502,2},{503,3},{504,4},{505,5},{506,6},{507,7},{5... | collective-permute-start | bytes 786440 | tf_op jit(solution)/shard_map/ppermute | solution.py:362
  166.2 23.7 %collective-permute-start.11 = (bf16[512,256]{1,0:T(8,128)(2,1)S(1)}, bf16[512,256]{1,0:T(8,128)(2,1)S(1)}, u32[]{:S(2)}, u32[]{:S(2)}) collective-permute-start(bf16[512,256]{1,0:T(8,128)(2,1)S(1)} %get-tuple-element.44), channel_id=1, source_target_pairs={{504,0},{505,1},{506,2},{507,3},{508,4},{509,5},{510,6},{511,7},{4... | collective-permute-start | bytes 786440 | tf_op jit(solution)/shard_map/ppermute | solution.py:362
  170.9 21.1 %collective-permute-start.10 = (bf16[512,256]{1,0:T(8,128)(2,1)S(1)}, bf16[512,256]{1,0:T(8,128)(2,1)S(1)}, u32[]{:S(2)}, u32[]{:S(2)}) collective-permute-start(bf16[512,256]{1,0:T(8,128)(2,1)S(1)} %get-tuple-element.44), channel_id=1, source_target_pairs={{508,0},{509,1},{510,2},{511,3},{496,4},{497,5},{498,6},{499,7},{5... | collective-permute-start | bytes 786440 | tf_op jit(solution)/shard_map/ppermute | solution.py:362
  175.9 18.9 %collective-permute-start.9 = (bf16[512,256]{1,0:T(8,128)(2,1)S(1)}, bf16[512,256]{1,0:T(8,128)(2,1)S(1)}, u32[]{:S(2)}, u32[]{:S(2)}) collective-permute-start(bf16[512,256]{1,0:T(8,128)(2,1)S(1)} %get-tuple-element.44), channel_id=1, source_target_pairs={{496,0},{497,1},{498,2},{499,3},{500,4},{501,5},{502,6},{503,7},{5... | collective-permute-start | bytes 786440 | tf_op jit(solution)/shard_map/ppermute | solution.py:362
  185.9 8.9 %copy-start.11 = (bf16[512,256]{1,0:T(8,128)(2,1)}, bf16[512,256]{1,0:T(8,128)(2,1)S(1)}, u32[]{:S(2)}) copy-start(bf16[512,256]{1,0:T(8,128)(2,1)S(1)} %collective-permute-done.12.refs_3_) | copy-start | bytes 786436
  202.3 31.9 %copy-start.3 = (bf16[512,256]{1,0:T(8,128)(2,1)S(1)}, bf16[512,256]{1,0:T(8,128)(2,1)}, u32[]{:S(2)}) copy-start(bf16[512,256]{1,0:T(8,128)(2,1)} %copy-done.2) | copy-start | bytes 786436
  214.5 19.7 %all-to-all-start.3 = ((bf16[4,512,256]{2,1,0:T(8,128)(2,1)}), bf16[4,512,256]{2,1,0:T(8,128)(2,1)S(1)}, u32[]{:S(2)}, u32[]{:S(2)}) async-start(bf16[4,512,256]{2,1,0:T(8,128)(2,1)} %get-tuple-element.46), calls=%async_computation.3 | async-start | bytes 2097152 | tf_op jit(solution)/shard_map/all_to_all | solution.py:333
  (6 other events, 23.0 us)

commit v3 on v1

v3 whole, which is shorter than its diff:
```python
import functools

import jax
import jax.numpy as jnp
from jax import lax
from jax.experimental import pallas as pl
from jax.experimental.pallas import tpu as pltpu
from jax.sharding import PartitionSpec as P

D = 4096
HEAD_DIM = 128
SIDE = 4
BLOCK = 256
KV_ROWS = 64
TOKENS = 512
HALF = 256
ROW_MAX = 128
HOST_ROWS = 2
SLOTS = 32
SENT_ROWS = TOKENS + 2 * KV_ROWS + 16
AXES = ("section", "tensor")
norm_eps = 1e-05
masked_score = -1e30
f32, bf16 = jnp.float32, jnp.bfloat16
VMEM = pl.BlockSpec(memory_space=pltpu.VMEM)
ANY = pl.BlockSpec(memory_space=pl.ANY)
SMEM = pl.BlockSpec(memory_space=pltpu.SMEM)
NT = (((1,), (1,)), ((), ()))


def place(section, first, second):
    return SIDE * first + second if section % 2 == 0 else SIDE * second + first


def rings(sections, along_a):
    groups = []
    for s in range(sections):
        for i in range(SIDE):
            ring = [(place(s, j, i) if along_a else place(s, i, j)) for j in range(SIDE)]
            groups.append([s * SIDE * SIDE + t for t in ring])
    return groups


def head_rings(sections):
    return [[(s * SIDE + g) * SIDE + i for i in range(SIDE)] for s in range(sections) for g in range(SIDE)]


def call(body, out_shape, operands, specs, flops, moved, **more):
    return pl.pallas_call(
        body,
        out_shape=out_shape,
        in_specs=specs,
        out_specs=jax.tree.map(lambda _: VMEM, out_shape),
        compiler_params=pltpu.CompilerParams(vmem_limit_bytes=12 << 20),
        cost_estimate=pl.CostEstimate(flops=flops, bytes_accessed=moved, transcendentals=0),
        **more,
    )(*operands)


def prepare_body(x_ref, gain_ref, query_ref, keyval_ref, packed_ref, own_ref, packed, own, sems):
    odd = lax.axis_index("section") % 2
    arrivals = []
    for i in range(SIDE):
        for j in range(SIDE):
            start = pl.multiple_of(jnp.where(odd == 1, SIDE * i + j, SIDE * j + i) * BLOCK, BLOCK)
            arrivals.append((query_ref.at[pl.ds(start, BLOCK)], packed.at[i, j, pl.ds(0, BLOCK)]))
            arrivals.append((keyval_ref.at[:, pl.ds(start, BLOCK)], packed.at[i, j, pl.ds(BLOCK, KV_ROWS)]))
    arrivals.append((x_ref, own.at[pl.ds(0, TOKENS)]))
    arrivals = [pltpu.make_async_copy(src, dst, sems.at[n]) for n, (src, dst) in enumerate(arrivals)]
    for copy in arrivals:
        copy.start()
    own[TOKENS:] = jnp.broadcast_to(gain_ref[...].astype(f32), (16, BLOCK)).astype(bf16)
    leaving = []
    for i in range(SIDE + 1):
        for copy in arrivals[2 * SIDE * i : 2 * SIDE * (i + 1)]:
            copy.wait()
        src, dst = (packed.at[i], packed_ref.at[i]) if i < SIDE else (own, own_ref)
        leaving.append(pltpu.make_async_copy(src, dst, sems.at[len(arrivals) + i]))
        leaving[-1].start()
    for copy in leaving:
        copy.wait()


def prepare(x, gain, w_query, w_kv):
    packed = (SIDE, SIDE, BLOCK + KV_ROWS, BLOCK)
    own = (TOKENS + 16, BLOCK)
    return pl.pallas_call(
        prepare_body,
        out_shape=(jax.ShapeDtypeStruct(packed, bf16), jax.ShapeDtypeStruct(own, bf16)),
        in_specs=[ANY, VMEM, ANY, ANY],
        out_specs=(ANY, ANY),
        scratch_shapes=[
            pltpu.VMEM(packed, bf16),
            pltpu.VMEM(own, bf16),
            pltpu.SemaphoreType.DMA((2 * SIDE * SIDE + SIDE + 2,)),
        ],
        cost_estimate=pl.CostEstimate(flops=0, bytes_accessed=6 << 20, transcendentals=0),
    )(x, gain, w_query, w_kv)


def ring_place():
    section, tensor = lax.axis_index("section"), lax.axis_index("tensor")
    return jnp.where(section % 2 == 1, tensor % SIDE, tensor // SIDE)


def project_body(is_second, *refs):
    x_refs = refs[:SIDE]
    if is_second:
        gain_ref, w_ref, out_ref, wide_ref, kv_ref = refs[SIDE:]
    else:
        w_ref, out_ref, gain_ref, wide_ref, kv_ref = refs[SIDE:]
    here = ring_place()
    ones = jnp.ones((8, BLOCK), bf16)
    squares = jnp.zeros((8, TOKENS), f32)
    origins = [(here + SIDE - d) % SIDE for d in range(SIDE)]
    for d in range(SIDE):
        cols = slice(d * BLOCK, (d + 1) * BLOCK)
        if not is_second:
            gain_ref[16 * d : 16 * (d + 1)] = x_refs[d][TOKENS:]
        part = x_refs[d][:TOKENS].astype(f32)
        wide_ref[:, cols] = (part * gain_ref[16 * d : 16 * d + 1].astype(f32)).astype(bf16)
        square = part * part
        upper = square.astype(bf16)
        lower = (square - upper.astype(f32)).astype(bf16)
        squares += lax.dot_general(ones, upper, NT, preferred_element_type=f32)
        squares += lax.dot_general(ones, lower, NT, preferred_element_type=f32)
        for b in range(SIDE):
            kv_ref[b * KV_ROWS : (b + 1) * KV_ROWS, cols] = w_ref[b, origins[d], BLOCK:]
    keyval = lax.dot_general(kv_ref[...], wide_ref[...], NT, preferred_element_type=f32).astype(bf16)
    first = squares.astype(bf16)
    second = (squares - first.astype(f32)).astype(bf16)
    stats = [first[:1, :HALF], first[:1, HALF:], second[:1, :HALF], second[:1, HALF:]]
    stats = jnp.concatenate([s.astype(f32) for s in stats] + [jnp.zeros((12, HALF), f32)], axis=0).astype(bf16)
    for b in range(SIDE):
        total = jnp.zeros((TOKENS, BLOCK), f32)
        for d in range(SIDE):
            total += jnp.dot(
                wide_ref[:, d * BLOCK : (d + 1) * BLOCK],
                w_ref[b, origins[d], :BLOCK],
                preferred_element_type=f32,
            )
        out_ref[b, :TOKENS] = total.astype(bf16)
        rows = slice(b * KV_ROWS, (b + 1) * KV_ROWS)
        out_ref[b, TOKENS : TOKENS + KV_ROWS] = keyval[rows, :HALF]
        out_ref[b, TOKENS + KV_ROWS : TOKENS + 2 * KV_ROWS] = keyval[rows, HALF:]
        out_ref[b, TOKENS + 2 * KV_ROWS :] = stats


def project(is_second, blocks, gains, weights):
    parts = jax.ShapeDtypeStruct((SIDE, SENT_ROWS, BLOCK), bf16)
    return call(
        functools.partial(project_body, is_second),
        parts if is_second else (parts, jax.ShapeDtypeStruct((16 * SIDE, BLOCK), bf16)),
        (*blocks, *gains, weights),
        [VMEM] * (SIDE + len(gains) + 1),
        2 * TOKENS * 1024 * 1280,
        6 << 20,
        scratch_shapes=[pltpu.VMEM((TOKENS, SIDE * BLOCK), bf16), pltpu.VMEM((SIDE * KV_ROWS, SIDE * BLOCK), bf16)],
    )


def down(row):
    return jnp.transpose(jnp.broadcast_to(row, (HEAD_DIM, HEAD_DIM)))


def combine_body(parts_ref, query_ref, keyval_ref):
    tail = parts_ref[0, TOKENS:].astype(f32)
    for b in range(1, SIDE):
        tail += parts_ref[b, TOKENS:].astype(f32)
    stats = tail[2 * KV_ROWS :]
    for h in range(2):
        mean = (stats[h : h + 1] + stats[2 + h : 3 + h]) / D
        scale = lax.rsqrt(mean + norm_eps)
        keyval = (tail[h * KV_ROWS : (h + 1) * KV_ROWS] * scale).astype(bf16)
        for b in range(SIDE):
            keyval_ref[b, :, h * HALF : (h + 1) * HALF] = keyval
        for q in range(2):
            start = h * HALF + q * HEAD_DIM
            rows = slice(start, start + HEAD_DIM)
            total = parts_ref[0, rows].astype(f32)
            for b in range(1, SIDE):
                total += parts_ref[b, rows].astype(f32)
            factor = down(scale[:, q * HEAD_DIM : (q + 1) * HEAD_DIM])
            query_ref[rows] = (total * jnp.concatenate([factor, factor], axis=1)).astype(bf16)


def combine(parts):
    return call(
        combine_body,
        (jax.ShapeDtypeStruct((TOKENS, BLOCK), bf16), jax.ShapeDtypeStruct((SIDE, KV_ROWS, TOKENS), bf16)),
        (parts,),
        [VMEM],
        TOKENS * BLOCK * 8,
        2 << 20,
    )


def attend_body(is_second, lengths_ref, x_ref, query_ref, keyval_ref, segments_ref, *refs):
    section = lax.axis_index("section")
    if is_second:
        (out_ref,) = refs
    else:
        *frame_refs, out_ref, sent_ref, held, sems = refs
    if is_second:
        ids = segments_ref[pl.ds(jnp.maximum(section - 1, 0), 1), :]
        spot = lax.broadcasted_iota(jnp.int32, (1, TOKENS), 1)

        def count(k, carried):
            end, slot = carried
            end = end + lengths_ref[k]
            return end, slot + (spot >= end).astype(jnp.int32)

        _, slot = lax.fori_loop(0, SLOTS, count, (jnp.int32(0), jnp.zeros((1, TOKENS), jnp.int32)))
        ids = jnp.where(section == 0, slot, ids)
    else:
        ids = segments_ref[pl.ds(section, 1), :]
    ids = ids.astype(f32)
    steps = []
    for i in range(TOKENS // HEAD_DIM):
        rows = slice(i * HEAD_DIM, (i + 1) * HEAD_DIM)
        low = max(i - 1, 0) * HEAD_DIM
        width = (i + 1) * HEAD_DIM - low
        cols = slice(low, low + width)
        own = down(ids[:, rows])
        if width > HEAD_DIM:
            own = jnp.concatenate([own, own], axis=1)
        place_r = lax.broadcasted_iota(jnp.int32, (HEAD_DIM, width), 0) + i * HEAD_DIM
        place_c = lax.broadcasted_iota(jnp.int32, (HEAD_DIM, width), 1) + low
        allowed = (own == ids[:, cols]) & (place_c <= place_r)
        keys = jnp.concatenate([keyval_ref[0, :, cols], keyval_ref[1, :, cols]], axis=0)
        for h in range(2):
            lanes = slice(h * HEAD_DIM, (h + 1) * HEAD_DIM)
            scores = jnp.dot(query_ref[rows, lanes], keys, preferred_element_type=f32) * HEAD_DIM ** (-0.5)
            steps.append((rows, cols, lanes, jnp.where(allowed, scores, masked_score)))
    for n, (rows, cols, lanes, scores) in enumerate(steps):
        grown = jnp.exp(scores - jnp.max(scores, axis=1, keepdims=True))
        weights = (grown * (1.0 / jnp.sum(grown, axis=1, keepdims=True))).astype(bf16)
        steps[n] = (rows, cols, lanes, weights)
    for rows, cols, lanes, weights in steps:
        values = jnp.concatenate([keyval_ref[2, :, cols], keyval_ref[3, :, cols]], axis=0)
        context = lax.dot_general(weights, values, NT, preferred_element_type=f32).astype(bf16)
        done = (x_ref[rows, lanes].astype(f32) + context.astype(f32)).astype(bf16)
        out_ref[rows, lanes] = done
        if not is_second:
            sent_ref[rows, lanes] = done
    if not is_second:

        @pl.when(section == lax.axis_size("section") - 1)
        def _():
            copies = [pltpu.make_async_copy(ref, held.at[n], sems.at[n]) for n, ref in enumerate(frame_refs)]
            for copy in copies:
                copy.start()
            for copy in copies:
                copy.wait()
            sent_ref[...] = functools.reduce(jnp.add, [held[n].astype(f32) for n in range(SIDE)]).astype(bf16)


def attend(is_second, lengths, x, query, keyval, segments, frames):
    made = jax.ShapeDtypeStruct((TOKENS, BLOCK), bf16)
    held = pltpu.VMEM((SIDE, TOKENS, BLOCK), bf16)
    return call(
        functools.partial(attend_body, is_second),
        made if is_second else (made, made),
        (lengths, x, query, keyval, segments, *frames),
        [SMEM] + [VMEM] * 4 + [ANY] * len(frames),
        2 * TOKENS * 256 * 128 * 4,
        1 << 20,
        scratch_shapes=[] if is_second else [held, pltpu.SemaphoreType.DMA((SIDE,))],
    )


def frame_body(ids_ref, lengths_ref, pool_ref, out_ref, total_ref):
    total_ref[...] = jnp.zeros_like(total_ref)
    section = lax.axis_index("section")
    row = lax.broadcasted_iota(jnp.int32, (TOKENS, ROW_MAX), 0)
    col = lax.broadcasted_iota(jnp.int32, (TOKENS, ROW_MAX), 1)

    def take(k, start):
        length = lengths_ref[k]
        which = ids_ref[k] - HOST_ROWS * section

        @pl.when((which >= 0) & (which < HOST_ROWS))
        def _():
            hit = ((row - start == col) & (col < length)).astype(f32).astype(bf16)
            total_ref[...] += jnp.dot(hit, pool_ref[which], preferred_element_type=f32)

        return start + length

    lax.fori_loop(0, SLOTS, take, jnp.int32(0))
    out_ref[...] = total_ref[...].astype(bf16)


def make_frame(row_ids, row_lengths, pool):
    return call(
        frame_body,
        jax.ShapeDtypeStruct((TOKENS, BLOCK), bf16),
        (row_ids, row_lengths, pool),
        [SMEM, SMEM, VMEM],
        2 * TOKENS * 128 * 256,
        1 << 20,
        scratch_shapes=[pltpu.VMEM((TOKENS, BLOCK), f32)],
    )


def bring(array, sections, step, count):
    last = sections - 1
    got = []
    for n in range(1, count + 1):
        route = [(i - n * step, i) for i in range(sections) if (last - i) % ((count + 1) * step) == 0]
        got.append(lax.ppermute(array, "section", route))
    return got


def total_of(arrays):
    total = arrays[0].astype(f32)
    for array in arrays[1:]:
        total = total + array.astype(f32)
    return total.astype(bf16)


def per_device(activations, gain, w_query, w_kv, segments, pool, row_ids, row_lengths):
    sections = lax.axis_size("section")
    ring_b, ring_y = rings(sections, False), head_rings(sections)
    barrier = lax.optimization_barrier
    grid = [(s, a, b) for s in range(sections) for a in range(SIDE) for b in range(SIDE)]

    def number(s, a, b, like):
        return s * SIDE * SIDE + place(like, a % SIDE, b)

    def exchange(array, ring):
        return lax.all_to_all(array, AXES, 0, 0, axis_index_groups=ring)

    x = activations[0]
    packed, own = prepare(x, gain, w_query[0], w_kv[0])
    weights = exchange(packed, ring_b)
    blocks = [own]
    for d in range(1, SIDE):
        route = [(number(s, a - d, b, s), number(s, a, b, s)) for s, a, b in grid]
        blocks.append(lax.ppermute(own, AXES, route))

    blocks, pool = barrier((blocks, pool))
    frame = make_frame(row_ids, row_lengths, pool)
    frame = frame + bring(frame, sections, 1, 1)[0]
    weights, frame = barrier((weights, frame))
    pieces = bring(frame, sections, 2, 3)

    parts, gains = project(False, blocks, [], weights)
    parts = exchange(parts, ring_b)
    frame = total_of([frame, *pieces])
    parts, frame = barrier((parts, frame))
    frames = [frame, *bring(frame, sections, 8, 3)]
    query, keyval = combine(parts)
    first, sent = attend(False, row_lengths, x, query, exchange(keyval, ring_y), segments, frames)

    blocks = []
    for d in range(SIDE):
        route = [(number((s - 1) % sections, a - d, b, s), number(s, a, b, s)) for s, a, b in grid]
        blocks.append(lax.ppermute(sent, AXES, route))
    query, keyval = combine(exchange(project(True, blocks, [gains], weights), ring_b))
    second = attend(True, row_lengths, blocks[0], query, exchange(keyval, ring_y), segments, [])
    return first[None], second[None]


def solution(mesh):
    return jax.shard_map(
        per_device,
        mesh=mesh,
        in_specs=(
            P("section", None, "tensor"),
            P("section", "tensor"),
            P("section", None, "tensor"),
            P("section", "tensor", None),
            P(),
            P("section", None, "tensor"),
            P(),
            P(),
        ),
        out_specs=(P("section", None, "tensor"), P("section", None, "tensor")),
        check_vma=False,
    )
```

time: 155 us -> 138 us (0.89)
  starting transfers between devices: 21.5 us -> 39.4 us
  blocking collectives: 54.4 us -> 37 us
  waiting for transfers between devices: 46.7 us -> 39.7 us
  Pallas kernels: 22.4 us -> 15.4 us
  other arithmetic: 2.94 us -> 0.21 us
    ppermute x6 -> x14, starting transfers between devices: 4.17 us -> 29.7 us  [the longest x3 12.3 us: per_device(): blocks.append(lax.ppermute(own, AXES, route))]
    all_gather x2 -> x0, blocking collectives: 24.5 us -> none  [layer(): lax.all_gather(keyval, AXES, axis=0, axis_index_groups=ring_y, tiled=True)]
    all_to_all x3 -> x2, waiting for transfers between devices: 26.3 us -> 10.2 us  [exchange(): return lax.all_to_all(array, AXES, 0, 0, axis_index_groups=ring)]
    ppermute x6 -> x14, waiting for transfers between devices: 20.4 us -> 29.4 us  [the longest x4 19 us: per_device(): blocks.append(lax.ppermute(sent, AXES, route))]
    all_to_all x3 -> x2, starting transfers between devices: 17.3 us -> 9.66 us  [exchange(): return lax.all_to_all(array, AXES, 0, 0, axis_index_groups=ring)]
    all_to_all x2 -> x3, blocking collectives: 29.8 us -> 37 us  [exchange(): return lax.all_to_all(array, AXES, 0, 0, axis_index_groups=ring)]
    pallas_call x1, Pallas kernels: 9.57 us -> 3.77 us  [prepare(): pl.pallas_call(prepare_body, out_shape=(jax.ShapeDtypeStruct(packed, bf16...]
    unnamed x18 -> x22, local copies, waits for them, and re-layouts: 3.31 us -> 4.42 us
  transfers between devices with their start and end apart: 9 -> 16, of which waited for: 3 -> 8; matrix products, arithmetic and copies ran while one was open for 0% -> 0% of each run, Pallas kernels for 11% -> 2%
where the time goes in v3:
time: 138 us; the launch traced here: 137 us
  waiting for transfers between devices  39.7 us (29%)
  starting transfers between devices  39.4 us (29%)
  blocking collectives  37 us (27%)
  Pallas kernels  15.4 us (11%)
  local copies, waits for them, and re-layouts  4.42 us (3%)
    all_to_all x3, blocking collectives, exchange(): return lax.all_to_all(array, AXES, 0, 0, axis_index_groups=ring)  37 us
    ppermute x4, waiting for transfers between devices, per_device(): blocks.append(lax.ppermute(sent, AXES, route))  19 us
    ppermute x3, starting transfers between devices, per_device(): blocks.append(lax.ppermute(own, AXES, route))  12.3 us
    ppermute x4, starting transfers between devices, per_device(): blocks.append(lax.ppermute(sent, AXES, route))  12 us
    pallas_call x7, Pallas kernels, call(): pl.pallas_call(body, out_shape=out_shape, in_specs=specs, out_specs=jax.t...  11.6 us
    all_to_all x2, waiting for transfers between devices, exchange(): return lax.all_to_all(array, AXES, 0, 0, axis_index_groups=ring)  10.2 us
    all_to_all x2, starting transfers between devices, exchange(): return lax.all_to_all(array, AXES, 0, 0, axis_index_groups=ring)  9.66 us
    ppermute x3, waiting for transfers between devices, per_device(): blocks.append(lax.ppermute(own, AXES, route))  9.32 us
  transfers between devices with their start and end apart: 16, of which 8 were waited for; matrix products, arithmetic and copies ran while one was open for 0% of the time, Pallas kernels for 2%

profile of v3, /device:TPU:6, one launch (start us, length us, event | category | flops | bytes accessed | tf_op | source)
XLA Modules:
  0.0 136.9 jit_solution(5642094588683735546)
XLA Ops:
  0.6 3.8 %shard_map.95 = (bf16[4,4,320,256]{3,2,1,0:T(8,128)(2,1)}, bf16[528,256]{1,0:T(8,128)(2,1)}) custom-call(bf16[512,256]{1,0:T(8,128)(2,1)} %bitcast.5, bf16[1,256]{1,0:T(2,128)(2,1)} %gain_ref.1, bf16[4096,256]{1,0:T(8,128)(2,1)} %bitcast.7, bf16[64,4096]{1,0:T(8,128)(2,1)} %bitcast.8), custom_call_target="tpu_custom_call" | custom-call | bytes 6291456 | tf_op jit(solution)/shard_map/pallas_call | solution.py:87
  4.5 4.6 %all-to-all-start = ((bf16[4,4,320,256]{3,2,1,0:T(8,128)(2,1)}), bf16[4,4,320,256]{3,2,1,0:T(8,128)(2,1)S(1)}, u32[]{:S(2)}, u32[]{:S(2)}) async-start(bf16[4,4,320,256]{3,2,1,0:T(8,128)(2,1)} %get-tuple-element.26), calls=%async_computation | async-start | bytes 5242880 | tf_op jit(solution)/shard_map/all_to_all | solution.py:331
  9.1 2.7 %collective-permute-start.2 = (bf16[528,256]{1,0:T(8,128)(2,1)S(1)}, bf16[528,256]{1,0:T(8,128)(2,1)S(1)}, u32[]{:S(2)}, u32[]{:S(2)}) collective-permute-start(bf16[528,256]{1,0:T(8,128)(2,1)S(1)} %copy-done.6), channel_id=1, source_target_pairs={{4,0},{5,1},{6,2},{7,3},{8,4},{9,5},{10,6},{11,7},{12,8},{13,9},{1... | collective-permute-start | bytes 811016 | tf_op jit(solution)/shard_map/ppermute | solution.py:339
  11.8 7.6 %collective-permute-start.1 = (bf16[528,256]{1,0:T(8,128)(2,1)S(1)}, bf16[528,256]{1,0:T(8,128)(2,1)S(1)}, u32[]{:S(2)}, u32[]{:S(2)}) collective-permute-start(bf16[528,256]{1,0:T(8,128)(2,1)S(1)} %copy-done.6), channel_id=1, source_target_pairs={{8,0},{9,1},{10,2},{11,3},{12,4},{13,5},{14,6},{15,7},{0,8},{1,9},... | collective-permute-start | bytes 811016 | tf_op jit(solution)/shard_map/ppermute | solution.py:339
  19.4 1.9 %collective-permute-start = (bf16[528,256]{1,0:T(8,128)(2,1)S(1)}, bf16[528,256]{1,0:T(8,128)(2,1)S(1)}, u32[]{:S(2)}, u32[]{:S(2)}) collective-permute-start(bf16[528,256]{1,0:T(8,128)(2,1)S(1)} %copy-done.6), channel_id=1, source_target_pairs={{12,0},{13,1},{14,2},{15,3},{0,4},{1,5},{2,6},{3,7},{4,8},{5,9},{6... | collective-permute-start | bytes 811016 | tf_op jit(solution)/shard_map/ppermute | solution.py:339
  21.3 2.3 %collective-permute-done.2.refs_3_ = bf16[528,256]{1,0:T(8,128)(2,1)S(1)} collective-permute-done((bf16[528,256]{1,0:T(8,128)(2,1)S(1)}, bf16[528,256]{1,0:T(8,128)(2,1)S(1)}, u32[]{:S(2)}, u32[]{:S(2)}) %collective-permute-start.2) | collective-permute-done | bytes 270368 | tf_op jit(solution)/shard_map/ppermute | solution.py:339
  23.6 7.0 %collective-permute-done.1.refs_2_ = bf16[528,256]{1,0:T(8,128)(2,1)S(1)} collective-permute-done((bf16[528,256]{1,0:T(8,128)(2,1)S(1)}, bf16[528,256]{1,0:T(8,128)(2,1)S(1)}, u32[]{:S(2)}, u32[]{:S(2)}) %collective-permute-start.1) | collective-permute-done | bytes 270368 | tf_op jit(solution)/shard_map/ppermute | solution.py:339
  37.8 2.1 %shard_map.97 = (bf16[4,656,256]{2,1,0:T(8,128)(2,1)S(1)}, bf16[64,256]{1,0:T(8,128)(2,1)S(1)}) custom-call(bf16[528,256]{1,0:T(8,128)(2,1)S(1)} %copy-done.6, bf16[528,256]{1,0:T(8,128)(2,1)S(1)} %copy-done.10, bf16[528,256]{1,0:T(8,128)(2,1)S(1)} %copy-done.8, bf16[528,256]{1,0:T(8,128)(2,1)S(1)} %collective-permute-done.2.refs_3_, ...), custom_call_target="tpu_custom_call" | custom-call | flops 1342177280 | bytes 6291456 | tf_op jit(solution)/shard_map/pallas_call | solution.py:49
  41.1 5.1 %all-to-all-start.1 = ((bf16[4,656,256]{2,1,0:T(8,128)(2,1)}), bf16[4,656,256]{2,1,0:T(8,128)(2,1)}, u32[]{:S(2)}, u32[]{:S(2)}) async-start(bf16[4,656,256]{2,1,0:T(8,128)(2,1)} %copy-done), calls=%async_computation.1 | async-start | bytes 2686976 | tf_op jit(solution)/shard_map/all_to_all | solution.py:331
  48.5 10.2 %all-to-all-done.1.parts_ref = bf16[4,656,256]{2,1,0:T(8,128)(2,1)} async-done(((bf16[4,656,256]{2,1,0:T(8,128)(2,1)}), bf16[4,656,256]{2,1,0:T(8,128)(2,1)}, u32[]{:S(2)}, u32[]{:S(2)}) %all-to-all-start.1) | async-done | bytes 1343520 | tf_op jit(solution)/shard_map/all_to_all | solution.py:331
  60.7 1.5 %shard_map.98 = (bf16[512,256]{1,0:T(8,128)(2,1)S(1)}, bf16[4,64,512]{2,1,0:T(8,128)(2,1)S(1)}) custom-call(bf16[4,656,256]{2,1,0:T(8,128)(2,1)} %all-to-all-done.1.parts_ref), custom_call_target="tpu_custom_call" | custom-call | flops 1048576 | bytes 2097152 | tf_op jit(solution)/shard_map/pallas_call | solution.py:49
  62.3 9.4 %all_to_all.25.keyval_ref = bf16[4,64,512]{2,1,0:T(8,128)(2,1)S(1)} all-to-all(bf16[4,64,512]{2,1,0:T(8,128)(2,1)S(1)} %get-tuple-element.33), channel_id=1, replica_groups={{0,1,2,3},{4,5,6,7},{8,9,10,11},{12,13,14,15},{16,17,18,19},{20,21,22,2..., dimensions={0} | all-to-all | bytes 524288 | tf_op jit(solution)/shard_map/all_to_all | solution.py:331
  71.7 2.0 %shard_map.99 = (bf16[512,256]{1,0:T(8,128)(2,1)}, bf16[512,256]{1,0:T(8,128)(2,1)S(1)}) custom-call(s32[32]{0:T(128)S(1)} %copy-done.4, bf16[512,256]{1,0:T(8,128)(2,1)S(1)} %bitcast.6, bf16[512,256]{1,0:T(8,128)(2,1)S(1)} %get-tuple-element.32.query_ref, bf16[4,64,512]{2,1,0:T(8,128)(2,1)S(1)} %all_to_all.25.keyval_ref, s32[32,512]{1,0:T(8,128)S(1)} %copy-done.2, ...), custom_call_target="tpu_custom_call" | custom-call | flops 134217728 | bytes 1048576 | tf_op jit(solution)/shard_map/pallas_call | solution.py:49
  73.7 1.9 %collective-permute-start.13 = (bf16[512,256]{1,0:T(8,128)(2,1)S(1)}, bf16[512,256]{1,0:T(8,128)(2,1)S(1)}, u32[]{:S(2)}, u32[]{:S(2)}) collective-permute-start(bf16[512,256]{1,0:T(8,128)(2,1)S(1)} %get-tuple-element.36), channel_id=1, source_target_pairs={{500,0},{501,1},{502,2},{503,3},{504,4},{505,5},{506,6},{507,7},{5... | collective-permute-start | bytes 786440 | tf_op jit(solution)/shard_map/ppermute | solution.py:358
  75.7 4.3 %collective-permute-start.12 = (bf16[512,256]{1,0:T(8,128)(2,1)S(1)}, bf16[512,256]{1,0:T(8,128)(2,1)S(1)}, u32[]{:S(2)}, u32[]{:S(2)}) collective-permute-start(bf16[512,256]{1,0:T(8,128)(2,1)S(1)} %get-tuple-element.36), channel_id=1, source_target_pairs={{504,0},{505,1},{506,2},{507,3},{508,4},{509,5},{510,6},{511,7},{4... | collective-permute-start | bytes 786440 | tf_op jit(solution)/shard_map/ppermute | solution.py:358
  80.0 4.5 %collective-permute-start.11 = (bf16[512,256]{1,0:T(8,128)(2,1)S(1)}, bf16[512,256]{1,0:T(8,128)(2,1)S(1)}, u32[]{:S(2)}, u32[]{:S(2)}) collective-permute-start(bf16[512,256]{1,0:T(8,128)(2,1)S(1)} %get-tuple-element.36), channel_id=1, source_target_pairs={{508,0},{509,1},{510,2},{511,3},{496,4},{497,5},{498,6},{499,7},{5... | collective-permute-start | bytes 786440 | tf_op jit(solution)/shard_map/ppermute | solution.py:358
  85.8 10.1 %collective-permute-done.13.refs_3_ = bf16[512,256]{1,0:T(8,128)(2,1)S(1)} collective-permute-done((bf16[512,256]{1,0:T(8,128)(2,1)S(1)}, bf16[512,256]{1,0:T(8,128)(2,1)S(1)}, u32[]{:S(2)}, u32[]{:S(2)}) %collective-permute-start.13) | collective-permute-done | bytes 262176 | tf_op jit(solution)/shard_map/ppermute | solution.py:358
  95.9 3.9 %collective-permute-done.12.refs_2_ = bf16[512,256]{1,0:T(8,128)(2,1)S(1)} collective-permute-done((bf16[512,256]{1,0:T(8,128)(2,1)S(1)}, bf16[512,256]{1,0:T(8,128)(2,1)S(1)}, u32[]{:S(2)}, u32[]{:S(2)}) %collective-permute-start.12) | collective-permute-done | bytes 262176 | tf_op jit(solution)/shard_map/ppermute | solution.py:358
  99.8 2.3 %collective-permute-done.11.refs_1_ = bf16[512,256]{1,0:T(8,128)(2,1)S(1)} collective-permute-done((bf16[512,256]{1,0:T(8,128)(2,1)S(1)}, bf16[512,256]{1,0:T(8,128)(2,1)S(1)}, u32[]{:S(2)}, u32[]{:S(2)}) %collective-permute-start.11) | collective-permute-done | bytes 262176 | tf_op jit(solution)/shard_map/ppermute | solution.py:358
  102.1 2.6 %collective-permute-done.10.refs_0_.x_ref = bf16[512,256]{1,0:T(8,128)(2,1)S(1)} collective-permute-done((bf16[512,256]{1,0:T(8,128)(2,1)S(1)}, bf16[512,256]{1,0:T(8,128)(2,1)S(1)}, u32[]{:S(2)}, u32[]{:S(2)}) %collective-permute-start.10) | collective-permute-done | bytes 262176 | tf_op jit(solution)/shard_map/ppermute | solution.py:358
  104.7 2.1 %shard_map.100 = bf16[4,656,256]{2,1,0:T(8,128)(2,1)S(1)} custom-call(bf16[512,256]{1,0:T(8,128)(2,1)S(1)} %collective-permute-done.10.refs_0_.x_ref, bf16[512,256]{1,0:T(8,128)(2,1)S(1)} %collective-permute-done.11.refs_1_, bf16[512,256]{1,0:T(8,128)(2,1)S(1)} %collective-permute-done.12.refs_2_, bf16[512,256]{1,0:T(8,128)(2,1)S(1)} %collective-permute-done.13.refs_3_, ...), custom_call_target="tpu_custom_call" | custom-call | flops 1342177280 | bytes 6291456 | tf_op jit(solution)/shard_map/pallas_call | solution.py:49
  106.9 18.5 %all_to_all.26.parts_ref = bf16[4,656,256]{2,1,0:T(8,128)(2,1)S(1)} all-to-all(bf16[4,656,256]{2,1,0:T(8,128)(2,1)S(1)} %shard_map.100), channel_id=1, replica_groups={{0,1,2,3},{4,5,6,7},{8,9,10,11},{12,13,14,15},{16,20,24,28},{17,21,25,2..., dimensions={0} | all-to-all | bytes 2686976 | tf_op jit(solution)/shard_map/all_to_all | solution.py:331
  125.6 9.1 %all_to_all.27.keyval_ref = bf16[4,64,512]{2,1,0:T(8,128)(2,1)S(1)} all-to-all(bf16[4,64,512]{2,1,0:T(8,128)(2,1)S(1)} %get-tuple-element.39), channel_id=1, replica_groups={{0,1,2,3},{4,5,6,7},{8,9,10,11},{12,13,14,15},{16,17,18,19},{20,21,22,2..., dimensions={0} | all-to-all | bytes 524288 | tf_op jit(solution)/shard_map/all_to_all | solution.py:331
  134.7 2.2 %shard_map.102 = bf16[512,256]{1,0:T(8,128)(2,1)} custom-call(s32[32]{0:T(128)S(1)} %copy-done.4, bf16[512,256]{1,0:T(8,128)(2,1)S(1)} %collective-permute-done.10.refs_0_.x_ref, bf16[512,256]{1,0:T(8,128)(2,1)S(1)} %get-tuple-element.38.query_ref, bf16[4,64,512]{2,1,0:T(8,128)(2,1)S(1)} %all_to_all.27.keyval_ref, s32[32,512]{1,0:T(8,128)S(1)} %copy-done.2), custom_call_target="tpu_custom_call" | custom-call | flops 134217728 | bytes 1048576 | tf_op jit(solution)/shard_map/pallas_call | solution.py:49
  (43 shorter events, 14.0 us)
Async XLA Ops:
  4.4 4.7 %copy-start.6 = (bf16[528,256]{1,0:T(8,128)(2,1)S(1)}, bf16[528,256]{1,0:T(8,128)(2,1)}, u32[]{:S(2)}) copy-start(bf16[528,256]{1,0:T(8,128)(2,1)} %get-tuple-element.22.refs_0_) | copy-start | bytes 811012
  4.4 27.7 %copy-start.3 = (bf16[2,128,256]{2,1,0:T(8,128)(2,1)S(1)}, bf16[2,128,256]{2,1,0:T(8,128)(2,1)}, u32[]{:S(2)}) copy-start(bf16[2,128,256]{2,1,0:T(8,128)(2,1)} %pool_ref) | copy-start | bytes 393220
  4.4 27.7 %copy-start.4 = (s32[32]{0:T(128)S(1)}, s32[32]{0:T(128)}, u32[]{:S(2)}) copy-start(s32[32]{0:T(128)} %lengths_ref.5) | copy-start | bytes 388
  4.4 27.7 %copy-start.5 = (s32[32]{0:T(128)S(1)}, s32[32]{0:T(128)}, u32[]{:S(2)}) copy-start(s32[32]{0:T(128)} %ids_ref.1) | copy-start | bytes 388
  4.5 31.5 %all-to-all-start = ((bf16[4,4,320,256]{3,2,1,0:T(8,128)(2,1)}), bf16[4,4,320,256]{3,2,1,0:T(8,128)(2,1)S(1)}, u32[]{:S(2)}, u32[]{:S(2)}) async-start(bf16[4,4,320,256]{3,2,1,0:T(8,128)(2,1)} %get-tuple-element.26), calls=%async_computation | async-start | bytes 5242880 | tf_op jit(solution)/shard_map/all_to_all | solution.py:331
  9.1 14.6 %collective-permute-start.2 = (bf16[528,256]{1,0:T(8,128)(2,1)S(1)}, bf16[528,256]{1,0:T(8,128)(2,1)S(1)}, u32[]{:S(2)}, u32[]{:S(2)}) collective-permute-start(bf16[528,256]{1,0:T(8,128)(2,1)S(1)} %copy-done.6), channel_id=1, source_target_pairs={{4,0},{5,1},{6,2},{7,3},{8,4},{9,5},{10,6},{11,7},{12,8},{13,9},{1... | collective-permute-start | bytes 811016 | tf_op jit(solution)/shard_map/ppermute | solution.py:339
  11.8 18.9 %collective-permute-start.1 = (bf16[528,256]{1,0:T(8,128)(2,1)S(1)}, bf16[528,256]{1,0:T(8,128)(2,1)S(1)}, u32[]{:S(2)}, u32[]{:S(2)}) collective-permute-start(bf16[528,256]{1,0:T(8,128)(2,1)S(1)} %copy-done.6), channel_id=1, source_target_pairs={{8,0},{9,1},{10,2},{11,3},{12,4},{13,5},{14,6},{15,7},{0,8},{1,9},... | collective-permute-start | bytes 811016 | tf_op jit(solution)/shard_map/ppermute | solution.py:339
  19.4 12.0 %collective-permute-start = (bf16[528,256]{1,0:T(8,128)(2,1)S(1)}, bf16[528,256]{1,0:T(8,128)(2,1)S(1)}, u32[]{:S(2)}, u32[]{:S(2)}) collective-permute-start(bf16[528,256]{1,0:T(8,128)(2,1)S(1)} %copy-done.6), channel_id=1, source_target_pairs={{12,0},{13,1},{14,2},{15,3},{0,4},{1,5},{2,6},{3,7},{4,8},{5,9},{6... | collective-permute-start | bytes 811016 | tf_op jit(solution)/shard_map/ppermute | solution.py:339
  33.4 2.4 %collective-permute-start.3 = (bf16[512,256]{1,0:T(8,128)(2,1)S(1)}, bf16[512,256]{1,0:T(8,128)(2,1)S(1)}, u32[]{:S(2)}, u32[]{:S(2)}) collective-permute-start(bf16[512,256]{1,0:T(8,128)(2,1)S(1)} %shard_map.96), channel_id=1, source_target_pairs={{0,16},{32,48},{64,80},{96,112},{128,144},{160,176},{192,208},{224... | collective-permute-start | bytes 786440 | tf_op jit(solution)/shard_map/ppermute | solution.py:310
  35.9 1.0 copy-start.8
  40.0 1.1 copy-start
  41.1 17.6 %all-to-all-start.1 = ((bf16[4,656,256]{2,1,0:T(8,128)(2,1)}), bf16[4,656,256]{2,1,0:T(8,128)(2,1)}, u32[]{:S(2)}, u32[]{:S(2)}) async-start(bf16[4,656,256]{2,1,0:T(8,128)(2,1)} %copy-done), calls=%async_computation.1 | async-start | bytes 2686976 | tf_op jit(solution)/shard_map/all_to_all | solution.py:331
  46.1 25.6 %copy-start.1 = (bf16[1,512,256]{2,1,0:T(8,128)(2,1)S(1)}, bf16[1,512,256]{2,1,0:T(8,128)(2,1)}, u32[]{:S(2)}) copy-start(bf16[1,512,256]{2,1,0:T(8,128)(2,1)} %param.8) | copy-start | bytes 786436
  46.1 25.6 %copy-start.2 = (s32[32,512]{1,0:T(8,128)S(1)}, s32[32,512]{1,0:T(8,128)}, u32[]{:S(2)}) copy-start(s32[32,512]{1,0:T(8,128)} %segments_ref.3) | copy-start | bytes 196612
  46.1 2.2 %collective-permute-start.6 = (bf16[512,256]{1,0:T(8,128)(2,1)S(1)}, bf16[512,256]{1,0:T(8,128)(2,1)S(1)}, u32[]{:S(2)}, u32[]{:S(2)}) collective-permute-start(bf16[512,256]{1,0:T(8,128)(2,1)S(1)} %add.12), channel_id=1, source_target_pairs={{16,112},{144,240},{272,368},{400,496},{17,113},{145,241},{273,369... | collective-permute-start | bytes 786440 | tf_op jit(solution)/shard_map/ppermute | solution.py:310
  46.9 1.4 %collective-permute-start.5 = (bf16[512,256]{1,0:T(8,128)(2,1)S(1)}, bf16[512,256]{1,0:T(8,128)(2,1)S(1)}, u32[]{:S(2)}, u32[]{:S(2)}) collective-permute-start(bf16[512,256]{1,0:T(8,128)(2,1)S(1)} %add.12), channel_id=1, source_target_pairs={{48,112},{176,240},{304,368},{432,496},{49,113},{177,241},{305,369... | collective-permute-start | bytes 786440 | tf_op jit(solution)/shard_map/ppermute | solution.py:310
  47.6 0.7 collective-permute-start.4
  58.7 13.0 %collective-permute-start.9 = (bf16[512,256]{1,0:T(8,128)(2,1)S(1)}, bf16[512,256]{1,0:T(8,128)(2,1)S(1)}, u32[]{:S(2)}, u32[]{:S(2)}) collective-permute-start(bf16[512,256]{1,0:T(8,128)(2,1)S(1)} %add_convert_fusion.refs_0_), channel_id=1, source_target_pairs={{112,496},{113,497},{114,498},{115,499},{116,500},{117,501},{118,5... | collective-permute-start | bytes 786440 | tf_op jit(solution)/shard_map/ppermute | solution.py:310
  59.4 12.3 %collective-permute-start.8 = (bf16[512,256]{1,0:T(8,128)(2,1)S(1)}, bf16[512,256]{1,0:T(8,128)(2,1)S(1)}, u32[]{:S(2)}, u32[]{:S(2)}) collective-permute-start(bf16[512,256]{1,0:T(8,128)(2,1)S(1)} %add_convert_fusion.refs_0_), channel_id=1, source_target_pairs={{240,496},{241,497},{242,498},{243,499},{244,500},{245,501},{246,5... | collective-permute-start | bytes 786440 | tf_op jit(solution)/shard_map/ppermute | solution.py:310
  60.0 11.6 %collective-permute-start.7 = (bf16[512,256]{1,0:T(8,128)(2,1)S(1)}, bf16[512,256]{1,0:T(8,128)(2,1)S(1)}, u32[]{:S(2)}, u32[]{:S(2)}) collective-permute-start(bf16[512,256]{1,0:T(8,128)(2,1)S(1)} %add_convert_fusion.refs_0_), channel_id=1, source_target_pairs={{368,496},{369,497},{370,498},{371,499},{372,500},{373,501},{374,5... | collective-permute-start | bytes 786440 | tf_op jit(solution)/shard_map/ppermute | solution.py:310
  73.7 22.1 %collective-permute-start.13 = (bf16[512,256]{1,0:T(8,128)(2,1)S(1)}, bf16[512,256]{1,0:T(8,128)(2,1)S(1)}, u32[]{:S(2)}, u32[]{:S(2)}) collective-permute-start(bf16[512,256]{1,0:T(8,128)(2,1)S(1)} %get-tuple-element.36), channel_id=1, source_target_pairs={{500,0},{501,1},{502,2},{503,3},{504,4},{505,5},{506,6},{507,7},{5... | collective-permute-start | bytes 786440 | tf_op jit(solution)/shard_map/ppermute | solution.py:358
  75.7 24.1 %collective-permute-start.12 = (bf16[512,256]{1,0:T(8,128)(2,1)S(1)}, bf16[512,256]{1,0:T(8,128)(2,1)S(1)}, u32[]{:S(2)}, u32[]{:S(2)}) collective-permute-start(bf16[512,256]{1,0:T(8,128)(2,1)S(1)} %get-tuple-element.36), channel_id=1, source_target_pairs={{504,0},{505,1},{506,2},{507,3},{508,4},{509,5},{510,6},{511,7},{4... | collective-permute-start | bytes 786440 | tf_op jit(solution)/shard_map/ppermute | solution.py:358
  80.0 22.1 %collective-permute-start.11 = (bf16[512,256]{1,0:T(8,128)(2,1)S(1)}, bf16[512,256]{1,0:T(8,128)(2,1)S(1)}, u32[]{:S(2)}, u32[]{:S(2)}) collective-permute-start(bf16[512,256]{1,0:T(8,128)(2,1)S(1)} %get-tuple-element.36), channel_id=1, source_target_pairs={{508,0},{509,1},{510,2},{511,3},{496,4},{497,5},{498,6},{499,7},{5... | collective-permute-start | bytes 786440 | tf_op jit(solution)/shard_map/ppermute | solution.py:358
  84.5 20.2 %collective-permute-start.10 = (bf16[512,256]{1,0:T(8,128)(2,1)S(1)}, bf16[512,256]{1,0:T(8,128)(2,1)S(1)}, u32[]{:S(2)}, u32[]{:S(2)}) collective-permute-start(bf16[512,256]{1,0:T(8,128)(2,1)S(1)} %get-tuple-element.36), channel_id=1, source_target_pairs={{496,0},{497,1},{498,2},{499,3},{500,4},{501,5},{502,6},{503,7},{5... | collective-permute-start | bytes 786440 | tf_op jit(solution)/shard_map/ppermute | solution.py:358
  (3 other events, 2.4 us)

commit v4 on v3

--- a/solution.py
+++ b/solution.py
@@ -108,7 +108,11 @@
     if is_second:
         gain_ref, w_ref, out_ref, wide_ref, kv_ref = refs[SIDE:]
     else:
-        w_ref, out_ref, gain_ref, wide_ref, kv_ref = refs[SIDE:]
+        w_ref, out_ref, gain_ref, wide_ref, kv_ref, held, sems = refs[SIDE:]
+        copies = [pltpu.make_async_copy(ref, held.at[d], sems.at[d]) for d, ref in enumerate(x_refs)]
+        for copy in copies:
+            copy.start()
+        x_refs = [held.at[d] for d in range(SIDE)]
     here = ring_place()
     ones = jnp.ones((8, BLOCK), bf16)
     squares = jnp.zeros((8, TOKENS), f32)
@@ -116,6 +120,7 @@
     for d in range(SIDE):
         cols = slice(d * BLOCK, (d + 1) * BLOCK)
         if not is_second:
+            copies[d].wait()
             gain_ref[16 * d : 16 * (d + 1)] = x_refs[d][TOKENS:]
         part = x_refs[d][:TOKENS].astype(f32)
         wide_ref[:, cols] = (part * gain_ref[16 * d : 16 * d + 1].astype(f32)).astype(bf16)
@@ -152,10 +157,14 @@
         functools.partial(project_body, is_second),
         parts if is_second else (parts, jax.ShapeDtypeStruct((16 * SIDE, BLOCK), bf16)),
         (*blocks, *gains, weights),
-        [VMEM] * (SIDE + len(gains) + 1),
+        [VMEM if is_second else ANY] * SIDE + [VMEM] * (len(gains) + 1),
         2 * TOKENS * 1024 * 1280,
         6 << 20,
-        scratch_shapes=[pltpu.VMEM((TOKENS, SIDE * BLOCK), bf16), pltpu.VMEM((SIDE * KV_ROWS, SIDE * BLOCK), bf16)],
+        scratch_shapes=[
+            pltpu.VMEM((TOKENS, SIDE * BLOCK), bf16),
+            pltpu.VMEM((SIDE * KV_ROWS, SIDE * BLOCK), bf16),
+            *([] if is_second else [pltpu.VMEM((SIDE, *blocks[0].shape), bf16), pltpu.SemaphoreType.DMA((SIDE,))]),
+        ],
     )
 
 
@@ -338,18 +347,19 @@
         route = [(number(s, a - d, b, s), number(s, a, b, s)) for s, a, b in grid]
         blocks.append(lax.ppermute(own, AXES, route))
 
-    blocks, pool = barrier((blocks, pool))
     frame = make_frame(row_ids, row_lengths, pool)
-    frame = frame + bring(frame, sections, 1, 1)[0]
-    weights, frame = barrier((weights, frame))
+    piece = bring(frame, sections, 1, 1)[0]
+    blocks[SIDE - 1], piece = barrier((blocks[SIDE - 1], piece))
+    frame = frame + piece
     pieces = bring(frame, sections, 2, 3)
+    weights, pieces = barrier((weights, pieces))
+    frame = total_of([frame, *pieces])
+    frames = [frame, *bring(frame, sections, 8, 3)]
 
     parts, gains = project(False, blocks, [], weights)
     parts = exchange(parts, ring_b)
-    frame = total_of([frame, *pieces])
-    parts, frame = barrier((parts, frame))
-    frames = [frame, *bring(frame, sections, 8, 3)]
     query, keyval = combine(parts)
+    keyval, frames = barrier((keyval, frames))
     first, sent = attend(False, row_lengths, x, query, exchange(keyval, ring_y), segments, frames)
 
     blocks = []

time: 138 us -> 129 us (0.935)
  waiting for transfers between devices: 39.7 us -> 32.2 us
  local copies, waits for them, and re-layouts: 4.42 us -> 2.49 us
  blocking collectives: 37 us -> 35.5 us
    ppermute x3, waiting for transfers between devices: 9.32 us -> 0.01 us  [per_device(): blocks.append(lax.ppermute(own, AXES, route))]
    ppermute x7, starting transfers between devices: 5.48 us -> 9.54 us  [bring(): got.append(lax.ppermute(array, 'section', route))]
    all_to_all x2, waiting for transfers between devices: 10.2 us -> 13.8 us  [exchange(): return lax.all_to_all(array, AXES, 0, 0, axis_index_groups=ring)]
    ppermute x3, starting transfers between devices: 12.3 us -> 10.2 us  [per_device(): blocks.append(lax.ppermute(own, AXES, route))]
    unnamed x22 -> x18, local copies, waits for them, and re-layouts: 4.42 us -> 2.49 us
    all_to_all x3, blocking collectives: 37 us -> 35.5 us  [exchange(): return lax.all_to_all(array, AXES, 0, 0, axis_index_groups=ring)]
  transfers between devices with their start and end apart: 16 -> 16, of which waited for: 8 -> 6; matrix products, arithmetic and copies ran while one was open for 0% -> 1% of each run, Pallas kernels for 2% -> 2%
where the time goes in v4:
time: 129 us
  starting transfers between devices  40 us (31%)
  blocking collectives  35.5 us (28%)
  waiting for transfers between devices  32.2 us (25%)
  Pallas kernels  16.2 us (13%)
  local copies, waits for them, and re-layouts  2.49 us (2%)
  other arithmetic  1.35 us (1%)
    all_to_all x3, blocking collectives, exchange(): return lax.all_to_all(array, AXES, 0, 0, axis_index_groups=ring)  35.5 us
    ppermute x4, waiting for transfers between devices, per_device(): blocks.append(lax.ppermute(sent, AXES, route))  18.4 us
    all_to_all x2, waiting for transfers between devices, exchange(): return lax.all_to_all(array, AXES, 0, 0, axis_index_groups=ring)  13.8 us
    pallas_call x7, Pallas kernels, call(): pl.pallas_call(body, out_shape=out_shape, in_specs=specs, out_specs=jax.t...  12.5 us
    ppermute x4, starting transfers between devices, per_device(): blocks.append(lax.ppermute(sent, AXES, route))  11.4 us
    ppermute x3, starting transfers between devices, per_device(): blocks.append(lax.ppermute(own, AXES, route))  10.2 us
    ppermute x7, starting transfers between devices, bring(): got.append(lax.ppermute(array, 'section', route))  9.54 us
    all_to_all x2, starting transfers between devices, exchange(): return lax.all_to_all(array, AXES, 0, 0, axis_index_groups=ring)  8.91 us
  transfers between devices with their start and end apart: 16, of which 6 were waited for; matrix products, arithmetic and copies ran while one was open for 1% of the time, Pallas kernels for 2%

profile of v4, /device:TPU:6, one launch (start us, length us, event | category | flops | bytes accessed | tf_op | source)
XLA Modules:
  0.0 128.6 jit_solution(239002196828806370)
XLA Ops:
  0.6 3.7 %shard_map.95 = (bf16[4,4,320,256]{3,2,1,0:T(8,128)(2,1)}, bf16[528,256]{1,0:T(8,128)(2,1)}) custom-call(bf16[512,256]{1,0:T(8,128)(2,1)} %bitcast.5, bf16[1,256]{1,0:T(2,128)(2,1)} %gain_ref.1, bf16[4096,256]{1,0:T(8,128)(2,1)} %bitcast.7, bf16[64,4096]{1,0:T(8,128)(2,1)} %bitcast.8), custom_call_target="tpu_custom_call" | custom-call | bytes 6291456 | tf_op jit(solution)/shard_map/pallas_call | solution.py:87
  4.4 4.6 %all-to-all-start = ((bf16[4,4,320,256]{3,2,1,0:T(8,128)(2,1)}), bf16[4,4,320,256]{3,2,1,0:T(8,128)(2,1)S(1)}, u32[]{:S(2)}, u32[]{:S(2)}) async-start(bf16[4,4,320,256]{3,2,1,0:T(8,128)(2,1)} %get-tuple-element.25), calls=%async_computation | async-start | bytes 5242880 | tf_op jit(solution)/shard_map/all_to_all | solution.py:340
  9.0 2.7 %collective-permute-start.2 = (bf16[528,256]{1,0:T(8,128)(2,1)S(1)}, bf16[528,256]{1,0:T(8,128)(2,1)S(1)}, u32[]{:S(2)}, u32[]{:S(2)}) collective-permute-start(bf16[528,256]{1,0:T(8,128)(2,1)S(1)} %copy-done.6), channel_id=1, source_target_pairs={{4,0},{5,1},{6,2},{7,3},{8,4},{9,5},{10,6},{11,7},{12,8},{13,9},{1... | collective-permute-start | bytes 811016 | tf_op jit(solution)/shard_map/ppermute | solution.py:348
  13.1 3.4 %collective-permute-start.3 = (bf16[512,256]{1,0:T(8,128)(2,1)S(1)}, bf16[512,256]{1,0:T(8,128)(2,1)S(1)}, u32[]{:S(2)}, u32[]{:S(2)}) collective-permute-start(bf16[512,256]{1,0:T(8,128)(2,1)S(1)} %shard_map.96), channel_id=1, source_target_pairs={{0,16},{32,48},{64,80},{96,112},{128,144},{160,176},{192,208},{224... | collective-permute-start | bytes 786440 | tf_op jit(solution)/shard_map/ppermute | solution.py:319
  16.5 5.5 %collective-permute-start.1 = (bf16[528,256]{1,0:T(8,128)(2,1)S(1)}, bf16[528,256]{1,0:T(8,128)(2,1)}, u32[]{:S(2)}, u32[]{:S(2)}) collective-permute-start(bf16[528,256]{1,0:T(8,128)(2,1)S(1)} %copy-done.6), channel_id=1, source_target_pairs={{8,0},{9,1},{10,2},{11,3},{12,4},{13,5},{14,6},{15,7},{0,8},{1,9},... | collective-permute-start | bytes 811016 | tf_op jit(solution)/shard_map/ppermute | solution.py:348
  22.0 1.9 %collective-permute-start = (bf16[528,256]{1,0:T(8,128)(2,1)S(1)}, bf16[528,256]{1,0:T(8,128)(2,1)}, u32[]{:S(2)}, u32[]{:S(2)}) collective-permute-start(bf16[528,256]{1,0:T(8,128)(2,1)S(1)} %copy-done.6), channel_id=1, source_target_pairs={{12,0},{13,1},{14,2},{15,3},{0,4},{1,5},{2,6},{3,7},{4,8},{5,9},{6... | collective-permute-start | bytes 811016 | tf_op jit(solution)/shard_map/ppermute | solution.py:348
  28.2 6.0 %all-to-all-done.refs_4_.refs_5_ = bf16[4,4,320,256]{3,2,1,0:T(8,128)(2,1)S(1)} async-done(((bf16[4,4,320,256]{3,2,1,0:T(8,128)(2,1)}), bf16[4,4,320,256]{3,2,1,0:T(8,128)(2,1)S(1)}, u32[]{:S(2)}, u32[]{:S(2)}) %all-to-all-start) | async-done | bytes 2621472 | tf_op jit(solution)/shard_map/all_to_all | solution.py:340
  34.2 3.0 %shard_map.97 = (bf16[4,656,256]{2,1,0:T(8,128)(2,1)S(1)}, bf16[64,256]{1,0:T(8,128)(2,1)S(1)}) custom-call(bf16[528,256]{1,0:T(8,128)(2,1)S(1)} %copy-done.6, bf16[528,256]{1,0:T(8,128)(2,1)} %collective-permute-done.refs_1_, bf16[528,256]{1,0:T(8,128)(2,1)} %collective-permute-done.1.refs_2_, bf16[528,256]{1,0:T(8,128)(2,1)S(1)} %collective-permute-done.2.refs_3_, ...), custom_call_target="tpu_custom_call" | custom-call | flops 1342177280 | bytes 6291456 | tf_op jit(solution)/shard_map/pallas_call | solution.py:49
  38.3 4.3 %all-to-all-start.1 = ((bf16[4,656,256]{2,1,0:T(8,128)(2,1)}), bf16[4,656,256]{2,1,0:T(8,128)(2,1)}, u32[]{:S(2)}, u32[]{:S(2)}) async-start(bf16[4,656,256]{2,1,0:T(8,128)(2,1)} %copy-done), calls=%async_computation.1 | async-start | bytes 2686976 | tf_op jit(solution)/shard_map/all_to_all | solution.py:340
  47.3 7.8 %all-to-all-done.1.parts_ref = bf16[4,656,256]{2,1,0:T(8,128)(2,1)} async-done(((bf16[4,656,256]{2,1,0:T(8,128)(2,1)}), bf16[4,656,256]{2,1,0:T(8,128)(2,1)}, u32[]{:S(2)}, u32[]{:S(2)}) %all-to-all-start.1) | async-done | bytes 1343520 | tf_op jit(solution)/shard_map/all_to_all | solution.py:340
  56.7 10.1 %all_to_all.25.keyval_ref = bf16[4,64,512]{2,1,0:T(8,128)(2,1)S(1)} all-to-all(bf16[4,64,512]{2,1,0:T(8,128)(2,1)S(1)} %get-tuple-element.34), channel_id=1, replica_groups={{0,1,2,3},{4,5,6,7},{8,9,10,11},{12,13,14,15},{16,17,18,19},{20,21,22,2..., dimensions={0} | all-to-all | bytes 524288 | tf_op jit(solution)/shard_map/all_to_all | solution.py:340
  66.8 2.0 %shard_map.99 = (bf16[512,256]{1,0:T(8,128)(2,1)}, bf16[512,256]{1,0:T(8,128)(2,1)S(1)}) custom-call(s32[32]{0:T(128)S(1)} %copy-done.4, bf16[512,256]{1,0:T(8,128)(2,1)S(1)} %bitcast.6, bf16[512,256]{1,0:T(8,128)(2,1)S(1)} %get-tuple-element.29.query_ref, bf16[4,64,512]{2,1,0:T(8,128)(2,1)S(1)} %all_to_all.25.keyval_ref, s32[32,512]{1,0:T(8,128)S(1)} %copy-done.2, ...), custom_call_target="tpu_custom_call" | custom-call | flops 134217728 | bytes 1048576 | tf_op jit(solution)/shard_map/pallas_call | solution.py:49
  68.9 2.5 %collective-permute-start.13 = (bf16[512,256]{1,0:T(8,128)(2,1)S(1)}, bf16[512,256]{1,0:T(8,128)(2,1)S(1)}, u32[]{:S(2)}, u32[]{:S(2)}) collective-permute-start(bf16[512,256]{1,0:T(8,128)(2,1)S(1)} %get-tuple-element.40), channel_id=1, source_target_pairs={{500,0},{501,1},{502,2},{503,3},{504,4},{505,5},{506,6},{507,7},{5... | collective-permute-start | bytes 786440 | tf_op jit(solution)/shard_map/ppermute | solution.py:368
  71.3 3.0 %collective-permute-start.12 = (bf16[512,256]{1,0:T(8,128)(2,1)S(1)}, bf16[512,256]{1,0:T(8,128)(2,1)S(1)}, u32[]{:S(2)}, u32[]{:S(2)}) collective-permute-start(bf16[512,256]{1,0:T(8,128)(2,1)S(1)} %get-tuple-element.40), channel_id=1, source_target_pairs={{504,0},{505,1},{506,2},{507,3},{508,4},{509,5},{510,6},{511,7},{4... | collective-permute-start | bytes 786440 | tf_op jit(solution)/shard_map/ppermute | solution.py:368
  74.4 2.2 %collective-permute-start.11 = (bf16[512,256]{1,0:T(8,128)(2,1)S(1)}, bf16[512,256]{1,0:T(8,128)(2,1)S(1)}, u32[]{:S(2)}, u32[]{:S(2)}) collective-permute-start(bf16[512,256]{1,0:T(8,128)(2,1)S(1)} %get-tuple-element.40), channel_id=1, source_target_pairs={{508,0},{509,1},{510,2},{511,3},{496,4},{497,5},{498,6},{499,7},{5... | collective-permute-start | bytes 786440 | tf_op jit(solution)/shard_map/ppermute | solution.py:368
  76.6 3.7 %collective-permute-start.10 = (bf16[512,256]{1,0:T(8,128)(2,1)S(1)}, bf16[512,256]{1,0:T(8,128)(2,1)S(1)}, u32[]{:S(2)}, u32[]{:S(2)}) collective-permute-start(bf16[512,256]{1,0:T(8,128)(2,1)S(1)} %get-tuple-element.40), channel_id=1, source_target_pairs={{496,0},{497,1},{498,2},{499,3},{500,4},{501,5},{502,6},{503,7},{5... | collective-permute-start | bytes 786440 | tf_op jit(solution)/shard_map/ppermute | solution.py:368
  80.3 9.5 %collective-permute-done.13.refs_3_ = bf16[512,256]{1,0:T(8,128)(2,1)S(1)} collective-permute-done((bf16[512,256]{1,0:T(8,128)(2,1)S(1)}, bf16[512,256]{1,0:T(8,128)(2,1)S(1)}, u32[]{:S(2)}, u32[]{:S(2)}) %collective-permute-start.13) | collective-permute-done | bytes 262176 | tf_op jit(solution)/shard_map/ppermute | solution.py:368
  89.8 4.0 %collective-permute-done.12.refs_2_ = bf16[512,256]{1,0:T(8,128)(2,1)S(1)} collective-permute-done((bf16[512,256]{1,0:T(8,128)(2,1)S(1)}, bf16[512,256]{1,0:T(8,128)(2,1)S(1)}, u32[]{:S(2)}, u32[]{:S(2)}) %collective-permute-start.12) | collective-permute-done | bytes 262176 | tf_op jit(solution)/shard_map/ppermute | solution.py:368
  93.8 2.3 %collective-permute-done.11.refs_1_ = bf16[512,256]{1,0:T(8,128)(2,1)S(1)} collective-permute-done((bf16[512,256]{1,0:T(8,128)(2,1)S(1)}, bf16[512,256]{1,0:T(8,128)(2,1)S(1)}, u32[]{:S(2)}, u32[]{:S(2)}) %collective-permute-start.11) | collective-permute-done | bytes 262176 | tf_op jit(solution)/shard_map/ppermute | solution.py:368
  96.0 2.6 %collective-permute-done.10.refs_0_.x_ref = bf16[512,256]{1,0:T(8,128)(2,1)S(1)} collective-permute-done((bf16[512,256]{1,0:T(8,128)(2,1)S(1)}, bf16[512,256]{1,0:T(8,128)(2,1)S(1)}, u32[]{:S(2)}, u32[]{:S(2)}) %collective-permute-start.10) | collective-permute-done | bytes 262176 | tf_op jit(solution)/shard_map/ppermute | solution.py:368
  98.7 2.1 %shard_map.100 = bf16[4,656,256]{2,1,0:T(8,128)(2,1)S(1)} custom-call(bf16[512,256]{1,0:T(8,128)(2,1)S(1)} %collective-permute-done.10.refs_0_.x_ref, bf16[512,256]{1,0:T(8,128)(2,1)S(1)} %collective-permute-done.11.refs_1_, bf16[512,256]{1,0:T(8,128)(2,1)S(1)} %collective-permute-done.12.refs_2_, bf16[512,256]{1,0:T(8,128)(2,1)S(1)} %collective-permute-done.13.refs_3_, ...), custom_call_target="tpu_custom_call" | custom-call | flops 1342177280 | bytes 6291456 | tf_op jit(solution)/shard_map/pallas_call | solution.py:49
  100.9 16.3 %all_to_all.26.parts_ref = bf16[4,656,256]{2,1,0:T(8,128)(2,1)S(1)} all-to-all(bf16[4,656,256]{2,1,0:T(8,128)(2,1)S(1)} %shard_map.100), channel_id=1, replica_groups={{0,1,2,3},{4,5,6,7},{8,9,10,11},{12,13,14,15},{16,20,24,28},{17,21,25,2..., dimensions={0} | all-to-all | bytes 2686976 | tf_op jit(solution)/shard_map/all_to_all | solution.py:340
  117.3 9.1 %all_to_all.27.keyval_ref = bf16[4,64,512]{2,1,0:T(8,128)(2,1)S(1)} all-to-all(bf16[4,64,512]{2,1,0:T(8,128)(2,1)S(1)} %get-tuple-element.43), channel_id=1, replica_groups={{0,1,2,3},{4,5,6,7},{8,9,10,11},{12,13,14,15},{16,17,18,19},{20,21,22,2..., dimensions={0} | all-to-all | bytes 524288 | tf_op jit(solution)/shard_map/all_to_all | solution.py:340
  126.4 2.2 %shard_map.102 = bf16[512,256]{1,0:T(8,128)(2,1)} custom-call(s32[32]{0:T(128)S(1)} %copy-done.4, bf16[512,256]{1,0:T(8,128)(2,1)S(1)} %collective-permute-done.10.refs_0_.x_ref, bf16[512,256]{1,0:T(8,128)(2,1)S(1)} %get-tuple-element.42.query_ref, bf16[4,64,512]{2,1,0:T(8,128)(2,1)S(1)} %all_to_all.27.keyval_ref, s32[32,512]{1,0:T(8,128)S(1)} %copy-done.2), custom_call_target="tpu_custom_call" | custom-call | flops 134217728 | bytes 1048576 | tf_op jit(solution)/shard_map/pallas_call | solution.py:49
  (39 shorter events, 13.0 us)
Async XLA Ops:
  4.4 4.7 %copy-start.6 = (bf16[528,256]{1,0:T(8,128)(2,1)S(1)}, bf16[528,256]{1,0:T(8,128)(2,1)}, u32[]{:S(2)}) copy-start(bf16[528,256]{1,0:T(8,128)(2,1)} %get-tuple-element.23.refs_0_) | copy-start | bytes 811012
  4.4 7.4 %copy-start.3 = (bf16[2,128,256]{2,1,0:T(8,128)(2,1)S(1)}, bf16[2,128,256]{2,1,0:T(8,128)(2,1)}, u32[]{:S(2)}) copy-start(bf16[2,128,256]{2,1,0:T(8,128)(2,1)} %pool_ref.1) | copy-start | bytes 393220
  4.4 7.4 %copy-start.4 = (s32[32]{0:T(128)S(1)}, s32[32]{0:T(128)}, u32[]{:S(2)}) copy-start(s32[32]{0:T(128)} %lengths_ref.5) | copy-start | bytes 388
  4.4 7.4 %copy-start.5 = (s32[32]{0:T(128)S(1)}, s32[32]{0:T(128)}, u32[]{:S(2)}) copy-start(s32[32]{0:T(128)} %ids_ref.1) | copy-start | bytes 388
  4.4 29.8 %all-to-all-start = ((bf16[4,4,320,256]{3,2,1,0:T(8,128)(2,1)}), bf16[4,4,320,256]{3,2,1,0:T(8,128)(2,1)S(1)}, u32[]{:S(2)}, u32[]{:S(2)}) async-start(bf16[4,4,320,256]{3,2,1,0:T(8,128)(2,1)} %get-tuple-element.25), calls=%async_computation | async-start | bytes 5242880 | tf_op jit(solution)/shard_map/all_to_all | solution.py:340
  9.0 14.9 %collective-permute-start.2 = (bf16[528,256]{1,0:T(8,128)(2,1)S(1)}, bf16[528,256]{1,0:T(8,128)(2,1)S(1)}, u32[]{:S(2)}, u32[]{:S(2)}) collective-permute-start(bf16[528,256]{1,0:T(8,128)(2,1)S(1)} %copy-done.6), channel_id=1, source_target_pairs={{4,0},{5,1},{6,2},{7,3},{8,4},{9,5},{10,6},{11,7},{12,8},{13,9},{1... | collective-permute-start | bytes 811016 | tf_op jit(solution)/shard_map/ppermute | solution.py:348
  13.1 10.9 %collective-permute-start.3 = (bf16[512,256]{1,0:T(8,128)(2,1)S(1)}, bf16[512,256]{1,0:T(8,128)(2,1)S(1)}, u32[]{:S(2)}, u32[]{:S(2)}) collective-permute-start(bf16[512,256]{1,0:T(8,128)(2,1)S(1)} %shard_map.96), channel_id=1, source_target_pairs={{0,16},{32,48},{64,80},{96,112},{128,144},{160,176},{192,208},{224... | collective-permute-start | bytes 786440 | tf_op jit(solution)/shard_map/ppermute | solution.py:319
  16.5 17.7 %collective-permute-start.1 = (bf16[528,256]{1,0:T(8,128)(2,1)S(1)}, bf16[528,256]{1,0:T(8,128)(2,1)}, u32[]{:S(2)}, u32[]{:S(2)}) collective-permute-start(bf16[528,256]{1,0:T(8,128)(2,1)S(1)} %copy-done.6), channel_id=1, source_target_pairs={{8,0},{9,1},{10,2},{11,3},{12,4},{13,5},{14,6},{15,7},{0,8},{1,9},... | collective-permute-start | bytes 811016 | tf_op jit(solution)/shard_map/ppermute | solution.py:348
  22.0 12.2 %collective-permute-start = (bf16[528,256]{1,0:T(8,128)(2,1)S(1)}, bf16[528,256]{1,0:T(8,128)(2,1)}, u32[]{:S(2)}, u32[]{:S(2)}) collective-permute-start(bf16[528,256]{1,0:T(8,128)(2,1)S(1)} %copy-done.6), channel_id=1, source_target_pairs={{12,0},{13,1},{14,2},{15,3},{0,4},{1,5},{2,6},{3,7},{4,8},{5,9},{6... | collective-permute-start | bytes 811016 | tf_op jit(solution)/shard_map/ppermute | solution.py:348
  24.1 2.7 %collective-permute-start.6 = (bf16[512,256]{1,0:T(8,128)(2,1)S(1)}, bf16[512,256]{1,0:T(8,128)(2,1)S(1)}, u32[]{:S(2)}, u32[]{:S(2)}) collective-permute-start(bf16[512,256]{1,0:T(8,128)(2,1)S(1)} %add.12), channel_id=1, source_target_pairs={{16,112},{144,240},{272,368},{400,496},{17,113},{145,241},{273,369... | collective-permute-start | bytes 786440 | tf_op jit(solution)/shard_map/ppermute | solution.py:319
  24.8 2.1 %collective-permute-start.5 = (bf16[512,256]{1,0:T(8,128)(2,1)S(1)}, bf16[512,256]{1,0:T(8,128)(2,1)S(1)}, u32[]{:S(2)}, u32[]{:S(2)}) collective-permute-start(bf16[512,256]{1,0:T(8,128)(2,1)S(1)} %add.12), channel_id=1, source_target_pairs={{48,112},{176,240},{304,368},{432,496},{49,113},{177,241},{305,369... | collective-permute-start | bytes 786440 | tf_op jit(solution)/shard_map/ppermute | solution.py:319
  25.4 2.8 %collective-permute-start.4 = (bf16[512,256]{1,0:T(8,128)(2,1)S(1)}, bf16[512,256]{1,0:T(8,128)(2,1)}, u32[]{:S(2)}, u32[]{:S(2)}) collective-permute-start(bf16[512,256]{1,0:T(8,128)(2,1)S(1)} %add.12), channel_id=1, source_target_pairs={{80,112},{208,240},{336,368},{464,496},{81,113},{209,241},{337,369... | collective-permute-start | bytes 786440 | tf_op jit(solution)/shard_map/ppermute | solution.py:319
  26.8 0.7 copy-start.7
  37.2 1.1 copy-start
  38.3 16.8 %all-to-all-start.1 = ((bf16[4,656,256]{2,1,0:T(8,128)(2,1)}), bf16[4,656,256]{2,1,0:T(8,128)(2,1)}, u32[]{:S(2)}, u32[]{:S(2)}) async-start(bf16[4,656,256]{2,1,0:T(8,128)(2,1)} %copy-done), calls=%async_computation.1 | async-start | bytes 2686976 | tf_op jit(solution)/shard_map/all_to_all | solution.py:340
  42.6 24.2 %copy-start.1 = (bf16[1,512,256]{2,1,0:T(8,128)(2,1)S(1)}, bf16[1,512,256]{2,1,0:T(8,128)(2,1)}, u32[]{:S(2)}) copy-start(bf16[1,512,256]{2,1,0:T(8,128)(2,1)} %param.8) | copy-start | bytes 786436
  42.6 24.2 %copy-start.2 = (s32[32,512]{1,0:T(8,128)S(1)}, s32[32,512]{1,0:T(8,128)}, u32[]{:S(2)}) copy-start(s32[32,512]{1,0:T(8,128)} %segments_ref.3) | copy-start | bytes 196612
  43.9 12.7 %collective-permute-start.9 = (bf16[512,256]{1,0:T(8,128)(2,1)S(1)}, bf16[512,256]{1,0:T(8,128)(2,1)S(1)}, u32[]{:S(2)}, u32[]{:S(2)}) collective-permute-start(bf16[512,256]{1,0:T(8,128)(2,1)S(1)} %add_convert_fusion.refs_0_), channel_id=1, source_target_pairs={{112,496},{113,497},{114,498},{115,499},{116,500},{117,501},{118,5... | collective-permute-start | bytes 786440 | tf_op jit(solution)/shard_map/ppermute | solution.py:319
  44.6 12.1 %collective-permute-start.8 = (bf16[512,256]{1,0:T(8,128)(2,1)S(1)}, bf16[512,256]{1,0:T(8,128)(2,1)}, u32[]{:S(2)}, u32[]{:S(2)}) collective-permute-start(bf16[512,256]{1,0:T(8,128)(2,1)S(1)} %add_convert_fusion.refs_0_), channel_id=1, source_target_pairs={{240,496},{241,497},{242,498},{243,499},{244,500},{245,501},{246,5... | collective-permute-start | bytes 786440 | tf_op jit(solution)/shard_map/ppermute | solution.py:319
  46.0 10.7 %collective-permute-start.7 = (bf16[512,256]{1,0:T(8,128)(2,1)S(1)}, bf16[512,256]{1,0:T(8,128)(2,1)}, u32[]{:S(2)}, u32[]{:S(2)}) collective-permute-start(bf16[512,256]{1,0:T(8,128)(2,1)S(1)} %add_convert_fusion.refs_0_), channel_id=1, source_target_pairs={{368,496},{369,497},{370,498},{371,499},{372,500},{373,501},{374,5... | collective-permute-start | bytes 786440 | tf_op jit(solution)/shard_map/ppermute | solution.py:319
  68.9 20.9 %collective-permute-start.13 = (bf16[512,256]{1,0:T(8,128)(2,1)S(1)}, bf16[512,256]{1,0:T(8,128)(2,1)S(1)}, u32[]{:S(2)}, u32[]{:S(2)}) collective-permute-start(bf16[512,256]{1,0:T(8,128)(2,1)S(1)} %get-tuple-element.40), channel_id=1, source_target_pairs={{500,0},{501,1},{502,2},{503,3},{504,4},{505,5},{506,6},{507,7},{5... | collective-permute-start | bytes 786440 | tf_op jit(solution)/shard_map/ppermute | solution.py:368
  71.3 22.4 %collective-permute-start.12 = (bf16[512,256]{1,0:T(8,128)(2,1)S(1)}, bf16[512,256]{1,0:T(8,128)(2,1)S(1)}, u32[]{:S(2)}, u32[]{:S(2)}) collective-permute-start(bf16[512,256]{1,0:T(8,128)(2,1)S(1)} %get-tuple-element.40), channel_id=1, source_target_pairs={{504,0},{505,1},{506,2},{507,3},{508,4},{509,5},{510,6},{511,7},{4... | collective-permute-start | bytes 786440 | tf_op jit(solution)/shard_map/ppermute | solution.py:368
  74.4 21.7 %collective-permute-start.11 = (bf16[512,256]{1,0:T(8,128)(2,1)S(1)}, bf16[512,256]{1,0:T(8,128)(2,1)S(1)}, u32[]{:S(2)}, u32[]{:S(2)}) collective-permute-start(bf16[512,256]{1,0:T(8,128)(2,1)S(1)} %get-tuple-element.40), channel_id=1, source_target_pairs={{508,0},{509,1},{510,2},{511,3},{496,4},{497,5},{498,6},{499,7},{5... | collective-permute-start | bytes 786440 | tf_op jit(solution)/shard_map/ppermute | solution.py:368
  76.6 22.1 %collective-permute-start.10 = (bf16[512,256]{1,0:T(8,128)(2,1)S(1)}, bf16[512,256]{1,0:T(8,128)(2,1)S(1)}, u32[]{:S(2)}, u32[]{:S(2)}) collective-permute-start(bf16[512,256]{1,0:T(8,128)(2,1)S(1)} %get-tuple-element.40), channel_id=1, source_target_pairs={{496,0},{497,1},{498,2},{499,3},{500,4},{501,5},{502,6},{503,7},{5... | collective-permute-start | bytes 786440 | tf_op jit(solution)/shard_map/ppermute | solution.py:368
  (1 other events, 0.7 us)

commit v5 on v4

--- a/solution.py
+++ b/solution.py
@@ -17,6 +17,7 @@
 ROW_MAX = 128
 HOST_ROWS = 2
 SLOTS = 32
+NEAR = 8
 SENT_ROWS = TOKENS + 2 * KV_ROWS + 16
 AXES = ("section", "tensor")
 norm_eps = 1e-05
@@ -57,8 +58,16 @@
     )(*operands)
 
 
-def prepare_body(x_ref, gain_ref, query_ref, keyval_ref, packed_ref, own_ref, packed, own, sems):
-    odd = lax.axis_index("section") % 2
+def prepare_body(ids_ref, x_ref, gain_ref, query_ref, keyval_ref, pool_ref, *refs):
+    packed_ref, own_ref, row_ref, packed, own, row, sems = refs
+    section = lax.axis_index("section")
+    odd = section % 2
+
+    def find(k, which):
+        local = ids_ref[k] - HOST_ROWS * section
+        return jnp.where((local >= 0) & (local < HOST_ROWS), local, which)
+
+    which = lax.fori_loop(0, SLOTS, find, jnp.int32(0))
     arrivals = []
     for i in range(SIDE):
         for j in range(SIDE):
@@ -66,36 +75,40 @@
             arrivals.append((query_ref.at[pl.ds(start, BLOCK)], packed.at[i, j, pl.ds(0, BLOCK)]))
             arrivals.append((keyval_ref.at[:, pl.ds(start, BLOCK)], packed.at[i, j, pl.ds(BLOCK, KV_ROWS)]))
     arrivals.append((x_ref, own.at[pl.ds(0, TOKENS)]))
+    arrivals.append((pool_ref.at[which], row))
     arrivals = [pltpu.make_async_copy(src, dst, sems.at[n]) for n, (src, dst) in enumerate(arrivals)]
     for copy in arrivals:
         copy.start()
     own[TOKENS:] = jnp.broadcast_to(gain_ref[...].astype(f32), (16, BLOCK)).astype(bf16)
     leaving = []
-    for i in range(SIDE + 1):
-        for copy in arrivals[2 * SIDE * i : 2 * SIDE * (i + 1)]:
+    ready = [(packed.at[i], packed_ref.at[i], arrivals[2 * SIDE * i : 2 * SIDE * (i + 1)]) for i in range(SIDE)]
+    ready += [(own, own_ref, arrivals[-2:-1]), (row, row_ref, arrivals[-1:])]
+    for n, (src, dst, waits) in enumerate(ready):
+        for copy in waits:
             copy.wait()
-        src, dst = (packed.at[i], packed_ref.at[i]) if i < SIDE else (own, own_ref)
-        leaving.append(pltpu.make_async_copy(src, dst, sems.at[len(arrivals) + i]))
+        leaving.append(pltpu.make_async_copy(src, dst, sems.at[len(arrivals) + n]))
         leaving[-1].start()
     for copy in leaving:
         copy.wait()
 
 
-def prepare(x, gain, w_query, w_kv):
+def prepare(row_ids, x, gain, w_query, w_kv, pool):
     packed = (SIDE, SIDE, BLOCK + KV_ROWS, BLOCK)
     own = (TOKENS + 16, BLOCK)
+    row = pool.shape[1:]
     return pl.pallas_call(
         prepare_body,
-        out_shape=(jax.ShapeDtypeStruct(packed, bf16), jax.ShapeDtypeStruct(own, bf16)),
-        in_specs=[ANY, VMEM, ANY, ANY],
-        out_specs=(ANY, ANY),
+        out_shape=tuple(jax.ShapeDtypeStruct(shape, bf16) for shape in (packed, own, row)),
+        in_specs=[SMEM, ANY, VMEM, ANY, ANY, ANY],
+        out_specs=(ANY, ANY, ANY),
         scratch_shapes=[
             pltpu.VMEM(packed, bf16),
             pltpu.VMEM(own, bf16),
-            pltpu.SemaphoreType.DMA((2 * SIDE * SIDE + SIDE + 2,)),
+            pltpu.VMEM(row, bf16),
+            pltpu.SemaphoreType.DMA((2 * SIDE * SIDE + SIDE + 4,)),
         ],
         cost_estimate=pl.CostEstimate(flops=0, bytes_accessed=6 << 20, transcendentals=0),
-    )(x, gain, w_query, w_kv)
+    )(row_ids, x, gain, w_query, w_kv, pool)
 
 
 def ring_place():
@@ -278,53 +291,48 @@
     )
 
 
-def frame_body(ids_ref, lengths_ref, pool_ref, out_ref, total_ref):
-    total_ref[...] = jnp.zeros_like(total_ref)
-    section = lax.axis_index("section")
-    row = lax.broadcasted_iota(jnp.int32, (TOKENS, ROW_MAX), 0)
+def frame_body(ids_ref, lengths_ref, rows_ref, out_ref, starts, counts, hits_ref):
+    base = lax.div(lax.axis_index("section"), NEAR) * NEAR
+    for n in range(NEAR):
+        starts[n] = 0
+        counts[n] = 0
+
+    def note(k, start):
+        length = lengths_ref[k]
+        host = lax.div(ids_ref[k], HOST_ROWS) - base
+
+        @pl.when((host >= 0) & (host < NEAR))
+        def _():
+            starts[host] = start
+            counts[host] = length
+
+        return start + length
+
+    lax.fori_loop(0, SLOTS, note, jnp.int32(0))
+    offset = lax.broadcasted_iota(jnp.int32, (TOKENS, ROW_MAX), 0) - lax.broadcasted_iota(
+        jnp.int32, (TOKENS, ROW_MAX), 1
+    )
     col = lax.broadcasted_iota(jnp.int32, (TOKENS, ROW_MAX), 1)
-
-    def take(k, start):
-        length = lengths_ref[k]
-        which = ids_ref[k] - HOST_ROWS * section
-
-        @pl.when((which >= 0) & (which < HOST_ROWS))
-        def _():
-            hit = ((row - start == col) & (col < length)).astype(f32).astype(bf16)
-            total_ref[...] += jnp.dot(hit, pool_ref[which], preferred_element_type=f32)
-
-        return start + length
-
-    lax.fori_loop(0, SLOTS, take, jnp.int32(0))
-    out_ref[...] = total_ref[...].astype(bf16)
-
-
-def make_frame(row_ids, row_lengths, pool):
+    for n in range(NEAR):
+        hit = (offset == starts[n]) & (col < counts[n])
+        hits_ref[:, n * ROW_MAX : (n + 1) * ROW_MAX] = hit.astype(f32).astype(bf16)
+    out_ref[...] = jnp.dot(hits_ref[...], rows_ref[...], preferred_element_type=f32).astype(bf16)
+
+
+def make_frame(row_ids, row_lengths, rows):
     return call(
         frame_body,
         jax.ShapeDtypeStruct((TOKENS, BLOCK), bf16),
-        (row_ids, row_lengths, pool),
+        (row_ids, row_lengths, rows),
         [SMEM, SMEM, VMEM],
-        2 * TOKENS * 128 * 256,
+        2 * TOKENS * NEAR * 128 * 256,
         1 << 20,
-        scratch_shapes=[pltpu.VMEM((TOKENS, BLOCK), f32)],
-    )
-
-
-def bring(array, sections, step, count):
-    last = sections - 1
-    got = []
-    for n in range(1, count + 1):
-        route = [(i - n * step, i) for i in range(sections) if (last - i) % ((count + 1) * step) == 0]
-        got.append(lax.ppermute(array, "section", route))
-    return got
-
-
-def total_of(arrays):
-    total = arrays[0].astype(f32)
-    for array in arrays[1:]:
-        total = total + array.astype(f32)
-    return total.astype(bf16)
+        scratch_shapes=[
+            pltpu.SMEM((NEAR,), jnp.int32),
+            pltpu.SMEM((NEAR,), jnp.int32),
+            pltpu.VMEM((TOKENS, NEAR * ROW_MAX), bf16),
+        ],
+    )
 
 
 def per_device(activations, gain, w_query, w_kv, segments, pool, row_ids, row_lengths):
@@ -340,21 +348,28 @@
         return lax.all_to_all(array, AXES, 0, 0, axis_index_groups=ring)
 
     x = activations[0]
-    packed, own = prepare(x, gain, w_query[0], w_kv[0])
+    packed, own, row = prepare(row_ids, x, gain, w_query[0], w_kv[0], pool)
     weights = exchange(packed, ring_b)
     blocks = [own]
     for d in range(1, SIDE):
         route = [(number(s, a - d, b, s), number(s, a, b, s)) for s, a, b in grid]
         blocks.append(lax.ppermute(own, AXES, route))
 
-    frame = make_frame(row_ids, row_lengths, pool)
-    piece = bring(frame, sections, 1, 1)[0]
-    blocks[SIDE - 1], piece = barrier((blocks[SIDE - 1], piece))
-    frame = frame + piece
-    pieces = bring(frame, sections, 2, 3)
-    weights, pieces = barrier((weights, pieces))
-    frame = total_of([frame, *pieces])
-    frames = [frame, *bring(frame, sections, 8, 3)]
+    tensors = range(SIDE * SIDE)
+    pairs = [[(s + c) * SIDE * SIDE + t for c in range(2)] for s in range(0, sections, 2) for t in tensors]
+    fours = [
+        [(s + c + 2 * z) * SIDE * SIDE + t for z in range(NEAR // 2)]
+        for s in range(0, sections, NEAR)
+        for c in range(2)
+        for t in tensors
+    ]
+    rows = lax.all_gather(row, AXES, axis=0, axis_index_groups=pairs, tiled=True)
+    rows = lax.all_gather(rows, AXES, axis=0, axis_index_groups=fours, tiled=True)
+    frame = make_frame(row_ids, row_lengths, rows)
+    weights, frame = barrier((weights, frame))
+    last = sections - 1
+    sources = [1 if n == 0 else (n * NEAR + 1 if 2 * n < sections // NEAR else n * NEAR + NEAR - 1) for n in range(last // NEAR)]
+    frames = [frame, *[lax.ppermute(frame, "section", [(source, last)]) for source in sources]]
 
     parts, gains = project(False, blocks, [], weights)
     parts = exchange(parts, ring_b)

time: 129 us -> 129 us (level); the launches traced: 129 us -> 127 us
  blocking collectives: 35.5 us -> 51.3 us
  waiting for transfers between devices: 32.2 us -> 20 us
  starting transfers between devices: 40 us -> 35.8 us
  other arithmetic: 1.35 us -> 0 us
    all_gather x0 -> x2, blocking collectives: none -> 17.6 us  [the longest x1 15.7 us: per_device(): lax.all_gather(rows, AXES, axis=0, axis_index_groups=fours, tiled=True)]
    ppermute x4, waiting for transfers between devices: 18.4 us -> 11 us  [per_device(): blocks.append(lax.ppermute(sent, AXES, route))]
    ppermute x7 -> x3, starting transfers between devices: 9.54 us -> 3.55 us  [per_device(): lax.ppermute(frame, 'section', [(source, last)])]
    all_to_all x2, waiting for transfers between devices: 13.8 us -> 9.01 us  [exchange(): return lax.all_to_all(array, AXES, 0, 0, axis_index_groups=ring)]
    all_to_all x3, blocking collectives: 35.5 us -> 33.7 us  [exchange(): return lax.all_to_all(array, AXES, 0, 0, axis_index_groups=ring)]
    ppermute x3, starting transfers between devices: 10.2 us -> 11.7 us  [per_device(): blocks.append(lax.ppermute(own, AXES, route))]
  transfers between devices with their start and end apart: 16 -> 12, of which waited for: 6 -> 5; matrix products, arithmetic and copies ran while one was open for 1% -> 0% of each run, Pallas kernels for 2% -> 2%
where the time goes in v5:
time: 129 us; the launch traced here: 127 us
  blocking collectives  51.3 us (40%)
  starting transfers between devices  35.8 us (28%)
  waiting for transfers between devices  20 us (16%)
  Pallas kernels  16.5 us (13%)
  local copies, waits for them, and re-layouts  2.74 us (2%)
    all_to_all x3, blocking collectives, exchange(): return lax.all_to_all(array, AXES, 0, 0, axis_index_groups=ring)  33.7 us
    all_gather x1, blocking collectives, per_device(): lax.all_gather(rows, AXES, axis=0, axis_index_groups=fours, tiled=True)  15.7 us
    pallas_call x7, Pallas kernels, call(): pl.pallas_call(body, out_shape=out_shape, in_specs=specs, out_specs=jax.t...  12.4 us
    ppermute x3, starting transfers between devices, per_device(): blocks.append(lax.ppermute(own, AXES, route))  11.7 us
    ppermute x4, waiting for transfers between devices, per_device(): blocks.append(lax.ppermute(sent, AXES, route))  11 us
    ppermute x4, starting transfers between devices, per_device(): blocks.append(lax.ppermute(sent, AXES, route))  10.9 us
    all_to_all x2, starting transfers between devices, exchange(): return lax.all_to_all(array, AXES, 0, 0, axis_index_groups=ring)  9.67 us
    all_to_all x2, waiting for transfers between devices, exchange(): return lax.all_to_all(array, AXES, 0, 0, axis_index_groups=ring)  9.01 us
  transfers between devices with their start and end apart: 12, of which 5 were waited for; matrix products, arithmetic and copies ran while one was open for 0% of the time, Pallas kernels for 2%

profile of v5, /device:TPU:6, one launch (start us, length us, event | category | flops | bytes accessed | tf_op | source)
XLA Modules:
  0.0 127.1 jit_solution(12358977662899052451)
XLA Ops:
  0.6 4.1 %shard_map.95 = (bf16[4,4,320,256]{3,2,1,0:T(8,128)(2,1)}, bf16[528,256]{1,0:T(8,128)(2,1)}, bf16[128,256]{1,0:T(8,128)(2,1)}) custom-call(s32[32]{0:T(128)} %ids_ref.3, bf16[512,256]{1,0:T(8,128)(2,1)} %bitcast.5, bf16[1,256]{1,0:T(2,128)(2,1)} %gain_ref.1, bf16[4096,256]{1,0:T(8,128)(2,1)} %bitcast.7, bf16[64,4096]{1,0:T(8,128)(2,1)} %bitcast.8, ...), custom_call_target="tpu_custom_call" | custom-call | bytes 6291456 | tf_op jit(solution)/shard_map/pallas_call | solution.py:99
  4.8 4.6 %all-to-all-start = ((bf16[4,4,320,256]{3,2,1,0:T(8,128)(2,1)}), bf16[4,4,320,256]{3,2,1,0:T(8,128)(2,1)S(1)}, u32[]{:S(2)}, u32[]{:S(2)}) async-start(bf16[4,4,320,256]{3,2,1,0:T(8,128)(2,1)} %get-tuple-element.21), calls=%async_computation | async-start | bytes 5242880 | tf_op jit(solution)/shard_map/all_to_all | solution.py:348
  9.4 7.0 %collective-permute-start = (bf16[528,256]{1,0:T(8,128)(2,1)S(1)}, bf16[528,256]{1,0:T(8,128)(2,1)S(1)}, u32[]{:S(2)}, u32[]{:S(2)}) collective-permute-start(bf16[528,256]{1,0:T(8,128)(2,1)S(1)} %copy-done.5), channel_id=1, source_target_pairs={{12,0},{13,1},{14,2},{15,3},{0,4},{1,5},{2,6},{3,7},{4,8},{5,9},{6... | collective-permute-start | bytes 811016 | tf_op jit(solution)/shard_map/ppermute | solution.py:356
  16.3 1.9 %collective-permute-start.1 = (bf16[528,256]{1,0:T(8,128)(2,1)S(1)}, bf16[528,256]{1,0:T(8,128)(2,1)}, u32[]{:S(2)}, u32[]{:S(2)}) collective-permute-start(bf16[528,256]{1,0:T(8,128)(2,1)S(1)} %copy-done.5), channel_id=1, source_target_pairs={{8,0},{9,1},{10,2},{11,3},{12,4},{13,5},{14,6},{15,7},{0,8},{1,9},... | collective-permute-start | bytes 811016 | tf_op jit(solution)/shard_map/ppermute | solution.py:356
  18.3 2.8 %collective-permute-start.2 = (bf16[528,256]{1,0:T(8,128)(2,1)S(1)}, bf16[528,256]{1,0:T(8,128)(2,1)}, u32[]{:S(2)}, u32[]{:S(2)}) collective-permute-start(bf16[528,256]{1,0:T(8,128)(2,1)S(1)} %copy-done.5), channel_id=1, source_target_pairs={{4,0},{5,1},{6,2},{7,3},{8,4},{9,5},{10,6},{11,7},{12,8},{13,9},{1... | collective-permute-start | bytes 811016 | tf_op jit(solution)/shard_map/ppermute | solution.py:356
  21.1 1.9 %all_gather.6 = bf16[256,256]{1,0:T(8,128)(2,1)S(1)} all-gather(bf16[128,256]{1,0:T(8,128)(2,1)S(1)} %copy-done.8), channel_id=1, replica_groups={{0,16},{1,17},{2,18},{3,19},{4,20},{5,21},{6,22},{7,23},{8,24},{9,25},{..., dimensions={0}, use_global_device_ids=true | all-gather | bytes 196608 | tf_op jit(solution)/shard_map/all_gather | solution.py:366
  23.0 15.7 %all_gather.7.rows_ref = bf16[1024,256]{1,0:T(8,128)(2,1)S(1)} all-gather(bf16[256,256]{1,0:T(8,128)(2,1)S(1)} %all_gather.6), channel_id=1, replica_groups={{0,32,64,96},{1,33,65,97},{2,34,66,98},{3,35,67,99},{4,36,68,100},{5,37..., dimensions={0}, use_global_device_ids=true | all-gather | bytes 655360 | tf_op jit(solution)/shard_map/all_gather | solution.py:367
  41.7 2.9 %shard_map.97 = (bf16[4,656,256]{2,1,0:T(8,128)(2,1)S(1)}, bf16[64,256]{1,0:T(8,128)(2,1)S(1)}) custom-call(bf16[528,256]{1,0:T(8,128)(2,1)S(1)} %copy-done.5, bf16[528,256]{1,0:T(8,128)(2,1)S(1)} %copy-done.7, bf16[528,256]{1,0:T(8,128)(2,1)} %collective-permute-done.1.refs_2_, bf16[528,256]{1,0:T(8,128)(2,1)} %collective-permute-done.2.refs_3_, ...), custom_call_target="tpu_custom_call" | custom-call | flops 1342177280 | bytes 6291456 | tf_op jit(solution)/shard_map/pallas_call | solution.py:50
  45.6 5.1 %all-to-all-start.1 = ((bf16[4,656,256]{2,1,0:T(8,128)(2,1)}), bf16[4,656,256]{2,1,0:T(8,128)(2,1)}, u32[]{:S(2)}, u32[]{:S(2)}) async-start(bf16[4,656,256]{2,1,0:T(8,128)(2,1)} %copy-done), calls=%async_computation.1 | async-start | bytes 2686976 | tf_op jit(solution)/shard_map/all_to_all | solution.py:348
  51.5 1.4 %collective-permute-start.4 = (bf16[512,256]{1,0:T(8,128)(2,1)S(1)}, bf16[512,256]{1,0:T(8,128)(2,1)}, u32[]{:S(2)}, u32[]{:S(2)}) collective-permute-start(bf16[512,256]{1,0:T(8,128)(2,1)S(1)} %shard_map.96.refs_0_), channel_id=1, source_target_pairs={{144,496},{145,497},{146,498},{147,499},{148,500},{149,501},{150,5... | collective-permute-start | bytes 786440 | tf_op jit(solution)/shard_map/ppermute | solution.py:372
  54.3 9.0 %all-to-all-done.1.parts_ref = bf16[4,656,256]{2,1,0:T(8,128)(2,1)} async-done(((bf16[4,656,256]{2,1,0:T(8,128)(2,1)}), bf16[4,656,256]{2,1,0:T(8,128)(2,1)}, u32[]{:S(2)}, u32[]{:S(2)}) %all-to-all-start.1) | async-done | bytes 1343520 | tf_op jit(solution)/shard_map/all_to_all | solution.py:348
  63.3 1.5 %shard_map.98 = (bf16[512,256]{1,0:T(8,128)(2,1)S(1)}, bf16[4,64,512]{2,1,0:T(8,128)(2,1)S(1)}) custom-call(bf16[4,656,256]{2,1,0:T(8,128)(2,1)} %all-to-all-done.1.parts_ref), custom_call_target="tpu_custom_call" | custom-call | flops 1048576 | bytes 2097152 | tf_op jit(solution)/shard_map/pallas_call | solution.py:50
  64.8 9.7 %all_to_all.25.keyval_ref = bf16[4,64,512]{2,1,0:T(8,128)(2,1)S(1)} all-to-all(bf16[4,64,512]{2,1,0:T(8,128)(2,1)S(1)} %get-tuple-element.28), channel_id=1, replica_groups={{0,1,2,3},{4,5,6,7},{8,9,10,11},{12,13,14,15},{16,17,18,19},{20,21,22,2..., dimensions={0} | all-to-all | bytes 524288 | tf_op jit(solution)/shard_map/all_to_all | solution.py:348
  74.6 2.0 %shard_map.99 = (bf16[512,256]{1,0:T(8,128)(2,1)}, bf16[512,256]{1,0:T(8,128)(2,1)S(1)}) custom-call(s32[32]{0:T(128)S(1)} %copy-done.3, bf16[512,256]{1,0:T(8,128)(2,1)S(1)} %bitcast.6, bf16[512,256]{1,0:T(8,128)(2,1)S(1)} %get-tuple-element.25.query_ref, bf16[4,64,512]{2,1,0:T(8,128)(2,1)S(1)} %all_to_all.25.keyval_ref, s32[32,512]{1,0:T(8,128)S(1)} %copy-done.2, ...), custom_call_target="tpu_custom_call" | custom-call | flops 134217728 | bytes 1048576 | tf_op jit(solution)/shard_map/pallas_call | solution.py:50
  76.6 2.3 %collective-permute-start.7 = (bf16[512,256]{1,0:T(8,128)(2,1)S(1)}, bf16[512,256]{1,0:T(8,128)(2,1)S(1)}, u32[]{:S(2)}, u32[]{:S(2)}) collective-permute-start(bf16[512,256]{1,0:T(8,128)(2,1)S(1)} %get-tuple-element.34), channel_id=1, source_target_pairs={{508,0},{509,1},{510,2},{511,3},{496,4},{497,5},{498,6},{499,7},{5... | collective-permute-start | bytes 786440 | tf_op jit(solution)/shard_map/ppermute | solution.py:383
  78.9 4.1 %collective-permute-start.8 = (bf16[512,256]{1,0:T(8,128)(2,1)S(1)}, bf16[512,256]{1,0:T(8,128)(2,1)S(1)}, u32[]{:S(2)}, u32[]{:S(2)}) collective-permute-start(bf16[512,256]{1,0:T(8,128)(2,1)S(1)} %get-tuple-element.34), channel_id=1, source_target_pairs={{504,0},{505,1},{506,2},{507,3},{508,4},{509,5},{510,6},{511,7},{4... | collective-permute-start | bytes 786440 | tf_op jit(solution)/shard_map/ppermute | solution.py:383
  83.1 4.5 %collective-permute-start.9 = (bf16[512,256]{1,0:T(8,128)(2,1)S(1)}, bf16[512,256]{1,0:T(8,128)(2,1)S(1)}, u32[]{:S(2)}, u32[]{:S(2)}) collective-permute-start(bf16[512,256]{1,0:T(8,128)(2,1)S(1)} %get-tuple-element.34), channel_id=1, source_target_pairs={{500,0},{501,1},{502,2},{503,3},{504,4},{505,5},{506,6},{507,7},{5... | collective-permute-start | bytes 786440 | tf_op jit(solution)/shard_map/ppermute | solution.py:383
  87.5 1.8 %collective-permute-done.6.refs_0_.x_ref = bf16[512,256]{1,0:T(8,128)(2,1)S(1)} collective-permute-done((bf16[512,256]{1,0:T(8,128)(2,1)S(1)}, bf16[512,256]{1,0:T(8,128)(2,1)S(1)}, u32[]{:S(2)}, u32[]{:S(2)}) %collective-permute-start.6) | collective-permute-done | bytes 262176 | tf_op jit(solution)/shard_map/ppermute | solution.py:383
  89.3 3.1 %collective-permute-done.7.refs_1_ = bf16[512,256]{1,0:T(8,128)(2,1)S(1)} collective-permute-done((bf16[512,256]{1,0:T(8,128)(2,1)S(1)}, bf16[512,256]{1,0:T(8,128)(2,1)S(1)}, u32[]{:S(2)}, u32[]{:S(2)}) %collective-permute-start.7) | collective-permute-done | bytes 262176 | tf_op jit(solution)/shard_map/ppermute | solution.py:383
  92.5 5.5 %collective-permute-done.8.refs_2_ = bf16[512,256]{1,0:T(8,128)(2,1)S(1)} collective-permute-done((bf16[512,256]{1,0:T(8,128)(2,1)S(1)}, bf16[512,256]{1,0:T(8,128)(2,1)S(1)}, u32[]{:S(2)}, u32[]{:S(2)}) %collective-permute-start.8) | collective-permute-done | bytes 262176 | tf_op jit(solution)/shard_map/ppermute | solution.py:383
  98.5 2.1 %shard_map.100 = bf16[4,656,256]{2,1,0:T(8,128)(2,1)S(1)} custom-call(bf16[512,256]{1,0:T(8,128)(2,1)S(1)} %collective-permute-done.6.refs_0_.x_ref, bf16[512,256]{1,0:T(8,128)(2,1)S(1)} %collective-permute-done.7.refs_1_, bf16[512,256]{1,0:T(8,128)(2,1)S(1)} %collective-permute-done.8.refs_2_, bf16[512,256]{1,0:T(8,128)(2,1)S(1)} %collective-permute-done.9.refs_3_, ...), custom_call_target="tpu_custom_call" | custom-call | flops 1342177280 | bytes 6291456 | tf_op jit(solution)/shard_map/pallas_call | solution.py:50
  100.7 14.9 %all_to_all.26.parts_ref = bf16[4,656,256]{2,1,0:T(8,128)(2,1)S(1)} all-to-all(bf16[4,656,256]{2,1,0:T(8,128)(2,1)S(1)} %shard_map.100), channel_id=1, replica_groups={{0,1,2,3},{4,5,6,7},{8,9,10,11},{12,13,14,15},{16,20,24,28},{17,21,25,2..., dimensions={0} | all-to-all | bytes 2686976 | tf_op jit(solution)/shard_map/all_to_all | solution.py:348
  115.8 9.1 %all_to_all.27.keyval_ref = bf16[4,64,512]{2,1,0:T(8,128)(2,1)S(1)} all-to-all(bf16[4,64,512]{2,1,0:T(8,128)(2,1)S(1)} %get-tuple-element.37), channel_id=1, replica_groups={{0,1,2,3},{4,5,6,7},{8,9,10,11},{12,13,14,15},{16,17,18,19},{20,21,22,2..., dimensions={0} | all-to-all | bytes 524288 | tf_op jit(solution)/shard_map/all_to_all | solution.py:348
  124.8 2.2 %shard_map.102 = bf16[512,256]{1,0:T(8,128)(2,1)} custom-call(s32[32]{0:T(128)S(1)} %copy-done.3, bf16[512,256]{1,0:T(8,128)(2,1)S(1)} %collective-permute-done.6.refs_0_.x_ref, bf16[512,256]{1,0:T(8,128)(2,1)S(1)} %get-tuple-element.36.query_ref, bf16[4,64,512]{2,1,0:T(8,128)(2,1)S(1)} %all_to_all.27.keyval_ref, s32[32,512]{1,0:T(8,128)S(1)} %copy-done.2), custom_call_target="tpu_custom_call" | custom-call | flops 134217728 | bytes 1048576 | tf_op jit(solution)/shard_map/pallas_call | solution.py:50
  (31 shorter events, 7.0 us)
Async XLA Ops:
  4.7 4.7 %copy-start.5 = (bf16[528,256]{1,0:T(8,128)(2,1)S(1)}, bf16[528,256]{1,0:T(8,128)(2,1)}, u32[]{:S(2)}) copy-start(bf16[528,256]{1,0:T(8,128)(2,1)} %get-tuple-element.20.refs_0_) | copy-start | bytes 811012
  4.7 16.3 %copy-start.8 = (bf16[128,256]{1,0:T(8,128)(2,1)S(1)}, bf16[128,256]{1,0:T(8,128)(2,1)}, u32[]{:S(2)}) copy-start(bf16[128,256]{1,0:T(8,128)(2,1)} %get-tuple-element.22) | copy-start | bytes 196612
  4.7 33.9 %copy-start.3 = (s32[32]{0:T(128)S(1)}, s32[32]{0:T(128)}, u32[]{:S(2)}) copy-start(s32[32]{0:T(128)} %lengths_ref.5) | copy-start | bytes 388
  4.7 33.9 %copy-start.4 = (s32[32]{0:T(128)S(1)}, s32[32]{0:T(128)}, u32[]{:S(2)}) copy-start(s32[32]{0:T(128)} %ids_ref.3) | copy-start | bytes 388
  4.8 35.2 %all-to-all-start = ((bf16[4,4,320,256]{3,2,1,0:T(8,128)(2,1)}), bf16[4,4,320,256]{3,2,1,0:T(8,128)(2,1)S(1)}, u32[]{:S(2)}, u32[]{:S(2)}) async-start(bf16[4,4,320,256]{3,2,1,0:T(8,128)(2,1)} %get-tuple-element.21), calls=%async_computation | async-start | bytes 5242880 | tf_op jit(solution)/shard_map/all_to_all | solution.py:348
  9.4 30.6 %collective-permute-start = (bf16[528,256]{1,0:T(8,128)(2,1)S(1)}, bf16[528,256]{1,0:T(8,128)(2,1)S(1)}, u32[]{:S(2)}, u32[]{:S(2)}) collective-permute-start(bf16[528,256]{1,0:T(8,128)(2,1)S(1)} %copy-done.5), channel_id=1, source_target_pairs={{12,0},{13,1},{14,2},{15,3},{0,4},{1,5},{2,6},{3,7},{4,8},{5,9},{6... | collective-permute-start | bytes 811016 | tf_op jit(solution)/shard_map/ppermute | solution.py:356
  16.3 24.4 %collective-permute-start.1 = (bf16[528,256]{1,0:T(8,128)(2,1)S(1)}, bf16[528,256]{1,0:T(8,128)(2,1)}, u32[]{:S(2)}, u32[]{:S(2)}) collective-permute-start(bf16[528,256]{1,0:T(8,128)(2,1)S(1)} %copy-done.5), channel_id=1, source_target_pairs={{8,0},{9,1},{10,2},{11,3},{12,4},{13,5},{14,6},{15,7},{0,8},{1,9},... | collective-permute-start | bytes 811016 | tf_op jit(solution)/shard_map/ppermute | solution.py:356
  18.3 22.4 %collective-permute-start.2 = (bf16[528,256]{1,0:T(8,128)(2,1)S(1)}, bf16[528,256]{1,0:T(8,128)(2,1)}, u32[]{:S(2)}, u32[]{:S(2)}) collective-permute-start(bf16[528,256]{1,0:T(8,128)(2,1)S(1)} %copy-done.5), channel_id=1, source_target_pairs={{4,0},{5,1},{6,2},{7,3},{8,4},{9,5},{10,6},{11,7},{12,8},{13,9},{1... | collective-permute-start | bytes 811016 | tf_op jit(solution)/shard_map/ppermute | solution.py:356
  40.0 0.7 copy-start.6
  40.7 1.0 copy-start.7
  44.6 1.1 copy-start
  45.6 17.6 %all-to-all-start.1 = ((bf16[4,656,256]{2,1,0:T(8,128)(2,1)}), bf16[4,656,256]{2,1,0:T(8,128)(2,1)}, u32[]{:S(2)}, u32[]{:S(2)}) async-start(bf16[4,656,256]{2,1,0:T(8,128)(2,1)} %copy-done), calls=%async_computation.1 | async-start | bytes 2686976 | tf_op jit(solution)/shard_map/all_to_all | solution.py:348
  50.7 23.9 %copy-start.1 = (bf16[1,512,256]{2,1,0:T(8,128)(2,1)S(1)}, bf16[1,512,256]{2,1,0:T(8,128)(2,1)}, u32[]{:S(2)}) copy-start(bf16[1,512,256]{2,1,0:T(8,128)(2,1)} %param.8) | copy-start | bytes 786436
  50.7 23.9 %copy-start.2 = (s32[32,512]{1,0:T(8,128)S(1)}, s32[32,512]{1,0:T(8,128)}, u32[]{:S(2)}) copy-start(s32[32,512]{1,0:T(8,128)} %segments_ref.3) | copy-start | bytes 196612
  50.7 14.1 %collective-permute-start.3 = (bf16[512,256]{1,0:T(8,128)(2,1)S(1)}, bf16[512,256]{1,0:T(8,128)(2,1)S(1)}, u32[]{:S(2)}, u32[]{:S(2)}) collective-permute-start(bf16[512,256]{1,0:T(8,128)(2,1)S(1)} %shard_map.96.refs_0_), channel_id=1, source_target_pairs={{16,496},{17,497},{18,498},{19,499},{20,500},{21,501},{22,502},{23... | collective-permute-start | bytes 786440 | tf_op jit(solution)/shard_map/ppermute | solution.py:372
  51.5 13.3 %collective-permute-start.4 = (bf16[512,256]{1,0:T(8,128)(2,1)S(1)}, bf16[512,256]{1,0:T(8,128)(2,1)}, u32[]{:S(2)}, u32[]{:S(2)}) collective-permute-start(bf16[512,256]{1,0:T(8,128)(2,1)S(1)} %shard_map.96.refs_0_), channel_id=1, source_target_pairs={{144,496},{145,497},{146,498},{147,499},{148,500},{149,501},{150,5... | collective-permute-start | bytes 786440 | tf_op jit(solution)/shard_map/ppermute | solution.py:372
  52.9 11.9 %collective-permute-start.5 = (bf16[512,256]{1,0:T(8,128)(2,1)S(1)}, bf16[512,256]{1,0:T(8,128)(2,1)}, u32[]{:S(2)}, u32[]{:S(2)}) collective-permute-start(bf16[512,256]{1,0:T(8,128)(2,1)S(1)} %shard_map.96.refs_0_), channel_id=1, source_target_pairs={{368,496},{369,497},{370,498},{371,499},{372,500},{373,501},{374,5... | collective-permute-start | bytes 786440 | tf_op jit(solution)/shard_map/ppermute | solution.py:372
  76.6 12.7 %collective-permute-start.6 = (bf16[512,256]{1,0:T(8,128)(2,1)S(1)}, bf16[512,256]{1,0:T(8,128)(2,1)S(1)}, u32[]{:S(2)}, u32[]{:S(2)}) collective-permute-start(bf16[512,256]{1,0:T(8,128)(2,1)S(1)} %get-tuple-element.34), channel_id=1, source_target_pairs={{496,0},{497,1},{498,2},{499,3},{500,4},{501,5},{502,6},{503,7},{5... | collective-permute-start | bytes 786440 | tf_op jit(solution)/shard_map/ppermute | solution.py:383
  76.6 15.8 %collective-permute-start.7 = (bf16[512,256]{1,0:T(8,128)(2,1)S(1)}, bf16[512,256]{1,0:T(8,128)(2,1)S(1)}, u32[]{:S(2)}, u32[]{:S(2)}) collective-permute-start(bf16[512,256]{1,0:T(8,128)(2,1)S(1)} %get-tuple-element.34), channel_id=1, source_target_pairs={{508,0},{509,1},{510,2},{511,3},{496,4},{497,5},{498,6},{499,7},{5... | collective-permute-start | bytes 786440 | tf_op jit(solution)/shard_map/ppermute | solution.py:383
  78.9 19.0 %collective-permute-start.8 = (bf16[512,256]{1,0:T(8,128)(2,1)S(1)}, bf16[512,256]{1,0:T(8,128)(2,1)S(1)}, u32[]{:S(2)}, u32[]{:S(2)}) collective-permute-start(bf16[512,256]{1,0:T(8,128)(2,1)S(1)} %get-tuple-element.34), channel_id=1, source_target_pairs={{504,0},{505,1},{506,2},{507,3},{508,4},{509,5},{510,6},{511,7},{4... | collective-permute-start | bytes 786440 | tf_op jit(solution)/shard_map/ppermute | solution.py:383
  83.1 15.5 %collective-permute-start.9 = (bf16[512,256]{1,0:T(8,128)(2,1)S(1)}, bf16[512,256]{1,0:T(8,128)(2,1)S(1)}, u32[]{:S(2)}, u32[]{:S(2)}) collective-permute-start(bf16[512,256]{1,0:T(8,128)(2,1)S(1)} %get-tuple-element.34), channel_id=1, source_target_pairs={{500,0},{501,1},{502,2},{503,3},{504,4},{505,5},{506,6},{507,7},{5... | collective-permute-start | bytes 786440 | tf_op jit(solution)/shard_map/ppermute | solution.py:383

commit v6 on v5

--- a/solution.py
+++ b/solution.py
@@ -291,20 +291,24 @@
     )
 
 
-def frame_body(ids_ref, lengths_ref, rows_ref, out_ref, starts, counts, hits_ref):
-    base = lax.div(lax.axis_index("section"), NEAR) * NEAR
+def frame_body(ids_ref, lengths_ref, *refs):
+    pair_refs, (out_ref, starts, counts, rows_ref, hits_ref) = refs[: NEAR // 2], refs[NEAR // 2 :]
+    section = lax.axis_index("section")
     for n in range(NEAR):
         starts[n] = 0
         counts[n] = 0
+    for n, ref in enumerate(pair_refs):
+        rows_ref[2 * n * ROW_MAX : 2 * (n + 1) * ROW_MAX] = ref[...]
 
     def note(k, start):
         length = lengths_ref[k]
-        host = lax.div(ids_ref[k], HOST_ROWS) - base
-
-        @pl.when((host >= 0) & (host < NEAR))
+        behind = section - lax.div(ids_ref[k], HOST_ROWS)
+
+        @pl.when((behind >= 0) & (behind < NEAR))
         def _():
-            starts[host] = start
-            counts[host] = length
+            spot = behind + 1 - 2 * (behind % 2)
+            starts[spot] = start
+            counts[spot] = length
 
         return start + length
 
@@ -323,16 +327,26 @@
     return call(
         frame_body,
         jax.ShapeDtypeStruct((TOKENS, BLOCK), bf16),
-        (row_ids, row_lengths, rows),
-        [SMEM, SMEM, VMEM],
+        (row_ids, row_lengths, *rows),
+        [SMEM, SMEM] + [VMEM] * (NEAR // 2),
         2 * TOKENS * NEAR * 128 * 256,
         1 << 20,
         scratch_shapes=[
             pltpu.SMEM((NEAR,), jnp.int32),
             pltpu.SMEM((NEAR,), jnp.int32),
+            pltpu.VMEM((NEAR * ROW_MAX, BLOCK), bf16),
             pltpu.VMEM((TOKENS, NEAR * ROW_MAX), bf16),
         ],
     )
+
+
+def bring(array, sections, step, count):
+    last, span = sections - 1, (count + 1) * step
+    got = []
+    for n in range(1, count + 1):
+        route = [(i - n * step, i) for i in range(sections) if (last - i) % span == 0]
+        got.append(lax.ppermute(array, "section", route))
+    return got
 
 
 def per_device(activations, gain, w_query, w_kv, segments, pool, row_ids, row_lengths):
@@ -355,21 +369,12 @@
         route = [(number(s, a - d, b, s), number(s, a, b, s)) for s, a, b in grid]
         blocks.append(lax.ppermute(own, AXES, route))
 
-    tensors = range(SIDE * SIDE)
-    pairs = [[(s + c) * SIDE * SIDE + t for c in range(2)] for s in range(0, sections, 2) for t in tensors]
-    fours = [
-        [(s + c + 2 * z) * SIDE * SIDE + t for z in range(NEAR // 2)]
-        for s in range(0, sections, NEAR)
-        for c in range(2)
-        for t in tensors
-    ]
-    rows = lax.all_gather(row, AXES, axis=0, axis_index_groups=pairs, tiled=True)
-    rows = lax.all_gather(rows, AXES, axis=0, axis_index_groups=fours, tiled=True)
-    frame = make_frame(row_ids, row_lengths, rows)
+    pair = jnp.concatenate([*bring(row, sections, 1, 1), row], axis=0)
+    blocks[SIDE - 1], pair = barrier((blocks[SIDE - 1], pair))
+    pairs = [pair, *bring(pair, sections, 2, NEAR // 2 - 1)]
+    frame = make_frame(row_ids, row_lengths, pairs)
     weights, frame = barrier((weights, frame))
-    last = sections - 1
-    sources = [1 if n == 0 else (n * NEAR + 1 if 2 * n < sections // NEAR else n * NEAR + NEAR - 1) for n in range(last // NEAR)]
-    frames = [frame, *[lax.ppermute(frame, "section", [(source, last)]) for source in sources]]
+    frames = [frame, *bring(frame, sections, NEAR, sections // NEAR - 1)]
 
     parts, gains = project(False, blocks, [], weights)
     parts = exchange(parts, ring_b)

time: 129 us -> 126 us (0.977)
  blocking collectives: 51.3 us -> 34.2 us
  waiting for transfers between devices: 20 us -> 30 us
  starting transfers between devices: 35.8 us -> 41 us
    all_gather x2 -> x0, blocking collectives: 17.6 us -> none  [the longest x1 15.7 us: per_device(): lax.all_gather(rows, AXES, axis=0, axis_index_groups=fours, tiled=True)]
    all_to_all x2, waiting for transfers between devices: 9.01 us -> 16 us  [exchange(): return lax.all_to_all(array, AXES, 0, 0, axis_index_groups=ring)]
    ppermute x3 -> x7, starting transfers between devices: 3.55 us -> 8.92 us  [bring(): got.append(lax.ppermute(array, 'section', route))]
    ppermute x4, starting transfers between devices: 10.9 us -> 13.1 us  [per_device(): blocks.append(lax.ppermute(sent, AXES, route))]
    ppermute x4, waiting for transfers between devices: 11 us -> 13.1 us  [per_device(): blocks.append(lax.ppermute(sent, AXES, route))]
    ppermute x3, starting transfers between devices: 11.7 us -> 10.2 us  [per_device(): blocks.append(lax.ppermute(own, AXES, route))]
  transfers between devices with their start and end apart: 12 -> 16, of which waited for: 5 -> 7; matrix products, arithmetic and copies ran while one was open for 0% -> 0% of each run, Pallas kernels for 2% -> 2%
where the time goes in v6:
time: 126 us; the launch traced here: 125 us
  starting transfers between devices  41 us (33%)
  blocking collectives  34.2 us (27%)
  waiting for transfers between devices  30 us (24%)
  Pallas kernels  16.7 us (13%)
  local copies, waits for them, and re-layouts  2.07 us (2%)
    all_to_all x3, blocking collectives, exchange(): return lax.all_to_all(array, AXES, 0, 0, axis_index_groups=ring)  34.2 us
    all_to_all x2, waiting for transfers between devices, exchange(): return lax.all_to_all(array, AXES, 0, 0, axis_index_groups=ring)  16 us
    ppermute x4, starting transfers between devices, per_device(): blocks.append(lax.ppermute(sent, AXES, route))  13.1 us
    ppermute x4, waiting for transfers between devices, per_device(): blocks.append(lax.ppermute(sent, AXES, route))  13.1 us
    pallas_call x7, Pallas kernels, call(): pl.pallas_call(body, out_shape=out_shape, in_specs=specs, out_specs=jax.t...  12.6 us
    ppermute x3, starting transfers between devices, per_device(): blocks.append(lax.ppermute(own, AXES, route))  10.2 us
    ppermute x7, starting transfers between devices, bring(): got.append(lax.ppermute(array, 'section', route))  8.92 us
    all_to_all x2, starting transfers between devices, exchange(): return lax.all_to_all(array, AXES, 0, 0, axis_index_groups=ring)  8.9 us
  transfers between devices with their start and end apart: 16, of which 7 were waited for; matrix products, arithmetic and copies ran while one was open for 0% of the time, Pallas kernels for 2%

profile of v6, /device:TPU:6, one launch (start us, length us, event | category | flops | bytes accessed | tf_op | source)
XLA Modules:
  0.0 125.0 jit_solution(2709790348955417857)
XLA Ops:
  0.6 4.1 %shard_map.95 = (bf16[4,4,320,256]{3,2,1,0:T(8,128)(2,1)}, bf16[528,256]{1,0:T(8,128)(2,1)}, bf16[128,256]{1,0:T(8,128)(2,1)}) custom-call(s32[32]{0:T(128)} %ids_ref.3, bf16[512,256]{1,0:T(8,128)(2,1)} %bitcast.5, bf16[1,256]{1,0:T(2,128)(2,1)} %gain_ref.1, bf16[4096,256]{1,0:T(8,128)(2,1)} %bitcast.7, bf16[64,4096]{1,0:T(8,128)(2,1)} %bitcast.8, ...), custom_call_target="tpu_custom_call" | custom-call | bytes 6291456 | tf_op jit(solution)/shard_map/pallas_call | solution.py:99
  4.8 4.6 %all-to-all-start = ((bf16[4,4,320,256]{3,2,1,0:T(8,128)(2,1)}), bf16[4,4,320,256]{3,2,1,0:T(8,128)(2,1)S(1)}, u32[]{:S(2)}, u32[]{:S(2)}) async-start(bf16[4,4,320,256]{3,2,1,0:T(8,128)(2,1)} %get-tuple-element.25), calls=%async_computation | async-start | bytes 5242880 | tf_op jit(solution)/shard_map/all_to_all | solution.py:362
  9.4 2.7 %collective-permute-start.2 = (bf16[528,256]{1,0:T(8,128)(2,1)S(1)}, bf16[528,256]{1,0:T(8,128)(2,1)S(1)}, u32[]{:S(2)}, u32[]{:S(2)}) collective-permute-start(bf16[528,256]{1,0:T(8,128)(2,1)S(1)} %copy-done.5), channel_id=1, source_target_pairs={{4,0},{5,1},{6,2},{7,3},{8,4},{9,5},{10,6},{11,7},{12,8},{13,9},{1... | collective-permute-start | bytes 811016 | tf_op jit(solution)/shard_map/ppermute | solution.py:370
  12.1 3.4 %collective-permute-start.3 = (bf16[128,256]{1,0:T(8,128)(2,1)S(1)}, bf16[128,256]{1,0:T(8,128)(2,1)S(1)}, u32[]{:S(2)}, u32[]{:S(2)}) collective-permute-start(bf16[128,256]{1,0:T(8,128)(2,1)S(1)} %copy-done.8), channel_id=1, source_target_pairs={{0,16},{32,48},{64,80},{96,112},{128,144},{160,176},{192,208},{224... | collective-permute-start | bytes 196616 | tf_op jit(solution)/shard_map/ppermute | solution.py:348
  15.5 4.1 %collective-permute-start = (bf16[528,256]{1,0:T(8,128)(2,1)S(1)}, bf16[528,256]{1,0:T(8,128)(2,1)}, u32[]{:S(2)}, u32[]{:S(2)}) collective-permute-start(bf16[528,256]{1,0:T(8,128)(2,1)S(1)} %copy-done.5), channel_id=1, source_target_pairs={{12,0},{13,1},{14,2},{15,3},{0,4},{1,5},{2,6},{3,7},{4,8},{5,9},{6... | collective-permute-start | bytes 811016 | tf_op jit(solution)/shard_map/ppermute | solution.py:370
  19.6 3.4 %collective-permute-start.1 = (bf16[528,256]{1,0:T(8,128)(2,1)S(1)}, bf16[528,256]{1,0:T(8,128)(2,1)}, u32[]{:S(2)}, u32[]{:S(2)}) collective-permute-start(bf16[528,256]{1,0:T(8,128)(2,1)S(1)} %copy-done.5), channel_id=1, source_target_pairs={{8,0},{9,1},{10,2},{11,3},{12,4},{13,5},{14,6},{15,7},{0,8},{1,9},... | collective-permute-start | bytes 811016 | tf_op jit(solution)/shard_map/ppermute | solution.py:370
  27.5 7.0 %all-to-all-done.refs_4_.refs_5_ = bf16[4,4,320,256]{3,2,1,0:T(8,128)(2,1)S(1)} async-done(((bf16[4,4,320,256]{3,2,1,0:T(8,128)(2,1)}), bf16[4,4,320,256]{3,2,1,0:T(8,128)(2,1)S(1)}, u32[]{:S(2)}, u32[]{:S(2)}) %all-to-all-start) | async-done | bytes 2621472 | tf_op jit(solution)/shard_map/all_to_all | solution.py:362
  35.5 3.0 %shard_map.97 = (bf16[4,656,256]{2,1,0:T(8,128)(2,1)S(1)}, bf16[64,256]{1,0:T(8,128)(2,1)S(1)}) custom-call(bf16[528,256]{1,0:T(8,128)(2,1)S(1)} %copy-done.5, bf16[528,256]{1,0:T(8,128)(2,1)} %collective-permute-done.refs_1_, bf16[528,256]{1,0:T(8,128)(2,1)} %collective-permute-done.1.refs_2_, bf16[528,256]{1,0:T(8,128)(2,1)S(1)} %copy-done.7, ...), custom_call_target="tpu_custom_call" | custom-call | flops 1342177280 | bytes 6291456 | tf_op jit(solution)/shard_map/pallas_call | solution.py:50
  39.6 4.3 %all-to-all-start.1 = ((bf16[4,656,256]{2,1,0:T(8,128)(2,1)}), bf16[4,656,256]{2,1,0:T(8,128)(2,1)}, u32[]{:S(2)}, u32[]{:S(2)}) async-start(bf16[4,656,256]{2,1,0:T(8,128)(2,1)} %copy-done), calls=%async_computation.1 | async-start | bytes 2686976 | tf_op jit(solution)/shard_map/all_to_all | solution.py:362
  47.5 9.0 %all-to-all-done.1.parts_ref = bf16[4,656,256]{2,1,0:T(8,128)(2,1)} async-done(((bf16[4,656,256]{2,1,0:T(8,128)(2,1)}), bf16[4,656,256]{2,1,0:T(8,128)(2,1)}, u32[]{:S(2)}, u32[]{:S(2)}) %all-to-all-start.1) | async-done | bytes 1343520 | tf_op jit(solution)/shard_map/all_to_all | solution.py:362
  56.4 1.5 %shard_map.98 = (bf16[512,256]{1,0:T(8,128)(2,1)S(1)}, bf16[4,64,512]{2,1,0:T(8,128)(2,1)S(1)}) custom-call(bf16[4,656,256]{2,1,0:T(8,128)(2,1)} %all-to-all-done.1.parts_ref), custom_call_target="tpu_custom_call" | custom-call | flops 1048576 | bytes 2097152 | tf_op jit(solution)/shard_map/pallas_call | solution.py:50
  58.0 9.1 %all_to_all.25.keyval_ref = bf16[4,64,512]{2,1,0:T(8,128)(2,1)S(1)} all-to-all(bf16[4,64,512]{2,1,0:T(8,128)(2,1)S(1)} %get-tuple-element.32), channel_id=1, replica_groups={{0,1,2,3},{4,5,6,7},{8,9,10,11},{12,13,14,15},{16,17,18,19},{20,21,22,2..., dimensions={0} | all-to-all | bytes 524288 | tf_op jit(solution)/shard_map/all_to_all | solution.py:362
  67.1 2.0 %shard_map.99 = (bf16[512,256]{1,0:T(8,128)(2,1)}, bf16[512,256]{1,0:T(8,128)(2,1)S(1)}) custom-call(s32[32]{0:T(128)S(1)} %copy-done.3, bf16[512,256]{1,0:T(8,128)(2,1)S(1)} %bitcast.6, bf16[512,256]{1,0:T(8,128)(2,1)S(1)} %get-tuple-element.29.query_ref, bf16[4,64,512]{2,1,0:T(8,128)(2,1)S(1)} %all_to_all.25.keyval_ref, s32[32,512]{1,0:T(8,128)S(1)} %copy-done.2, ...), custom_call_target="tpu_custom_call" | custom-call | flops 134217728 | bytes 1048576 | tf_op jit(solution)/shard_map/pallas_call | solution.py:50
  69.1 4.1 %collective-permute-start.11 = (bf16[512,256]{1,0:T(8,128)(2,1)S(1)}, bf16[512,256]{1,0:T(8,128)(2,1)S(1)}, u32[]{:S(2)}, u32[]{:S(2)}) collective-permute-start(bf16[512,256]{1,0:T(8,128)(2,1)S(1)} %get-tuple-element.38), channel_id=1, source_target_pairs={{508,0},{509,1},{510,2},{511,3},{496,4},{497,5},{498,6},{499,7},{5... | collective-permute-start | bytes 786440 | tf_op jit(solution)/shard_map/ppermute | solution.py:388
  73.2 2.2 %collective-permute-start.12 = (bf16[512,256]{1,0:T(8,128)(2,1)S(1)}, bf16[512,256]{1,0:T(8,128)(2,1)S(1)}, u32[]{:S(2)}, u32[]{:S(2)}) collective-permute-start(bf16[512,256]{1,0:T(8,128)(2,1)S(1)} %get-tuple-element.38), channel_id=1, source_target_pairs={{504,0},{505,1},{506,2},{507,3},{508,4},{509,5},{510,6},{511,7},{4... | collective-permute-start | bytes 786440 | tf_op jit(solution)/shard_map/ppermute | solution.py:388
  75.4 6.8 %collective-permute-start.13 = (bf16[512,256]{1,0:T(8,128)(2,1)S(1)}, bf16[512,256]{1,0:T(8,128)(2,1)S(1)}, u32[]{:S(2)}, u32[]{:S(2)}) collective-permute-start(bf16[512,256]{1,0:T(8,128)(2,1)S(1)} %get-tuple-element.38), channel_id=1, source_target_pairs={{500,0},{501,1},{502,2},{503,3},{504,4},{505,5},{506,6},{507,7},{5... | collective-permute-start | bytes 786440 | tf_op jit(solution)/shard_map/ppermute | solution.py:388
  82.2 3.6 %collective-permute-done.10.refs_0_.x_ref = bf16[512,256]{1,0:T(8,128)(2,1)S(1)} collective-permute-done((bf16[512,256]{1,0:T(8,128)(2,1)S(1)}, bf16[512,256]{1,0:T(8,128)(2,1)S(1)}, u32[]{:S(2)}, u32[]{:S(2)}) %collective-permute-start.10) | collective-permute-done | bytes 262176 | tf_op jit(solution)/shard_map/ppermute | solution.py:388
  85.8 3.1 %collective-permute-done.11.refs_1_ = bf16[512,256]{1,0:T(8,128)(2,1)S(1)} collective-permute-done((bf16[512,256]{1,0:T(8,128)(2,1)S(1)}, bf16[512,256]{1,0:T(8,128)(2,1)S(1)}, u32[]{:S(2)}, u32[]{:S(2)}) %collective-permute-start.11) | collective-permute-done | bytes 262176 | tf_op jit(solution)/shard_map/ppermute | solution.py:388
  88.9 4.5 %collective-permute-done.12.refs_2_ = bf16[512,256]{1,0:T(8,128)(2,1)S(1)} collective-permute-done((bf16[512,256]{1,0:T(8,128)(2,1)S(1)}, bf16[512,256]{1,0:T(8,128)(2,1)S(1)}, u32[]{:S(2)}, u32[]{:S(2)}) %collective-permute-start.12) | collective-permute-done | bytes 262176 | tf_op jit(solution)/shard_map/ppermute | solution.py:388
  93.5 1.8 %collective-permute-done.13.refs_3_ = bf16[512,256]{1,0:T(8,128)(2,1)S(1)} collective-permute-done((bf16[512,256]{1,0:T(8,128)(2,1)S(1)}, bf16[512,256]{1,0:T(8,128)(2,1)S(1)}, u32[]{:S(2)}, u32[]{:S(2)}) %collective-permute-start.13) | collective-permute-done | bytes 262176 | tf_op jit(solution)/shard_map/ppermute | solution.py:388
  95.3 2.1 %shard_map.100 = bf16[4,656,256]{2,1,0:T(8,128)(2,1)S(1)} custom-call(bf16[512,256]{1,0:T(8,128)(2,1)S(1)} %collective-permute-done.10.refs_0_.x_ref, bf16[512,256]{1,0:T(8,128)(2,1)S(1)} %collective-permute-done.11.refs_1_, bf16[512,256]{1,0:T(8,128)(2,1)S(1)} %collective-permute-done.12.refs_2_, bf16[512,256]{1,0:T(8,128)(2,1)S(1)} %collective-permute-done.13.refs_3_, ...), custom_call_target="tpu_custom_call" | custom-call | flops 1342177280 | bytes 6291456 | tf_op jit(solution)/shard_map/pallas_call | solution.py:50
  97.4 16.0 %all_to_all.26.parts_ref = bf16[4,656,256]{2,1,0:T(8,128)(2,1)S(1)} all-to-all(bf16[4,656,256]{2,1,0:T(8,128)(2,1)S(1)} %shard_map.100), channel_id=1, replica_groups={{0,1,2,3},{4,5,6,7},{8,9,10,11},{12,13,14,15},{16,20,24,28},{17,21,25,2..., dimensions={0} | all-to-all | bytes 2686976 | tf_op jit(solution)/shard_map/all_to_all | solution.py:362
  113.6 9.1 %all_to_all.27.keyval_ref = bf16[4,64,512]{2,1,0:T(8,128)(2,1)S(1)} all-to-all(bf16[4,64,512]{2,1,0:T(8,128)(2,1)S(1)} %get-tuple-element.41), channel_id=1, replica_groups={{0,1,2,3},{4,5,6,7},{8,9,10,11},{12,13,14,15},{16,17,18,19},{20,21,22,2..., dimensions={0} | all-to-all | bytes 524288 | tf_op jit(solution)/shard_map/all_to_all | solution.py:362
  122.7 2.2 %shard_map.102 = bf16[512,256]{1,0:T(8,128)(2,1)} custom-call(s32[32]{0:T(128)S(1)} %copy-done.3, bf16[512,256]{1,0:T(8,128)(2,1)S(1)} %collective-permute-done.10.refs_0_.x_ref, bf16[512,256]{1,0:T(8,128)(2,1)S(1)} %get-tuple-element.40.query_ref, bf16[4,64,512]{2,1,0:T(8,128)(2,1)S(1)} %all_to_all.27.keyval_ref, s32[32,512]{1,0:T(8,128)S(1)} %copy-done.2), custom_call_target="tpu_custom_call" | custom-call | flops 134217728 | bytes 1048576 | tf_op jit(solution)/shard_map/pallas_call | solution.py:50
  (38 shorter events, 10.3 us)
Async XLA Ops:
  4.7 4.7 %copy-start.5 = (bf16[528,256]{1,0:T(8,128)(2,1)S(1)}, bf16[528,256]{1,0:T(8,128)(2,1)}, u32[]{:S(2)}) copy-start(bf16[528,256]{1,0:T(8,128)(2,1)} %get-tuple-element.22.refs_0_) | copy-start | bytes 811012
  4.7 7.4 %copy-start.8 = (bf16[128,256]{1,0:T(8,128)(2,1)S(1)}, bf16[128,256]{1,0:T(8,128)(2,1)}, u32[]{:S(2)}) copy-start(bf16[128,256]{1,0:T(8,128)(2,1)} %get-tuple-element.23) | copy-start | bytes 196612
  4.8 21.3 %copy-start.3 = (s32[32]{0:T(128)S(1)}, s32[32]{0:T(128)}, u32[]{:S(2)}) copy-start(s32[32]{0:T(128)} %lengths_ref.5) | copy-start | bytes 388
  4.8 21.3 %copy-start.4 = (s32[32]{0:T(128)S(1)}, s32[32]{0:T(128)}, u32[]{:S(2)}) copy-start(s32[32]{0:T(128)} %ids_ref.3) | copy-start | bytes 388
  4.8 29.7 %all-to-all-start = ((bf16[4,4,320,256]{3,2,1,0:T(8,128)(2,1)}), bf16[4,4,320,256]{3,2,1,0:T(8,128)(2,1)S(1)}, u32[]{:S(2)}, u32[]{:S(2)}) async-start(bf16[4,4,320,256]{3,2,1,0:T(8,128)(2,1)} %get-tuple-element.25), calls=%async_computation | async-start | bytes 5242880 | tf_op jit(solution)/shard_map/all_to_all | solution.py:362
  9.4 14.6 %collective-permute-start.2 = (bf16[528,256]{1,0:T(8,128)(2,1)S(1)}, bf16[528,256]{1,0:T(8,128)(2,1)S(1)}, u32[]{:S(2)}, u32[]{:S(2)}) collective-permute-start(bf16[528,256]{1,0:T(8,128)(2,1)S(1)} %copy-done.5), channel_id=1, source_target_pairs={{4,0},{5,1},{6,2},{7,3},{8,4},{9,5},{10,6},{11,7},{12,8},{13,9},{1... | collective-permute-start | bytes 811016 | tf_op jit(solution)/shard_map/ppermute | solution.py:370
  12.1 10.9 %collective-permute-start.3 = (bf16[128,256]{1,0:T(8,128)(2,1)S(1)}, bf16[128,256]{1,0:T(8,128)(2,1)S(1)}, u32[]{:S(2)}, u32[]{:S(2)}) collective-permute-start(bf16[128,256]{1,0:T(8,128)(2,1)S(1)} %copy-done.8), channel_id=1, source_target_pairs={{0,16},{32,48},{64,80},{96,112},{128,144},{160,176},{192,208},{224... | collective-permute-start | bytes 196616 | tf_op jit(solution)/shard_map/ppermute | solution.py:348
  15.5 19.0 %collective-permute-start = (bf16[528,256]{1,0:T(8,128)(2,1)S(1)}, bf16[528,256]{1,0:T(8,128)(2,1)}, u32[]{:S(2)}, u32[]{:S(2)}) collective-permute-start(bf16[528,256]{1,0:T(8,128)(2,1)S(1)} %copy-done.5), channel_id=1, source_target_pairs={{12,0},{13,1},{14,2},{15,3},{0,4},{1,5},{2,6},{3,7},{4,8},{5,9},{6... | collective-permute-start | bytes 811016 | tf_op jit(solution)/shard_map/ppermute | solution.py:370
  19.6 14.9 %collective-permute-start.1 = (bf16[528,256]{1,0:T(8,128)(2,1)S(1)}, bf16[528,256]{1,0:T(8,128)(2,1)}, u32[]{:S(2)}, u32[]{:S(2)}) collective-permute-start(bf16[528,256]{1,0:T(8,128)(2,1)S(1)} %copy-done.5), channel_id=1, source_target_pairs={{8,0},{9,1},{10,2},{11,3},{12,4},{13,5},{14,6},{15,7},{0,8},{1,9},... | collective-permute-start | bytes 811016 | tf_op jit(solution)/shard_map/ppermute | solution.py:370
  24.0 10.5 %copy-start.6 = (bf16[528,256]{1,0:T(8,128)(2,1)}, bf16[528,256]{1,0:T(8,128)(2,1)S(1)}, u32[]{:S(2)}) copy-start(bf16[528,256]{1,0:T(8,128)(2,1)S(1)} %collective-permute-done.2.refs_3_) | copy-start | bytes 811012
  24.0 2.0 %collective-permute-start.4 = (bf16[256,256]{1,0:T(8,128)(2,1)S(1)}, bf16[256,256]{1,0:T(8,128)(2,1)S(1)}, u32[]{:S(2)}, u32[]{:S(2)}) collective-permute-start(bf16[256,256]{1,0:T(8,128)(2,1)S(1)} %pad_maximum_fusion.refs_0_), channel_id=1, source_target_pairs={{80,112},{208,240},{336,368},{464,496},{81,113},{209,241},{337,369... | collective-permute-start | bytes 393224 | tf_op jit(solution)/shard_map/ppermute | solution.py:348
  24.6 1.4 %collective-permute-start.5 = (bf16[256,256]{1,0:T(8,128)(2,1)S(1)}, bf16[256,256]{1,0:T(8,128)(2,1)S(1)}, u32[]{:S(2)}, u32[]{:S(2)}) collective-permute-start(bf16[256,256]{1,0:T(8,128)(2,1)S(1)} %pad_maximum_fusion.refs_0_), channel_id=1, source_target_pairs={{48,112},{176,240},{304,368},{432,496},{49,113},{177,241},{305,369... | collective-permute-start | bytes 393224 | tf_op jit(solution)/shard_map/ppermute | solution.py:348
  25.3 0.7 collective-permute-start.6
  38.5 1.1 copy-start
  39.6 16.8 %all-to-all-start.1 = ((bf16[4,656,256]{2,1,0:T(8,128)(2,1)}), bf16[4,656,256]{2,1,0:T(8,128)(2,1)}, u32[]{:S(2)}, u32[]{:S(2)}) async-start(bf16[4,656,256]{2,1,0:T(8,128)(2,1)} %copy-done), calls=%async_computation.1 | async-start | bytes 2686976 | tf_op jit(solution)/shard_map/all_to_all | solution.py:362
  43.9 23.2 %copy-start.1 = (bf16[1,512,256]{2,1,0:T(8,128)(2,1)S(1)}, bf16[1,512,256]{2,1,0:T(8,128)(2,1)}, u32[]{:S(2)}) copy-start(bf16[1,512,256]{2,1,0:T(8,128)(2,1)} %param.8) | copy-start | bytes 786436
  43.9 23.1 %copy-start.2 = (s32[32,512]{1,0:T(8,128)S(1)}, s32[32,512]{1,0:T(8,128)}, u32[]{:S(2)}) copy-start(s32[32,512]{1,0:T(8,128)} %segments_ref.3) | copy-start | bytes 196612
  43.9 14.0 %collective-permute-start.7 = (bf16[512,256]{1,0:T(8,128)(2,1)S(1)}, bf16[512,256]{1,0:T(8,128)(2,1)S(1)}, u32[]{:S(2)}, u32[]{:S(2)}) collective-permute-start(bf16[512,256]{1,0:T(8,128)(2,1)S(1)} %shard_map.96.refs_0_), channel_id=1, source_target_pairs={{368,496},{369,497},{370,498},{371,499},{372,500},{373,501},{374,5... | collective-permute-start | bytes 786440 | tf_op jit(solution)/shard_map/ppermute | solution.py:348
  44.7 13.2 %collective-permute-start.8 = (bf16[512,256]{1,0:T(8,128)(2,1)S(1)}, bf16[512,256]{1,0:T(8,128)(2,1)}, u32[]{:S(2)}, u32[]{:S(2)}) collective-permute-start(bf16[512,256]{1,0:T(8,128)(2,1)S(1)} %shard_map.96.refs_0_), channel_id=1, source_target_pairs={{240,496},{241,497},{242,498},{243,499},{244,500},{245,501},{246,5... | collective-permute-start | bytes 786440 | tf_op jit(solution)/shard_map/ppermute | solution.py:348
  46.1 11.9 %collective-permute-start.9 = (bf16[512,256]{1,0:T(8,128)(2,1)S(1)}, bf16[512,256]{1,0:T(8,128)(2,1)}, u32[]{:S(2)}, u32[]{:S(2)}) collective-permute-start(bf16[512,256]{1,0:T(8,128)(2,1)S(1)} %shard_map.96.refs_0_), channel_id=1, source_target_pairs={{112,496},{113,497},{114,498},{115,499},{116,500},{117,501},{118,5... | collective-permute-start | bytes 786440 | tf_op jit(solution)/shard_map/ppermute | solution.py:348
  69.1 16.7 %collective-permute-start.10 = (bf16[512,256]{1,0:T(8,128)(2,1)S(1)}, bf16[512,256]{1,0:T(8,128)(2,1)S(1)}, u32[]{:S(2)}, u32[]{:S(2)}) collective-permute-start(bf16[512,256]{1,0:T(8,128)(2,1)S(1)} %get-tuple-element.38), channel_id=1, source_target_pairs={{496,0},{497,1},{498,2},{499,3},{500,4},{501,5},{502,6},{503,7},{5... | collective-permute-start | bytes 786440 | tf_op jit(solution)/shard_map/ppermute | solution.py:388
  69.1 19.8 %collective-permute-start.11 = (bf16[512,256]{1,0:T(8,128)(2,1)S(1)}, bf16[512,256]{1,0:T(8,128)(2,1)S(1)}, u32[]{:S(2)}, u32[]{:S(2)}) collective-permute-start(bf16[512,256]{1,0:T(8,128)(2,1)S(1)} %get-tuple-element.38), channel_id=1, source_target_pairs={{508,0},{509,1},{510,2},{511,3},{496,4},{497,5},{498,6},{499,7},{5... | collective-permute-start | bytes 786440 | tf_op jit(solution)/shard_map/ppermute | solution.py:388
  73.2 20.3 %collective-permute-start.12 = (bf16[512,256]{1,0:T(8,128)(2,1)S(1)}, bf16[512,256]{1,0:T(8,128)(2,1)S(1)}, u32[]{:S(2)}, u32[]{:S(2)}) collective-permute-start(bf16[512,256]{1,0:T(8,128)(2,1)S(1)} %get-tuple-element.38), channel_id=1, source_target_pairs={{504,0},{505,1},{506,2},{507,3},{508,4},{509,5},{510,6},{511,7},{4... | collective-permute-start | bytes 786440 | tf_op jit(solution)/shard_map/ppermute | solution.py:388
  75.4 19.9 %collective-permute-start.13 = (bf16[512,256]{1,0:T(8,128)(2,1)S(1)}, bf16[512,256]{1,0:T(8,128)(2,1)S(1)}, u32[]{:S(2)}, u32[]{:S(2)}) collective-permute-start(bf16[512,256]{1,0:T(8,128)(2,1)S(1)} %get-tuple-element.38), channel_id=1, source_target_pairs={{500,0},{501,1},{502,2},{503,3},{504,4},{505,5},{506,6},{507,7},{5... | collective-permute-start | bytes 786440 | tf_op jit(solution)/shard_map/ppermute | solution.py:388
  (1 other events, 1.0 us)

commit v7 on v6

--- a/solution.py
+++ b/solution.py
@@ -46,13 +46,13 @@
     return [[(s * SIDE + g) * SIDE + i for i in range(SIDE)] for s in range(sections) for g in range(SIDE)]
 
 
-def call(body, out_shape, operands, specs, flops, moved, **more):
+def call(body, out_shape, operands, specs, flops, moved, vmem=12 << 20, **more):
     return pl.pallas_call(
         body,
         out_shape=out_shape,
         in_specs=specs,
         out_specs=jax.tree.map(lambda _: VMEM, out_shape),
-        compiler_params=pltpu.CompilerParams(vmem_limit_bytes=12 << 20),
+        compiler_params=pltpu.CompilerParams(vmem_limit_bytes=vmem),
         cost_estimate=pl.CostEstimate(flops=flops, bytes_accessed=moved, transcendentals=0),
         **more,
     )(*operands)
@@ -217,6 +217,77 @@
     )
 
 
+def combine_keyval_body(parts_ref, keyval_ref, scale_ref, held, sems):
+    copies = [
+        pltpu.make_async_copy(parts_ref.at[b, pl.ds(TOKENS, SENT_ROWS - TOKENS)], held.at[b], sems.at[b])
+        for b in range(SIDE)
+    ]
+    for copy in copies:
+        copy.start()
+    for copy in copies:
+        copy.wait()
+    tail = held[0].astype(f32)
+    for b in range(1, SIDE):
+        tail += held[b].astype(f32)
+    stats = tail[2 * KV_ROWS :]
+    for h in range(2):
+        cols = slice(h * HALF, (h + 1) * HALF)
+        scale = lax.rsqrt((stats[h : h + 1] + stats[2 + h : 3 + h]) / D + norm_eps)
+        scale_ref[:, cols] = jnp.broadcast_to(scale, (8, HALF))
+        keyval = (tail[h * KV_ROWS : (h + 1) * KV_ROWS] * scale).astype(bf16)
+        for b in range(SIDE):
+            keyval_ref[b, :, cols] = keyval
+
+
+def combine_keyval(parts):
+    return call(
+        combine_keyval_body,
+        (jax.ShapeDtypeStruct((SIDE, KV_ROWS, TOKENS), bf16), jax.ShapeDtypeStruct((8, TOKENS), f32)),
+        (parts,),
+        [ANY],
+        TOKENS * KV_ROWS * 8,
+        1 << 19,
+        vmem=61 << 20,
+        scratch_shapes=[
+            pltpu.VMEM((SIDE, SENT_ROWS - TOKENS, HALF), bf16),
+            pltpu.SemaphoreType.DMA((SIDE,)),
+        ],
+    )
+
+
+def combine_query_body(parts_ref, scale_ref, query_ref, held, sems):
+    blocks = TOKENS // HEAD_DIM
+    copies = [
+        pltpu.make_async_copy(
+            parts_ref.at[:, pl.ds(i * HEAD_DIM, HEAD_DIM)], held.at[:, pl.ds(i * HEAD_DIM, HEAD_DIM)], sems.at[i]
+        )
+        for i in range(blocks)
+    ]
+    for copy in copies:
+        copy.start()
+    for i in range(blocks):
+        copies[i].wait()
+        rows = slice(i * HEAD_DIM, (i + 1) * HEAD_DIM)
+        total = held[0, rows].astype(f32)
+        for b in range(1, SIDE):
+            total += held[b, rows].astype(f32)
+        factor = down(scale_ref[:1, rows])
+        query_ref[rows] = (total * jnp.concatenate([factor, factor], axis=1)).astype(bf16)
+
+
+def combine_query(parts, scale):
+    return call(
+        combine_query_body,
+        jax.ShapeDtypeStruct((TOKENS, BLOCK), bf16),
+        (parts, scale),
+        [ANY, VMEM],
+        TOKENS * BLOCK * 8,
+        2 << 20,
+        vmem=61 << 20,
+        scratch_shapes=[pltpu.VMEM((SIDE, TOKENS, BLOCK), bf16), pltpu.SemaphoreType.DMA((TOKENS // HEAD_DIM,))],
+    )
+
+
 def attend_body(is_second, lengths_ref, x_ref, query_ref, keyval_ref, segments_ref, *refs):
     section = lax.axis_index("section")
     if is_second:
@@ -378,8 +449,8 @@
 
     parts, gains = project(False, blocks, [], weights)
     parts = exchange(parts, ring_b)
-    query, keyval = combine(parts)
-    keyval, frames = barrier((keyval, frames))
+    keyval, scale = combine_keyval(parts)
+    query = combine_query(parts, scale)
     first, sent = attend(False, row_lengths, x, query, exchange(keyval, ring_y), segments, frames)
 
     blocks = []

time: 126 us -> 124 us (0.984); the launches traced: 125 us -> 122 us
  blocking collectives: 34.2 us -> 23.9 us
  starting transfers between devices: 41 us -> 45.8 us
  Pallas kernels: 16.7 us -> 20.7 us
  waiting for transfers between devices: 30 us -> 26.4 us
  local copies, waits for them, and re-layouts: 2.07 us -> 3.71 us
    all_to_all x3 -> x2, blocking collectives: 34.2 us -> 23.9 us  [exchange(): return lax.all_to_all(array, AXES, 0, 0, axis_index_groups=ring)]
    ppermute x4, waiting for transfers between devices: 13.1 us -> 6.78 us  [per_device(): blocks.append(lax.ppermute(sent, AXES, route))]
    all_to_all x2 -> x3, starting transfers between devices: 8.9 us -> 13.1 us  [exchange(): return lax.all_to_all(array, AXES, 0, 0, axis_index_groups=ring)]
    pallas_call x7 -> x8, Pallas kernels: 12.6 us -> 16.7 us  [call(): pl.pallas_call(body, out_shape=out_shape, in_specs=specs, out_specs=jax.t...]
    all_to_all x2 -> x3, waiting for transfers between devices: 16 us -> 18.6 us  [exchange(): return lax.all_to_all(array, AXES, 0, 0, axis_index_groups=ring)]
    unnamed x18 -> x20, local copies, waits for them, and re-layouts: 2.07 us -> 3.71 us
  transfers between devices with their start and end apart: 16 -> 17, of which waited for: 7 -> 6; matrix products, arithmetic and copies ran while one was open for 0% -> 0% of each run, Pallas kernels for 2% -> 6%
where the time goes in v7:
time: 124 us; the launch traced here: 122 us
  starting transfers between devices  45.8 us (37%)
  waiting for transfers between devices  26.4 us (21%)
  blocking collectives  23.9 us (19%)
  Pallas kernels  20.7 us (17%)
  local copies, waits for them, and re-layouts  3.71 us (3%)
    all_to_all x2, blocking collectives, exchange(): return lax.all_to_all(array, AXES, 0, 0, axis_index_groups=ring)  23.9 us
    all_to_all x3, waiting for transfers between devices, exchange(): return lax.all_to_all(array, AXES, 0, 0, axis_index_groups=ring)  18.6 us
    pallas_call x8, Pallas kernels, call(): pl.pallas_call(body, out_shape=out_shape, in_specs=specs, out_specs=jax.t...  16.7 us
    all_to_all x3, starting transfers between devices, exchange(): return lax.all_to_all(array, AXES, 0, 0, axis_index_groups=ring)  13.1 us
    ppermute x4, starting transfers between devices, per_device(): blocks.append(lax.ppermute(sent, AXES, route))  13.1 us
    ppermute x3, starting transfers between devices, per_device(): blocks.append(lax.ppermute(own, AXES, route))  10.2 us
    ppermute x7, starting transfers between devices, bring(): got.append(lax.ppermute(array, 'section', route))  9.49 us
    ppermute x4, waiting for transfers between devices, per_device(): blocks.append(lax.ppermute(sent, AXES, route))  6.78 us
  transfers between devices with their start and end apart: 17, of which 6 were waited for; matrix products, arithmetic and copies ran while one was open for 0% of the time, Pallas kernels for 6%

profile of v7, /device:TPU:6, one launch (start us, length us, event | category | flops | bytes accessed | tf_op | source)
XLA Modules:
  0.0 121.5 jit_solution(9830775640478237110)
XLA Ops:
  0.6 4.1 %shard_map.95 = (bf16[4,4,320,256]{3,2,1,0:T(8,128)(2,1)}, bf16[528,256]{1,0:T(8,128)(2,1)}, bf16[128,256]{1,0:T(8,128)(2,1)}) custom-call(s32[32]{0:T(128)} %ids_ref.3, bf16[512,256]{1,0:T(8,128)(2,1)} %bitcast.5, bf16[1,256]{1,0:T(2,128)(2,1)} %gain_ref.1, bf16[4096,256]{1,0:T(8,128)(2,1)} %bitcast.7, bf16[64,4096]{1,0:T(8,128)(2,1)} %bitcast.8, ...), custom_call_target="tpu_custom_call" | custom-call | bytes 6291456 | tf_op jit(solution)/shard_map/pallas_call | solution.py:99
  4.8 4.6 %all-to-all-start = ((bf16[4,4,320,256]{3,2,1,0:T(8,128)(2,1)}), bf16[4,4,320,256]{3,2,1,0:T(8,128)(2,1)S(1)}, u32[]{:S(2)}, u32[]{:S(2)}) async-start(bf16[4,4,320,256]{3,2,1,0:T(8,128)(2,1)} %get-tuple-element.20), calls=%async_computation | async-start | bytes 5242880 | tf_op jit(solution)/shard_map/all_to_all | solution.py:433
  9.4 2.7 %collective-permute-start.2 = (bf16[528,256]{1,0:T(8,128)(2,1)S(1)}, bf16[528,256]{1,0:T(8,128)(2,1)S(1)}, u32[]{:S(2)}, u32[]{:S(2)}) collective-permute-start(bf16[528,256]{1,0:T(8,128)(2,1)S(1)} %copy-done.6), channel_id=1, source_target_pairs={{4,0},{5,1},{6,2},{7,3},{8,4},{9,5},{10,6},{11,7},{12,8},{13,9},{1... | collective-permute-start | bytes 811016 | tf_op jit(solution)/shard_map/ppermute | solution.py:441
  12.1 3.4 %collective-permute-start.3 = (bf16[128,256]{1,0:T(8,128)(2,1)S(1)}, bf16[128,256]{1,0:T(8,128)(2,1)S(1)}, u32[]{:S(2)}, u32[]{:S(2)}) collective-permute-start(bf16[128,256]{1,0:T(8,128)(2,1)S(1)} %copy-done.9), channel_id=1, source_target_pairs={{0,16},{32,48},{64,80},{96,112},{128,144},{160,176},{192,208},{224... | collective-permute-start | bytes 196616 | tf_op jit(solution)/shard_map/ppermute | solution.py:419
  15.5 4.1 %collective-permute-start = (bf16[528,256]{1,0:T(8,128)(2,1)S(1)}, bf16[528,256]{1,0:T(8,128)(2,1)S(1)}, u32[]{:S(2)}, u32[]{:S(2)}) collective-permute-start(bf16[528,256]{1,0:T(8,128)(2,1)S(1)} %copy-done.6), channel_id=1, source_target_pairs={{12,0},{13,1},{14,2},{15,3},{0,4},{1,5},{2,6},{3,7},{4,8},{5,9},{6... | collective-permute-start | bytes 811016 | tf_op jit(solution)/shard_map/ppermute | solution.py:441
  19.6 3.4 %collective-permute-start.1 = (bf16[528,256]{1,0:T(8,128)(2,1)S(1)}, bf16[528,256]{1,0:T(8,128)(2,1)}, u32[]{:S(2)}, u32[]{:S(2)}) collective-permute-start(bf16[528,256]{1,0:T(8,128)(2,1)S(1)} %copy-done.6), channel_id=1, source_target_pairs={{8,0},{9,1},{10,2},{11,3},{12,4},{13,5},{14,6},{15,7},{0,8},{1,9},... | collective-permute-start | bytes 811016 | tf_op jit(solution)/shard_map/ppermute | solution.py:441
  26.0 2.2 %shard_map.96.refs_0_ = bf16[512,256]{1,0:T(8,128)(2,1)} custom-call(s32[32]{0:T(128)S(1)} %copy-done.5, s32[32]{0:T(128)S(1)} %copy-done.4, bf16[256,256]{1,0:T(8,128)(2,1)S(1)} %pad_maximum_fusion.refs_0_, bf16[256,256]{1,0:T(8,128)(2,1)S(1)} %collective-permute-done.4.refs_1_, bf16[256,256]{1,0:T(8,128)(2,1)S(1)} %collective-permute-done.5.refs_2_, ...), custom_call_target="tpu_custom_call" | custom-call | flops 268435456 | bytes 1048576 | tf_op jit(solution)/shard_map/pallas_call | solution.py:50
  28.2 6.3 %all-to-all-done.refs_4_.refs_5_ = bf16[4,4,320,256]{3,2,1,0:T(8,128)(2,1)S(1)} async-done(((bf16[4,4,320,256]{3,2,1,0:T(8,128)(2,1)}), bf16[4,4,320,256]{3,2,1,0:T(8,128)(2,1)S(1)}, u32[]{:S(2)}, u32[]{:S(2)}) %all-to-all-start) | async-done | bytes 2621472 | tf_op jit(solution)/shard_map/all_to_all | solution.py:433
  36.1 2.9 %shard_map.97 = (bf16[4,656,256]{2,1,0:T(8,128)(2,1)S(1)}, bf16[64,256]{1,0:T(8,128)(2,1)S(1)}) custom-call(bf16[528,256]{1,0:T(8,128)(2,1)S(1)} %copy-done.6, bf16[528,256]{1,0:T(8,128)(2,1)S(1)} %copy-done.8, bf16[528,256]{1,0:T(8,128)(2,1)} %collective-permute-done.1.refs_2_, bf16[528,256]{1,0:T(8,128)(2,1)S(1)} %collective-permute-done.2.refs_3_, ...), custom_call_target="tpu_custom_call" | custom-call | flops 1342177280 | bytes 6291456 | tf_op jit(solution)/shard_map/pallas_call | solution.py:50
  40.1 4.3 %all-to-all-start.1 = ((bf16[4,656,256]{2,1,0:T(8,128)(2,1)}), bf16[4,656,256]{2,1,0:T(8,128)(2,1)}, u32[]{:S(2)}, u32[]{:S(2)}) async-start(bf16[4,656,256]{2,1,0:T(8,128)(2,1)} %copy-done), calls=%async_computation.1 | async-start | bytes 2686976 | tf_op jit(solution)/shard_map/all_to_all | solution.py:433
  48.5 8.4 %all-to-all-done.1.parts_ref = bf16[4,656,256]{2,1,0:T(8,128)(2,1)} async-done(((bf16[4,656,256]{2,1,0:T(8,128)(2,1)}), bf16[4,656,256]{2,1,0:T(8,128)(2,1)}, u32[]{:S(2)}, u32[]{:S(2)}) %all-to-all-start.1) | async-done | bytes 1343520 | tf_op jit(solution)/shard_map/all_to_all | solution.py:433
  58.8 4.2 %all-to-all-start.2 = ((bf16[4,64,512]{2,1,0:T(8,128)(2,1)}), bf16[4,64,512]{2,1,0:T(8,128)(2,1)}, u32[]{:S(2)}, u32[]{:S(2)}) async-start(bf16[4,64,512]{2,1,0:T(8,128)(2,1)} %get-tuple-element.25), calls=%async_computation.2 | async-start | bytes 524288 | tf_op jit(solution)/shard_map/all_to_all | solution.py:433
  63.0 2.8 %shard_map.99.query_ref = bf16[512,256]{1,0:T(8,128)(2,1)} custom-call(bf16[4,656,256]{2,1,0:T(8,128)(2,1)} %all-to-all-done.1.parts_ref, f32[8,512]{1,0:T(8,128)} %get-tuple-element.24.scale_ref), custom_call_target="tpu_custom_call" | custom-call | flops 1048576 | bytes 2097152 | tf_op jit(solution)/shard_map/pallas_call | solution.py:50
  65.8 3.9 %all-to-all-done.2.keyval_ref = bf16[4,64,512]{2,1,0:T(8,128)(2,1)} async-done(((bf16[4,64,512]{2,1,0:T(8,128)(2,1)}), bf16[4,64,512]{2,1,0:T(8,128)(2,1)}, u32[]{:S(2)}, u32[]{:S(2)}) %all-to-all-start.2) | async-done | bytes 262176 | tf_op jit(solution)/shard_map/all_to_all | solution.py:433
  70.7 2.4 %shard_map.100 = (bf16[512,256]{1,0:T(8,128)(2,1)}, bf16[512,256]{1,0:T(8,128)(2,1)S(1)}) custom-call(s32[32]{0:T(128)S(1)} %copy-done.4, bf16[512,256]{1,0:T(8,128)(2,1)S(1)} %bitcast.6, bf16[512,256]{1,0:T(8,128)(2,1)S(1)} %copy-done.2, bf16[4,64,512]{2,1,0:T(8,128)(2,1)} %all-to-all-done.2.keyval_ref, s32[32,512]{1,0:T(8,128)S(1)} %copy-done.3, ...), custom_call_target="tpu_custom_call" | custom-call | flops 134217728 | bytes 1048576 | tf_op jit(solution)/shard_map/pallas_call | solution.py:50
  73.1 4.1 %collective-permute-start.11 = (bf16[512,256]{1,0:T(8,128)(2,1)S(1)}, bf16[512,256]{1,0:T(8,128)(2,1)S(1)}, u32[]{:S(2)}, u32[]{:S(2)}) collective-permute-start(bf16[512,256]{1,0:T(8,128)(2,1)S(1)} %get-tuple-element.28), channel_id=1, source_target_pairs={{508,0},{509,1},{510,2},{511,3},{496,4},{497,5},{498,6},{499,7},{5... | collective-permute-start | bytes 786440 | tf_op jit(solution)/shard_map/ppermute | solution.py:459
  77.2 1.9 %collective-permute-start.12 = (bf16[512,256]{1,0:T(8,128)(2,1)S(1)}, bf16[512,256]{1,0:T(8,128)(2,1)S(1)}, u32[]{:S(2)}, u32[]{:S(2)}) collective-permute-start(bf16[512,256]{1,0:T(8,128)(2,1)S(1)} %get-tuple-element.28), channel_id=1, source_target_pairs={{504,0},{505,1},{506,2},{507,3},{508,4},{509,5},{510,6},{511,7},{4... | collective-permute-start | bytes 786440 | tf_op jit(solution)/shard_map/ppermute | solution.py:459
  79.1 7.0 %collective-permute-start.13 = (bf16[512,256]{1,0:T(8,128)(2,1)S(1)}, bf16[512,256]{1,0:T(8,128)(2,1)S(1)}, u32[]{:S(2)}, u32[]{:S(2)}) collective-permute-start(bf16[512,256]{1,0:T(8,128)(2,1)S(1)} %get-tuple-element.28), channel_id=1, source_target_pairs={{500,0},{501,1},{502,2},{503,3},{504,4},{505,5},{506,6},{507,7},{5... | collective-permute-start | bytes 786440 | tf_op jit(solution)/shard_map/ppermute | solution.py:459
  86.2 2.9 %collective-permute-done.12.refs_2_ = bf16[512,256]{1,0:T(8,128)(2,1)S(1)} collective-permute-done((bf16[512,256]{1,0:T(8,128)(2,1)S(1)}, bf16[512,256]{1,0:T(8,128)(2,1)S(1)}, u32[]{:S(2)}, u32[]{:S(2)}) %collective-permute-start.12) | collective-permute-done | bytes 262176 | tf_op jit(solution)/shard_map/ppermute | solution.py:459
  89.1 3.9 %collective-permute-done.13.refs_3_ = bf16[512,256]{1,0:T(8,128)(2,1)S(1)} collective-permute-done((bf16[512,256]{1,0:T(8,128)(2,1)S(1)}, bf16[512,256]{1,0:T(8,128)(2,1)S(1)}, u32[]{:S(2)}, u32[]{:S(2)}) %collective-permute-start.13) | collective-permute-done | bytes 262176 | tf_op jit(solution)/shard_map/ppermute | solution.py:459
  93.0 2.1 %shard_map.101 = bf16[4,656,256]{2,1,0:T(8,128)(2,1)S(1)} custom-call(bf16[512,256]{1,0:T(8,128)(2,1)S(1)} %collective-permute-done.10.refs_0_.x_ref, bf16[512,256]{1,0:T(8,128)(2,1)S(1)} %collective-permute-done.11.refs_1_, bf16[512,256]{1,0:T(8,128)(2,1)S(1)} %collective-permute-done.12.refs_2_, bf16[512,256]{1,0:T(8,128)(2,1)S(1)} %collective-permute-done.13.refs_3_, ...), custom_call_target="tpu_custom_call" | custom-call | flops 1342177280 | bytes 6291456 | tf_op jit(solution)/shard_map/pallas_call | solution.py:50
  95.1 14.9 %all_to_all.25.parts_ref = bf16[4,656,256]{2,1,0:T(8,128)(2,1)S(1)} all-to-all(bf16[4,656,256]{2,1,0:T(8,128)(2,1)S(1)} %shard_map.101), channel_id=1, replica_groups={{0,1,2,3},{4,5,6,7},{8,9,10,11},{12,13,14,15},{16,20,24,28},{17,21,25,2..., dimensions={0} | all-to-all | bytes 2686976 | tf_op jit(solution)/shard_map/all_to_all | solution.py:433
  110.2 9.1 %all_to_all.26.keyval_ref = bf16[4,64,512]{2,1,0:T(8,128)(2,1)S(1)} all-to-all(bf16[4,64,512]{2,1,0:T(8,128)(2,1)S(1)} %get-tuple-element.31), channel_id=1, replica_groups={{0,1,2,3},{4,5,6,7},{8,9,10,11},{12,13,14,15},{16,17,18,19},{20,21,22,2..., dimensions={0} | all-to-all | bytes 524288 | tf_op jit(solution)/shard_map/all_to_all | solution.py:433
  119.3 2.2 %shard_map.103 = bf16[512,256]{1,0:T(8,128)(2,1)} custom-call(s32[32]{0:T(128)S(1)} %copy-done.4, bf16[512,256]{1,0:T(8,128)(2,1)S(1)} %collective-permute-done.10.refs_0_.x_ref, bf16[512,256]{1,0:T(8,128)(2,1)S(1)} %get-tuple-element.30.query_ref, bf16[4,64,512]{2,1,0:T(8,128)(2,1)S(1)} %all_to_all.26.keyval_ref, s32[32,512]{1,0:T(8,128)S(1)} %copy-done.3), custom_call_target="tpu_custom_call" | custom-call | flops 134217728 | bytes 1048576 | tf_op jit(solution)/shard_map/pallas_call | solution.py:50
  (42 shorter events, 12.8 us)
Async XLA Ops:
  4.7 4.7 %copy-start.6 = (bf16[528,256]{1,0:T(8,128)(2,1)S(1)}, bf16[528,256]{1,0:T(8,128)(2,1)}, u32[]{:S(2)}) copy-start(bf16[528,256]{1,0:T(8,128)(2,1)} %get-tuple-element.17.refs_0_) | copy-start | bytes 811012
  4.7 7.4 %copy-start.9 = (bf16[128,256]{1,0:T(8,128)(2,1)S(1)}, bf16[128,256]{1,0:T(8,128)(2,1)}, u32[]{:S(2)}) copy-start(bf16[128,256]{1,0:T(8,128)(2,1)} %get-tuple-element.18) | copy-start | bytes 196612
  4.7 21.3 %copy-start.4 = (s32[32]{0:T(128)S(1)}, s32[32]{0:T(128)}, u32[]{:S(2)}) copy-start(s32[32]{0:T(128)} %lengths_ref.5) | copy-start | bytes 388
  4.7 21.3 %copy-start.5 = (s32[32]{0:T(128)S(1)}, s32[32]{0:T(128)}, u32[]{:S(2)}) copy-start(s32[32]{0:T(128)} %ids_ref.3) | copy-start | bytes 388
  4.8 29.7 %all-to-all-start = ((bf16[4,4,320,256]{3,2,1,0:T(8,128)(2,1)}), bf16[4,4,320,256]{3,2,1,0:T(8,128)(2,1)S(1)}, u32[]{:S(2)}, u32[]{:S(2)}) async-start(bf16[4,4,320,256]{3,2,1,0:T(8,128)(2,1)} %get-tuple-element.20), calls=%async_computation | async-start | bytes 5242880 | tf_op jit(solution)/shard_map/all_to_all | solution.py:433
  9.4 14.6 %collective-permute-start.2 = (bf16[528,256]{1,0:T(8,128)(2,1)S(1)}, bf16[528,256]{1,0:T(8,128)(2,1)S(1)}, u32[]{:S(2)}, u32[]{:S(2)}) collective-permute-start(bf16[528,256]{1,0:T(8,128)(2,1)S(1)} %copy-done.6), channel_id=1, source_target_pairs={{4,0},{5,1},{6,2},{7,3},{8,4},{9,5},{10,6},{11,7},{12,8},{13,9},{1... | collective-permute-start | bytes 811016 | tf_op jit(solution)/shard_map/ppermute | solution.py:441
  12.1 10.9 %collective-permute-start.3 = (bf16[128,256]{1,0:T(8,128)(2,1)S(1)}, bf16[128,256]{1,0:T(8,128)(2,1)S(1)}, u32[]{:S(2)}, u32[]{:S(2)}) collective-permute-start(bf16[128,256]{1,0:T(8,128)(2,1)S(1)} %copy-done.9), channel_id=1, source_target_pairs={{0,16},{32,48},{64,80},{96,112},{128,144},{160,176},{192,208},{224... | collective-permute-start | bytes 196616 | tf_op jit(solution)/shard_map/ppermute | solution.py:419
  15.5 19.0 %collective-permute-start = (bf16[528,256]{1,0:T(8,128)(2,1)S(1)}, bf16[528,256]{1,0:T(8,128)(2,1)S(1)}, u32[]{:S(2)}, u32[]{:S(2)}) collective-permute-start(bf16[528,256]{1,0:T(8,128)(2,1)S(1)} %copy-done.6), channel_id=1, source_target_pairs={{12,0},{13,1},{14,2},{15,3},{0,4},{1,5},{2,6},{3,7},{4,8},{5,9},{6... | collective-permute-start | bytes 811016 | tf_op jit(solution)/shard_map/ppermute | solution.py:441
  19.6 15.6 %collective-permute-start.1 = (bf16[528,256]{1,0:T(8,128)(2,1)S(1)}, bf16[528,256]{1,0:T(8,128)(2,1)}, u32[]{:S(2)}, u32[]{:S(2)}) collective-permute-start(bf16[528,256]{1,0:T(8,128)(2,1)S(1)} %copy-done.6), channel_id=1, source_target_pairs={{8,0},{9,1},{10,2},{11,3},{12,4},{13,5},{14,6},{15,7},{0,8},{1,9},... | collective-permute-start | bytes 811016 | tf_op jit(solution)/shard_map/ppermute | solution.py:441
  23.9 2.0 %collective-permute-start.4 = (bf16[256,256]{1,0:T(8,128)(2,1)S(1)}, bf16[256,256]{1,0:T(8,128)(2,1)S(1)}, u32[]{:S(2)}, u32[]{:S(2)}) collective-permute-start(bf16[256,256]{1,0:T(8,128)(2,1)S(1)} %pad_maximum_fusion.refs_0_), channel_id=1, source_target_pairs={{80,112},{208,240},{336,368},{464,496},{81,113},{209,241},{337,369... | collective-permute-start | bytes 393224 | tf_op jit(solution)/shard_map/ppermute | solution.py:419
  24.6 1.4 %collective-permute-start.5 = (bf16[256,256]{1,0:T(8,128)(2,1)S(1)}, bf16[256,256]{1,0:T(8,128)(2,1)S(1)}, u32[]{:S(2)}, u32[]{:S(2)}) collective-permute-start(bf16[256,256]{1,0:T(8,128)(2,1)S(1)} %pad_maximum_fusion.refs_0_), channel_id=1, source_target_pairs={{48,112},{176,240},{304,368},{432,496},{49,113},{177,241},{305,369... | collective-permute-start | bytes 393224 | tf_op jit(solution)/shard_map/ppermute | solution.py:419
  25.3 0.7 collective-permute-start.6
  39.0 1.1 copy-start
  40.1 16.8 %all-to-all-start.1 = ((bf16[4,656,256]{2,1,0:T(8,128)(2,1)}), bf16[4,656,256]{2,1,0:T(8,128)(2,1)}, u32[]{:S(2)}, u32[]{:S(2)}) async-start(bf16[4,656,256]{2,1,0:T(8,128)(2,1)} %copy-done), calls=%async_computation.1 | async-start | bytes 2686976 | tf_op jit(solution)/shard_map/all_to_all | solution.py:433
  44.4 21.4 %collective-permute-start.7 = (bf16[512,256]{1,0:T(8,128)(2,1)}, bf16[512,256]{1,0:T(8,128)(2,1)}, u32[]{:S(2)}, u32[]{:S(2)}) collective-permute-start(bf16[512,256]{1,0:T(8,128)(2,1)} %shard_map.96.refs_0_), channel_id=1, source_target_pairs={{368,496},{369,497},{370,498},{371,499},{372,500},{373,501},{374,5... | collective-permute-start | bytes 786440 | tf_op jit(solution)/shard_map/ppermute | solution.py:419
  45.8 20.0 %collective-permute-start.8 = (bf16[512,256]{1,0:T(8,128)(2,1)}, bf16[512,256]{1,0:T(8,128)(2,1)}, u32[]{:S(2)}, u32[]{:S(2)}) collective-permute-start(bf16[512,256]{1,0:T(8,128)(2,1)} %shard_map.96.refs_0_), channel_id=1, source_target_pairs={{240,496},{241,497},{242,498},{243,499},{244,500},{245,501},{246,5... | collective-permute-start | bytes 786440 | tf_op jit(solution)/shard_map/ppermute | solution.py:419
  47.2 18.6 %collective-permute-start.9 = (bf16[512,256]{1,0:T(8,128)(2,1)}, bf16[512,256]{1,0:T(8,128)(2,1)}, u32[]{:S(2)}, u32[]{:S(2)}) collective-permute-start(bf16[512,256]{1,0:T(8,128)(2,1)} %shard_map.96.refs_0_), channel_id=1, source_target_pairs={{112,496},{113,497},{114,498},{115,499},{116,500},{117,501},{118,5... | collective-permute-start | bytes 786440 | tf_op jit(solution)/shard_map/ppermute | solution.py:419
  58.7 11.0 %copy-start.1 = (bf16[1,512,256]{2,1,0:T(8,128)(2,1)S(1)}, bf16[1,512,256]{2,1,0:T(8,128)(2,1)}, u32[]{:S(2)}) copy-start(bf16[1,512,256]{2,1,0:T(8,128)(2,1)} %param.8) | copy-start | bytes 786436
  58.8 10.9 %copy-start.3 = (s32[32,512]{1,0:T(8,128)S(1)}, s32[32,512]{1,0:T(8,128)}, u32[]{:S(2)}) copy-start(s32[32,512]{1,0:T(8,128)} %segments_ref.3) | copy-start | bytes 196612
  58.8 10.9 %all-to-all-start.2 = ((bf16[4,64,512]{2,1,0:T(8,128)(2,1)}), bf16[4,64,512]{2,1,0:T(8,128)(2,1)}, u32[]{:S(2)}, u32[]{:S(2)}) async-start(bf16[4,64,512]{2,1,0:T(8,128)(2,1)} %get-tuple-element.25), calls=%async_computation.2 | async-start | bytes 524288 | tf_op jit(solution)/shard_map/all_to_all | solution.py:433
  73.1 13.1 %collective-permute-start.10 = (bf16[512,256]{1,0:T(8,128)(2,1)S(1)}, bf16[512,256]{1,0:T(8,128)(2,1)S(1)}, u32[]{:S(2)}, u32[]{:S(2)}) collective-permute-start(bf16[512,256]{1,0:T(8,128)(2,1)S(1)} %get-tuple-element.28), channel_id=1, source_target_pairs={{496,0},{497,1},{498,2},{499,3},{500,4},{501,5},{502,6},{503,7},{5... | collective-permute-start | bytes 786440 | tf_op jit(solution)/shard_map/ppermute | solution.py:459
  73.1 13.1 %collective-permute-start.11 = (bf16[512,256]{1,0:T(8,128)(2,1)S(1)}, bf16[512,256]{1,0:T(8,128)(2,1)S(1)}, u32[]{:S(2)}, u32[]{:S(2)}) collective-permute-start(bf16[512,256]{1,0:T(8,128)(2,1)S(1)} %get-tuple-element.28), channel_id=1, source_target_pairs={{508,0},{509,1},{510,2},{511,3},{496,4},{497,5},{498,6},{499,7},{5... | collective-permute-start | bytes 786440 | tf_op jit(solution)/shard_map/ppermute | solution.py:459
  77.2 11.9 %collective-permute-start.12 = (bf16[512,256]{1,0:T(8,128)(2,1)S(1)}, bf16[512,256]{1,0:T(8,128)(2,1)S(1)}, u32[]{:S(2)}, u32[]{:S(2)}) collective-permute-start(bf16[512,256]{1,0:T(8,128)(2,1)S(1)} %get-tuple-element.28), channel_id=1, source_target_pairs={{504,0},{505,1},{506,2},{507,3},{508,4},{509,5},{510,6},{511,7},{4... | collective-permute-start | bytes 786440 | tf_op jit(solution)/shard_map/ppermute | solution.py:459
  79.1 13.9 %collective-permute-start.13 = (bf16[512,256]{1,0:T(8,128)(2,1)S(1)}, bf16[512,256]{1,0:T(8,128)(2,1)S(1)}, u32[]{:S(2)}, u32[]{:S(2)}) collective-permute-start(bf16[512,256]{1,0:T(8,128)(2,1)S(1)} %get-tuple-element.28), channel_id=1, source_target_pairs={{500,0},{501,1},{502,2},{503,3},{504,4},{505,5},{506,6},{507,7},{5... | collective-permute-start | bytes 786440 | tf_op jit(solution)/shard_map/ppermute | solution.py:459
  (3 other events, 2.6 us)

commit v8 on v7

--- a/solution.py
+++ b/solution.py
@@ -119,7 +119,9 @@
 def project_body(is_second, *refs):
     x_refs = refs[:SIDE]
     if is_second:
-        gain_ref, w_ref, out_ref, wide_ref, kv_ref = refs[SIDE:]
+        gain_ref, w_ref, out_ref, kept_ref, wide_ref, kv_ref = refs[SIDE:]
+        x_refs = x_refs[::-1]
+        kept_ref[...] = x_refs[0][...]
     else:
         w_ref, out_ref, gain_ref, wide_ref, kv_ref, held, sems = refs[SIDE:]
         copies = [pltpu.make_async_copy(ref, held.at[d], sems.at[d]) for d, ref in enumerate(x_refs)]
@@ -168,7 +170,7 @@
     parts = jax.ShapeDtypeStruct((SIDE, SENT_ROWS, BLOCK), bf16)
     return call(
         functools.partial(project_body, is_second),
-        parts if is_second else (parts, jax.ShapeDtypeStruct((16 * SIDE, BLOCK), bf16)),
+        (parts, jax.ShapeDtypeStruct((TOKENS, BLOCK) if is_second else (16 * SIDE, BLOCK), bf16)),
         (*blocks, *gains, weights),
         [VMEM if is_second else ANY] * SIDE + [VMEM] * (len(gains) + 1),
         2 * TOKENS * 1024 * 1280,
@@ -247,7 +249,7 @@
         [ANY],
         TOKENS * KV_ROWS * 8,
         1 << 19,
-        vmem=61 << 20,
+        vmem=60 << 20,
         scratch_shapes=[
             pltpu.VMEM((SIDE, SENT_ROWS - TOKENS, HALF), bf16),
             pltpu.SemaphoreType.DMA((SIDE,)),
@@ -283,7 +285,7 @@
         [ANY, VMEM],
         TOKENS * BLOCK * 8,
         2 << 20,
-        vmem=61 << 20,
+        vmem=60 << 20,
         scratch_shapes=[pltpu.VMEM((SIDE, TOKENS, BLOCK), bf16), pltpu.SemaphoreType.DMA((TOKENS // HEAD_DIM,))],
     )
 
@@ -457,8 +459,9 @@
     for d in range(SIDE):
         route = [(number((s - 1) % sections, a - d, b, s), number(s, a, b, s)) for s, a, b in grid]
         blocks.append(lax.ppermute(sent, AXES, route))
-    query, keyval = combine(exchange(project(True, blocks, [gains], weights), ring_b))
-    second = attend(True, row_lengths, blocks[0], query, exchange(keyval, ring_y), segments, [])
+    parts, kept = project(True, blocks[::-1], [gains], weights)
+    query, keyval = combine(exchange(parts, ring_b))
+    second = attend(True, row_lengths, kept, query, exchange(keyval, ring_y), segments, [])
     return first[None], second[None]
 
 

time: 124 us -> 122 us (0.984)
  waiting for transfers between devices: 26.4 us -> 29.1 us
  local copies, waits for them, and re-layouts: 3.71 us -> 2.06 us
  starting transfers between devices: 45.8 us -> 44.2 us
    ppermute x4, waiting for transfers between devices: 6.78 us -> 8.87 us  [per_device(): blocks.append(lax.ppermute(sent, AXES, route))]
    unnamed x20 -> x16, local copies, waits for them, and re-layouts: 3.71 us -> 2.06 us
  transfers between devices with their start and end apart: 17 -> 17, of which waited for: 6 -> 8; matrix products, arithmetic and copies ran while one was open for 0% -> 0% of each run, Pallas kernels for 6% -> 5%
where the time goes in v8:
time: 122 us; the launch traced here: 121 us
  starting transfers between devices  44.2 us (36%)
  waiting for transfers between devices  29.1 us (24%)
  blocking collectives  24.5 us (20%)
  Pallas kernels  19.8 us (16%)
  local copies, waits for them, and re-layouts  2.06 us (2%)
    all_to_all x2, blocking collectives, exchange(): return lax.all_to_all(array, AXES, 0, 0, axis_index_groups=ring)  24.5 us
    all_to_all x3, waiting for transfers between devices, exchange(): return lax.all_to_all(array, AXES, 0, 0, axis_index_groups=ring)  19.3 us
    pallas_call x8, Pallas kernels, call(): pl.pallas_call(body, out_shape=out_shape, in_specs=specs, out_specs=jax.t...  15.7 us
    all_to_all x3, starting transfers between devices, exchange(): return lax.all_to_all(array, AXES, 0, 0, axis_index_groups=ring)  12.5 us
    ppermute x4, starting transfers between devices, per_device(): blocks.append(lax.ppermute(sent, AXES, route))  12.1 us
    ppermute x3, starting transfers between devices, per_device(): blocks.append(lax.ppermute(own, AXES, route))  10.2 us
    ppermute x7, starting transfers between devices, bring(): got.append(lax.ppermute(array, 'section', route))  9.45 us
    ppermute x4, waiting for transfers between devices, per_device(): blocks.append(lax.ppermute(sent, AXES, route))  8.87 us
  transfers between devices with their start and end apart: 17, of which 8 were waited for; matrix products, arithmetic and copies ran while one was open for 0% of the time, Pallas kernels for 5%

profile of v8, /device:TPU:6, one launch (start us, length us, event | category | flops | bytes accessed | tf_op | source)
XLA Modules:
  0.0 120.5 jit_solution(16869407039411541673)
XLA Ops:
  0.6 4.1 %shard_map.95 = (bf16[4,4,320,256]{3,2,1,0:T(8,128)(2,1)}, bf16[528,256]{1,0:T(8,128)(2,1)}, bf16[128,256]{1,0:T(8,128)(2,1)}) custom-call(s32[32]{0:T(128)} %ids_ref.3, bf16[512,256]{1,0:T(8,128)(2,1)} %bitcast.5, bf16[1,256]{1,0:T(2,128)(2,1)} %gain_ref.1, bf16[4096,256]{1,0:T(8,128)(2,1)} %bitcast.7, bf16[64,4096]{1,0:T(8,128)(2,1)} %bitcast.8, ...), custom_call_target="tpu_custom_call" | custom-call | bytes 6291456 | tf_op jit(solution)/shard_map/pallas_call | solution.py:99
  4.8 4.6 %all-to-all-start = ((bf16[4,4,320,256]{3,2,1,0:T(8,128)(2,1)}), bf16[4,4,320,256]{3,2,1,0:T(8,128)(2,1)S(1)}, u32[]{:S(2)}, u32[]{:S(2)}) async-start(bf16[4,4,320,256]{3,2,1,0:T(8,128)(2,1)} %get-tuple-element.22), calls=%async_computation | async-start | bytes 5242880 | tf_op jit(solution)/shard_map/all_to_all | solution.py:435
  9.4 2.7 %collective-permute-start.2 = (bf16[528,256]{1,0:T(8,128)(2,1)S(1)}, bf16[528,256]{1,0:T(8,128)(2,1)S(1)}, u32[]{:S(2)}, u32[]{:S(2)}) collective-permute-start(bf16[528,256]{1,0:T(8,128)(2,1)S(1)} %copy-done.6), channel_id=1, source_target_pairs={{4,0},{5,1},{6,2},{7,3},{8,4},{9,5},{10,6},{11,7},{12,8},{13,9},{1... | collective-permute-start | bytes 811016 | tf_op jit(solution)/shard_map/ppermute | solution.py:443
  12.1 3.4 %collective-permute-start.3 = (bf16[128,256]{1,0:T(8,128)(2,1)S(1)}, bf16[128,256]{1,0:T(8,128)(2,1)S(1)}, u32[]{:S(2)}, u32[]{:S(2)}) collective-permute-start(bf16[128,256]{1,0:T(8,128)(2,1)S(1)} %copy-done.7), channel_id=1, source_target_pairs={{0,16},{32,48},{64,80},{96,112},{128,144},{160,176},{192,208},{224... | collective-permute-start | bytes 196616 | tf_op jit(solution)/shard_map/ppermute | solution.py:421
  15.5 4.1 %collective-permute-start = (bf16[528,256]{1,0:T(8,128)(2,1)S(1)}, bf16[528,256]{1,0:T(8,128)(2,1)}, u32[]{:S(2)}, u32[]{:S(2)}) collective-permute-start(bf16[528,256]{1,0:T(8,128)(2,1)S(1)} %copy-done.6), channel_id=1, source_target_pairs={{12,0},{13,1},{14,2},{15,3},{0,4},{1,5},{2,6},{3,7},{4,8},{5,9},{6... | collective-permute-start | bytes 811016 | tf_op jit(solution)/shard_map/ppermute | solution.py:443
  19.6 3.4 %collective-permute-start.1 = (bf16[528,256]{1,0:T(8,128)(2,1)S(1)}, bf16[528,256]{1,0:T(8,128)(2,1)}, u32[]{:S(2)}, u32[]{:S(2)}) collective-permute-start(bf16[528,256]{1,0:T(8,128)(2,1)S(1)} %copy-done.6), channel_id=1, source_target_pairs={{8,0},{9,1},{10,2},{11,3},{12,4},{13,5},{14,6},{15,7},{0,8},{1,9},... | collective-permute-start | bytes 811016 | tf_op jit(solution)/shard_map/ppermute | solution.py:443
  27.5 7.0 %all-to-all-done.refs_4_.refs_5_ = bf16[4,4,320,256]{3,2,1,0:T(8,128)(2,1)S(1)} async-done(((bf16[4,4,320,256]{3,2,1,0:T(8,128)(2,1)}), bf16[4,4,320,256]{3,2,1,0:T(8,128)(2,1)S(1)}, u32[]{:S(2)}, u32[]{:S(2)}) %all-to-all-start) | async-done | bytes 2621472 | tf_op jit(solution)/shard_map/all_to_all | solution.py:435
  34.5 3.0 %shard_map.97 = (bf16[4,656,256]{2,1,0:T(8,128)(2,1)S(1)}, bf16[64,256]{1,0:T(8,128)(2,1)S(1)}) custom-call(bf16[528,256]{1,0:T(8,128)(2,1)S(1)} %copy-done.6, bf16[528,256]{1,0:T(8,128)(2,1)} %collective-permute-done.refs_1_, bf16[528,256]{1,0:T(8,128)(2,1)} %collective-permute-done.1.refs_2_, bf16[528,256]{1,0:T(8,128)(2,1)S(1)} %collective-permute-done.2.refs_3_, ...), custom_call_target="tpu_custom_call" | custom-call | flops 1342177280 | bytes 6291456 | tf_op jit(solution)/shard_map/pallas_call | solution.py:50
  38.6 4.3 %all-to-all-start.1 = ((bf16[4,656,256]{2,1,0:T(8,128)(2,1)}), bf16[4,656,256]{2,1,0:T(8,128)(2,1)}, u32[]{:S(2)}, u32[]{:S(2)}) async-start(bf16[4,656,256]{2,1,0:T(8,128)(2,1)} %copy-done), calls=%async_computation.1 | async-start | bytes 2686976 | tf_op jit(solution)/shard_map/all_to_all | solution.py:435
  47.0 8.5 %all-to-all-done.1.parts_ref = bf16[4,656,256]{2,1,0:T(8,128)(2,1)} async-done(((bf16[4,656,256]{2,1,0:T(8,128)(2,1)}), bf16[4,656,256]{2,1,0:T(8,128)(2,1)}, u32[]{:S(2)}, u32[]{:S(2)}) %all-to-all-start.1) | async-done | bytes 1343520 | tf_op jit(solution)/shard_map/all_to_all | solution.py:435
  57.3 3.6 %all-to-all-start.2 = ((bf16[4,64,512]{2,1,0:T(8,128)(2,1)}), bf16[4,64,512]{2,1,0:T(8,128)(2,1)S(1)}, u32[]{:S(2)}, u32[]{:S(2)}) async-start(bf16[4,64,512]{2,1,0:T(8,128)(2,1)} %get-tuple-element.27), calls=%async_computation.2 | async-start | bytes 524288 | tf_op jit(solution)/shard_map/all_to_all | solution.py:435
  60.8 2.8 %shard_map.99.query_ref = bf16[512,256]{1,0:T(8,128)(2,1)} custom-call(bf16[4,656,256]{2,1,0:T(8,128)(2,1)} %all-to-all-done.1.parts_ref, f32[8,512]{1,0:T(8,128)} %get-tuple-element.26.scale_ref), custom_call_target="tpu_custom_call" | custom-call | flops 1048576 | bytes 2097152 | tf_op jit(solution)/shard_map/pallas_call | solution.py:50
  63.7 3.8 %all-to-all-done.2.keyval_ref = bf16[4,64,512]{2,1,0:T(8,128)(2,1)S(1)} async-done(((bf16[4,64,512]{2,1,0:T(8,128)(2,1)}), bf16[4,64,512]{2,1,0:T(8,128)(2,1)S(1)}, u32[]{:S(2)}, u32[]{:S(2)}) %all-to-all-start.2) | async-done | bytes 262176 | tf_op jit(solution)/shard_map/all_to_all | solution.py:435
  68.4 2.0 %shard_map.100 = (bf16[512,256]{1,0:T(8,128)(2,1)}, bf16[512,256]{1,0:T(8,128)(2,1)S(1)}) custom-call(s32[32]{0:T(128)S(1)} %copy-done.4, bf16[512,256]{1,0:T(8,128)(2,1)S(1)} %bitcast.6, bf16[512,256]{1,0:T(8,128)(2,1)S(1)} %copy-done.2, bf16[4,64,512]{2,1,0:T(8,128)(2,1)S(1)} %all-to-all-done.2.keyval_ref, s32[32,512]{1,0:T(8,128)S(1)} %copy-done.3, ...), custom_call_target="tpu_custom_call" | custom-call | flops 134217728 | bytes 1048576 | tf_op jit(solution)/shard_map/pallas_call | solution.py:50
  70.5 1.9 %collective-permute-start.10 = (bf16[512,256]{1,0:T(8,128)(2,1)S(1)}, bf16[512,256]{1,0:T(8,128)(2,1)S(1)}, u32[]{:S(2)}, u32[]{:S(2)}) collective-permute-start(bf16[512,256]{1,0:T(8,128)(2,1)S(1)} %get-tuple-element.30), channel_id=1, source_target_pairs={{500,0},{501,1},{502,2},{503,3},{504,4},{505,5},{506,6},{507,7},{5... | collective-permute-start | bytes 786440 | tf_op jit(solution)/shard_map/ppermute | solution.py:461
  72.4 4.4 %collective-permute-start.11 = (bf16[512,256]{1,0:T(8,128)(2,1)S(1)}, bf16[512,256]{1,0:T(8,128)(2,1)S(1)}, u32[]{:S(2)}, u32[]{:S(2)}) collective-permute-start(bf16[512,256]{1,0:T(8,128)(2,1)S(1)} %get-tuple-element.30), channel_id=1, source_target_pairs={{504,0},{505,1},{506,2},{507,3},{508,4},{509,5},{510,6},{511,7},{4... | collective-permute-start | bytes 786440 | tf_op jit(solution)/shard_map/ppermute | solution.py:461
  76.8 2.5 %collective-permute-start.12 = (bf16[512,256]{1,0:T(8,128)(2,1)S(1)}, bf16[512,256]{1,0:T(8,128)(2,1)S(1)}, u32[]{:S(2)}, u32[]{:S(2)}) collective-permute-start(bf16[512,256]{1,0:T(8,128)(2,1)S(1)} %get-tuple-element.30), channel_id=1, source_target_pairs={{508,0},{509,1},{510,2},{511,3},{496,4},{497,5},{498,6},{499,7},{5... | collective-permute-start | bytes 786440 | tf_op jit(solution)/shard_map/ppermute | solution.py:461
  79.3 3.3 %collective-permute-start.13 = (bf16[512,256]{1,0:T(8,128)(2,1)S(1)}, bf16[512,256]{1,0:T(8,128)(2,1)S(1)}, u32[]{:S(2)}, u32[]{:S(2)}) collective-permute-start(bf16[512,256]{1,0:T(8,128)(2,1)S(1)} %get-tuple-element.30), channel_id=1, source_target_pairs={{496,0},{497,1},{498,2},{499,3},{500,4},{501,5},{502,6},{503,7},{5... | collective-permute-start | bytes 786440 | tf_op jit(solution)/shard_map/ppermute | solution.py:461
  83.9 3.6 %collective-permute-done.11.refs_1_ = bf16[512,256]{1,0:T(8,128)(2,1)S(1)} collective-permute-done((bf16[512,256]{1,0:T(8,128)(2,1)S(1)}, bf16[512,256]{1,0:T(8,128)(2,1)S(1)}, u32[]{:S(2)}, u32[]{:S(2)}) %collective-permute-start.11) | collective-permute-done | bytes 262176 | tf_op jit(solution)/shard_map/ppermute | solution.py:461
  88.9 2.6 %collective-permute-done.13.refs_3_ = bf16[512,256]{1,0:T(8,128)(2,1)S(1)} collective-permute-done((bf16[512,256]{1,0:T(8,128)(2,1)S(1)}, bf16[512,256]{1,0:T(8,128)(2,1)S(1)}, u32[]{:S(2)}, u32[]{:S(2)}) %collective-permute-start.13) | collective-permute-done | bytes 262176 | tf_op jit(solution)/shard_map/ppermute | solution.py:461
  91.5 2.1 %shard_map.101 = (bf16[4,656,256]{2,1,0:T(8,128)(2,1)S(1)}, bf16[512,256]{1,0:T(8,128)(2,1)S(1)}) custom-call(bf16[512,256]{1,0:T(8,128)(2,1)S(1)} %collective-permute-done.10.refs_0_, bf16[512,256]{1,0:T(8,128)(2,1)S(1)} %collective-permute-done.11.refs_1_, bf16[512,256]{1,0:T(8,128)(2,1)S(1)} %collective-permute-done.12.refs_2_, ...), custom_call_target="tpu_custom_call" | custom-call | flops 1342177280 | bytes 6291456 | tf_op jit(solution)/shard_map/pallas_call | solution.py:50
  93.6 15.4 %all_to_all.25.parts_ref = bf16[4,656,256]{2,1,0:T(8,128)(2,1)S(1)} all-to-all(bf16[4,656,256]{2,1,0:T(8,128)(2,1)S(1)} %get-tuple-element.33), channel_id=1, replica_groups={{0,1,2,3},{4,5,6,7},{8,9,10,11},{12,13,14,15},{16,20,24,28},{17,21,25,2..., dimensions={0} | all-to-all | bytes 2686976 | tf_op jit(solution)/shard_map/all_to_all | solution.py:435
  109.2 9.1 %all_to_all.26.keyval_ref = bf16[4,64,512]{2,1,0:T(8,128)(2,1)S(1)} all-to-all(bf16[4,64,512]{2,1,0:T(8,128)(2,1)S(1)} %get-tuple-element.35), channel_id=1, replica_groups={{0,1,2,3},{4,5,6,7},{8,9,10,11},{12,13,14,15},{16,17,18,19},{20,21,22,2..., dimensions={0} | all-to-all | bytes 524288 | tf_op jit(solution)/shard_map/all_to_all | solution.py:435
  118.3 2.2 %shard_map.103 = bf16[512,256]{1,0:T(8,128)(2,1)} custom-call(s32[32]{0:T(128)S(1)} %copy-done.4, bf16[512,256]{1,0:T(8,128)(2,1)S(1)} %get-tuple-element.32.x_ref, bf16[512,256]{1,0:T(8,128)(2,1)S(1)} %get-tuple-element.34.query_ref, bf16[4,64,512]{2,1,0:T(8,128)(2,1)S(1)} %all_to_all.26.keyval_ref, s32[32,512]{1,0:T(8,128)S(1)} %copy-done.3), custom_call_target="tpu_custom_call" | custom-call | flops 134217728 | bytes 1048576 | tf_op jit(solution)/shard_map/pallas_call | solution.py:50
  (38 shorter events, 15.2 us)
Async XLA Ops:
  4.7 4.7 %copy-start.6 = (bf16[528,256]{1,0:T(8,128)(2,1)S(1)}, bf16[528,256]{1,0:T(8,128)(2,1)}, u32[]{:S(2)}) copy-start(bf16[528,256]{1,0:T(8,128)(2,1)} %get-tuple-element.19.refs_0_) | copy-start | bytes 811012
  4.7 7.4 %copy-start.7 = (bf16[128,256]{1,0:T(8,128)(2,1)S(1)}, bf16[128,256]{1,0:T(8,128)(2,1)}, u32[]{:S(2)}) copy-start(bf16[128,256]{1,0:T(8,128)(2,1)} %get-tuple-element.20) | copy-start | bytes 196612
  4.8 21.3 %copy-start.4 = (s32[32]{0:T(128)S(1)}, s32[32]{0:T(128)}, u32[]{:S(2)}) copy-start(s32[32]{0:T(128)} %lengths_ref.5) | copy-start | bytes 388
  4.8 21.3 %copy-start.5 = (s32[32]{0:T(128)S(1)}, s32[32]{0:T(128)}, u32[]{:S(2)}) copy-start(s32[32]{0:T(128)} %ids_ref.3) | copy-start | bytes 388
  4.8 29.7 %all-to-all-start = ((bf16[4,4,320,256]{3,2,1,0:T(8,128)(2,1)}), bf16[4,4,320,256]{3,2,1,0:T(8,128)(2,1)S(1)}, u32[]{:S(2)}, u32[]{:S(2)}) async-start(bf16[4,4,320,256]{3,2,1,0:T(8,128)(2,1)} %get-tuple-element.22), calls=%async_computation | async-start | bytes 5242880 | tf_op jit(solution)/shard_map/all_to_all | solution.py:435
  9.4 14.6 %collective-permute-start.2 = (bf16[528,256]{1,0:T(8,128)(2,1)S(1)}, bf16[528,256]{1,0:T(8,128)(2,1)S(1)}, u32[]{:S(2)}, u32[]{:S(2)}) collective-permute-start(bf16[528,256]{1,0:T(8,128)(2,1)S(1)} %copy-done.6), channel_id=1, source_target_pairs={{4,0},{5,1},{6,2},{7,3},{8,4},{9,5},{10,6},{11,7},{12,8},{13,9},{1... | collective-permute-start | bytes 811016 | tf_op jit(solution)/shard_map/ppermute | solution.py:443
  12.1 10.9 %collective-permute-start.3 = (bf16[128,256]{1,0:T(8,128)(2,1)S(1)}, bf16[128,256]{1,0:T(8,128)(2,1)S(1)}, u32[]{:S(2)}, u32[]{:S(2)}) collective-permute-start(bf16[128,256]{1,0:T(8,128)(2,1)S(1)} %copy-done.7), channel_id=1, source_target_pairs={{0,16},{32,48},{64,80},{96,112},{128,144},{160,176},{192,208},{224... | collective-permute-start | bytes 196616 | tf_op jit(solution)/shard_map/ppermute | solution.py:421
  15.5 19.0 %collective-permute-start = (bf16[528,256]{1,0:T(8,128)(2,1)S(1)}, bf16[528,256]{1,0:T(8,128)(2,1)}, u32[]{:S(2)}, u32[]{:S(2)}) collective-permute-start(bf16[528,256]{1,0:T(8,128)(2,1)S(1)} %copy-done.6), channel_id=1, source_target_pairs={{12,0},{13,1},{14,2},{15,3},{0,4},{1,5},{2,6},{3,7},{4,8},{5,9},{6... | collective-permute-start | bytes 811016 | tf_op jit(solution)/shard_map/ppermute | solution.py:443
  19.6 14.9 %collective-permute-start.1 = (bf16[528,256]{1,0:T(8,128)(2,1)S(1)}, bf16[528,256]{1,0:T(8,128)(2,1)}, u32[]{:S(2)}, u32[]{:S(2)}) collective-permute-start(bf16[528,256]{1,0:T(8,128)(2,1)S(1)} %copy-done.6), channel_id=1, source_target_pairs={{8,0},{9,1},{10,2},{11,3},{12,4},{13,5},{14,6},{15,7},{0,8},{1,9},... | collective-permute-start | bytes 811016 | tf_op jit(solution)/shard_map/ppermute | solution.py:443
  24.0 2.0 %collective-permute-start.4 = (bf16[256,256]{1,0:T(8,128)(2,1)S(1)}, bf16[256,256]{1,0:T(8,128)(2,1)S(1)}, u32[]{:S(2)}, u32[]{:S(2)}) collective-permute-start(bf16[256,256]{1,0:T(8,128)(2,1)S(1)} %pad_maximum_fusion.refs_0_), channel_id=1, source_target_pairs={{80,112},{208,240},{336,368},{464,496},{81,113},{209,241},{337,369... | collective-permute-start | bytes 393224 | tf_op jit(solution)/shard_map/ppermute | solution.py:421
  24.6 1.4 %collective-permute-start.5 = (bf16[256,256]{1,0:T(8,128)(2,1)S(1)}, bf16[256,256]{1,0:T(8,128)(2,1)S(1)}, u32[]{:S(2)}, u32[]{:S(2)}) collective-permute-start(bf16[256,256]{1,0:T(8,128)(2,1)S(1)} %pad_maximum_fusion.refs_0_), channel_id=1, source_target_pairs={{48,112},{176,240},{304,368},{432,496},{49,113},{177,241},{305,369... | collective-permute-start | bytes 393224 | tf_op jit(solution)/shard_map/ppermute | solution.py:421
  25.3 0.7 collective-permute-start.6
  37.5 1.1 copy-start
  38.6 16.9 %all-to-all-start.1 = ((bf16[4,656,256]{2,1,0:T(8,128)(2,1)}), bf16[4,656,256]{2,1,0:T(8,128)(2,1)}, u32[]{:S(2)}, u32[]{:S(2)}) async-start(bf16[4,656,256]{2,1,0:T(8,128)(2,1)} %copy-done), calls=%async_computation.1 | async-start | bytes 2686976 | tf_op jit(solution)/shard_map/all_to_all | solution.py:435
  42.9 20.7 %collective-permute-start.7 = (bf16[512,256]{1,0:T(8,128)(2,1)S(1)}, bf16[512,256]{1,0:T(8,128)(2,1)}, u32[]{:S(2)}, u32[]{:S(2)}) collective-permute-start(bf16[512,256]{1,0:T(8,128)(2,1)S(1)} %shard_map.96.refs_0_), channel_id=1, source_target_pairs={{368,496},{369,497},{370,498},{371,499},{372,500},{373,501},{374,5... | collective-permute-start | bytes 786440 | tf_op jit(solution)/shard_map/ppermute | solution.py:421
  44.3 19.4 %collective-permute-start.8 = (bf16[512,256]{1,0:T(8,128)(2,1)S(1)}, bf16[512,256]{1,0:T(8,128)(2,1)}, u32[]{:S(2)}, u32[]{:S(2)}) collective-permute-start(bf16[512,256]{1,0:T(8,128)(2,1)S(1)} %shard_map.96.refs_0_), channel_id=1, source_target_pairs={{240,496},{241,497},{242,498},{243,499},{244,500},{245,501},{246,5... | collective-permute-start | bytes 786440 | tf_op jit(solution)/shard_map/ppermute | solution.py:421
  45.7 18.0 %collective-permute-start.9 = (bf16[512,256]{1,0:T(8,128)(2,1)S(1)}, bf16[512,256]{1,0:T(8,128)(2,1)}, u32[]{:S(2)}, u32[]{:S(2)}) collective-permute-start(bf16[512,256]{1,0:T(8,128)(2,1)S(1)} %shard_map.96.refs_0_), channel_id=1, source_target_pairs={{112,496},{113,497},{114,498},{115,499},{116,500},{117,501},{118,5... | collective-permute-start | bytes 786440 | tf_op jit(solution)/shard_map/ppermute | solution.py:421
  57.3 10.2 %copy-start.1 = (bf16[1,512,256]{2,1,0:T(8,128)(2,1)S(1)}, bf16[1,512,256]{2,1,0:T(8,128)(2,1)}, u32[]{:S(2)}) copy-start(bf16[1,512,256]{2,1,0:T(8,128)(2,1)} %param.8) | copy-start | bytes 786436
  57.3 10.2 %copy-start.3 = (s32[32,512]{1,0:T(8,128)S(1)}, s32[32,512]{1,0:T(8,128)}, u32[]{:S(2)}) copy-start(s32[32,512]{1,0:T(8,128)} %segments_ref.3) | copy-start | bytes 196612
  57.3 10.2 %all-to-all-start.2 = ((bf16[4,64,512]{2,1,0:T(8,128)(2,1)}), bf16[4,64,512]{2,1,0:T(8,128)(2,1)S(1)}, u32[]{:S(2)}, u32[]{:S(2)}) async-start(bf16[4,64,512]{2,1,0:T(8,128)(2,1)} %get-tuple-element.27), calls=%async_computation.2 | async-start | bytes 524288 | tf_op jit(solution)/shard_map/all_to_all | solution.py:435
  70.5 13.5 %collective-permute-start.10 = (bf16[512,256]{1,0:T(8,128)(2,1)S(1)}, bf16[512,256]{1,0:T(8,128)(2,1)S(1)}, u32[]{:S(2)}, u32[]{:S(2)}) collective-permute-start(bf16[512,256]{1,0:T(8,128)(2,1)S(1)} %get-tuple-element.30), channel_id=1, source_target_pairs={{500,0},{501,1},{502,2},{503,3},{504,4},{505,5},{506,6},{507,7},{5... | collective-permute-start | bytes 786440 | tf_op jit(solution)/shard_map/ppermute | solution.py:461
  72.4 15.1 %collective-permute-start.11 = (bf16[512,256]{1,0:T(8,128)(2,1)S(1)}, bf16[512,256]{1,0:T(8,128)(2,1)S(1)}, u32[]{:S(2)}, u32[]{:S(2)}) collective-permute-start(bf16[512,256]{1,0:T(8,128)(2,1)S(1)} %get-tuple-element.30), channel_id=1, source_target_pairs={{504,0},{505,1},{506,2},{507,3},{508,4},{509,5},{510,6},{511,7},{4... | collective-permute-start | bytes 786440 | tf_op jit(solution)/shard_map/ppermute | solution.py:461
  76.8 12.1 %collective-permute-start.12 = (bf16[512,256]{1,0:T(8,128)(2,1)S(1)}, bf16[512,256]{1,0:T(8,128)(2,1)S(1)}, u32[]{:S(2)}, u32[]{:S(2)}) collective-permute-start(bf16[512,256]{1,0:T(8,128)(2,1)S(1)} %get-tuple-element.30), channel_id=1, source_target_pairs={{508,0},{509,1},{510,2},{511,3},{496,4},{497,5},{498,6},{499,7},{5... | collective-permute-start | bytes 786440 | tf_op jit(solution)/shard_map/ppermute | solution.py:461
  79.3 12.2 %collective-permute-start.13 = (bf16[512,256]{1,0:T(8,128)(2,1)S(1)}, bf16[512,256]{1,0:T(8,128)(2,1)S(1)}, u32[]{:S(2)}, u32[]{:S(2)}) collective-permute-start(bf16[512,256]{1,0:T(8,128)(2,1)S(1)} %get-tuple-element.30), channel_id=1, source_target_pairs={{496,0},{497,1},{498,2},{499,3},{500,4},{501,5},{502,6},{503,7},{5... | collective-permute-start | bytes 786440 | tf_op jit(solution)/shard_map/ppermute | solution.py:461
  (1 other events, 1.0 us)
